TPU v7x, 32 devices: a whole 2x2x4 slice. The times are simulated.
32 devices in a mesh: bucket: 8 (over y, x, core), rep: 4 (over z).
Axes of the slice: x: 2, y: 2, z: 4, core: 2. Of those that a mesh axis runs over, the one named last changes fastest.
Arguments:
- src_table: float32 [16384, 256], P(('bucket', 'rep')), may hold values from -6 to 6
- src_state: float32 [16384], P(('bucket', 'rep')), may hold values from 0.05 to 0.5
- dst_table: float32 [4096, 256], P(('bucket', 'rep')), may hold values from -6 to 6
- dst_state: float32 [4096], P(('bucket', 'rep')), may hold values from 0.05 to 0.5
- rel_table: float32 [64, 256], replicated, may hold values from 0.25 to 1.75
- partners: int32 [2, 8], replicated, may hold values from 0 to 7, as said below
- tiles: int32 [8, 4, 2, 64], P('bucket', 'rep'), may hold values from 0 to 15
- tile_rel: int32 [8, 4, 2, 64], P('bucket', 'rep'), may hold values from 0 to 63
- counts: int32 [8, 4, 2], P('bucket', 'rep'), may hold values from 1 to 64, as said below
Outputs:
- src_out: float32 [16384, 256], P(('bucket', 'rep'))
- src_state_out: float32 [16384], P(('bucket', 'rep'))
- dst_out: float32 [4096, 256], P(('bucket', 'rep'))
- dst_state_out: float32 [4096], P(('bucket', 'rep'))
Inputs may be any that keep to these rules, and one draw needn't show every extreme that they name: partners[k, b] = b XOR m_k for one mask m_k of round k, 1 to 7, a different mask in each round. Only the first counts[b, r, k] slots of a device's round are live; some device holds 64 live tiles in every draw.
All inputs are finite; a program needn't handle non-finite values.
Results may differ from a plain program's by a relative error of at most 0.002.
Values may be sent and summed in bfloat16 or wider, within the bound.
No kernel may reach another device: no remote copies, remote signals or barrier semaphores. Data moves between devices by JAX's collectives and lax.ppermute only.
A program may use at most 64 MiB of HBM per device.

v0:
```python
import functools

import jax
import jax.numpy as jnp
from jax import lax
from jax.experimental import pallas as pl
from jax.experimental.pallas import tpu as pltpu
from jax.sharding import PartitionSpec as P

TILE = 128
GROUP = 4
LOW_BITS = 3
SHIFT = 16

learn_rate = 0.1

AXES = ("bucket", "rep")
SMEM = pl.BlockSpec(memory_space=pltpu.SMEM)
VMEM = pl.BlockSpec(memory_space=pltpu.VMEM)
GRANT = pltpu.CompilerParams(vmem_limit_bytes=12 * 1024 * 1024)


def bucket_send(rows, mask):
    buckets = lax.axis_size("bucket")
    bits = buckets.bit_length() - 1
    for first in range(0, bits, LOW_BITS):
        width = min(LOW_BITS, bits - first)
        least = 1 if width == bits else 0

        def branch(value, x, first=first):
            if value == 0:
                return x
            return lax.ppermute(x, "bucket", [(b, b ^ (value << first)) for b in range(buckets)])

        if width == bits:
            index = mask - 1
        else:
            index = jnp.bitwise_and(jnp.right_shift(mask, first), (1 << width) - 1)
        branches = [functools.partial(branch, value) for value in range(least, 1 << width)]
        rows = lax.switch(index, branches, rows)
    return rows


def rep_send(rows, offset):
    if offset == 0:
        return rows
    return lax.ppermute(rows, "rep", [(r, r ^ offset) for r in range(lax.axis_size("rep"))])


def sort_tiles(k, number, room, flip, none_rel, tiles, rel, counts, plan):
    bits = number.bit_length() - 1

    def place(t, ends):
        code = tiles[k, t]
        e = jnp.bitwise_xor(jnp.bitwise_and(code, number - 1), flip)
        p = ends[0]
        for i in range(1, number):
            p = jnp.where(e == i, ends[i], p)
        plan[0, number + e * room + p] = jnp.bitwise_or(
            jnp.left_shift(jnp.right_shift(code, bits), SHIFT), rel[k, t]
        )
        return tuple(ends[i] + jnp.where(e == i, 1, 0) for i in range(number))

    ends = lax.fori_loop(0, counts[k], place, (jnp.int32(0),) * number)
    for i in range(number):
        plan[0, i] = jnp.right_shift(ends[i] + (GROUP - 1), GROUP.bit_length() - 1)
        for extra in range(2 * GROUP):
            plan[0, number + i * room + ends[i] + extra] = jnp.int32(none_rel)


def first_kernel(rounds, number, room, none_rel, rep, tiles, rel, counts, partners, dst_ref, plan, rows_ref, *masks):
    shard_blocks = dst_ref.shape[0] // TILE
    rows_ref[...] = dst_ref[...].astype(jnp.bfloat16)
    for k in range(rounds):
        masks[k][0, 0] = partners[k, 0]
    sort_tiles(0, number, room, rep[0] * shard_blocks, none_rel, tiles, rel, counts, plan)


def later_kernel(k, shard_blocks, number, room, none_rel, rep, tiles, rel, counts, plan):
    sort_tiles(k, number, room, rep[0] * shard_blocks, none_rel, tiles, rel, counts, plan)


def round_kernel(src_ref, rel_ref, low_ref, row_ref):
    rels, width = rel_ref.shape
    low_ref[...] = src_ref[...].astype(jnp.bfloat16).astype(jnp.float32)
    row_ref[pl.ds(0, rels), :] = rel_ref[...] * (0.5 * width**-0.5)
    row_ref[pl.ds(rels, 8), :] = jnp.zeros((8, width), jnp.float32)


def round_source(src_table, rel_table):
    return pl.pallas_call(
        round_kernel,
        in_specs=[VMEM] * 2,
        out_specs=[VMEM] * 2,
        out_shape=[
            jax.ShapeDtypeStruct(src_table.shape, jnp.float32),
            jax.ShapeDtypeStruct((rel_table.shape[0] + 8, rel_table.shape[1]), jnp.float32),
        ],
        cost_estimate=pl.CostEstimate(
            flops=src_table.size, bytes_accessed=8 * src_table.size, transcendentals=0
        ),
        compiler_params=GRANT,
        name="round_source",
    )(src_table, rel_table)


def tile_kernel(block, number, room, carried, plan, low_ref, row_ref, dst_ref, *refs):
    src_grad, part, dst_grad, held_rows, held_slope = refs[carried:]
    shard_blocks = dst_ref.shape[0] // TILE
    if not carried:
        src_grad[...] = jnp.zeros_like(src_grad)
    row_id = lax.broadcasted_iota(jnp.int32, (TILE, TILE), 0)
    column_id = lax.broadcasted_iota(jnp.int32, (TILE, TILE), 1)
    offset = jnp.where(row_id == column_id, -1.0, 1.0).astype(jnp.float32)
    for i in range(shard_blocks):
        at = block * shard_blocks + i
        dst_rows = pl.ds(i * TILE, TILE)
        steps = plan[0, at]
        dst_grad[...] = jnp.zeros_like(dst_grad)

        def group(q, at=at):
            where, rows = [], []
            for g in range(GROUP):
                code = plan[0, number + at * room + q * GROUP + g]
                where.append(pl.multiple_of(jnp.right_shift(code, SHIFT) * TILE, TILE))
                rows.append(row_ref[pl.ds(jnp.bitwise_and(code, (1 << SHIFT) - 1), 1), :])
            return where, rows

        def slopes(q, slot, dst_rows=dst_rows):
            where, rows = group(q)
            src_rel = jnp.concatenate(
                [(low_ref[pl.ds(s, TILE), :] * row).astype(jnp.bfloat16) for s, row in zip(where, rows)],
                0,
            )
            scores = lax.dot_general(
                src_rel, dst_ref[dst_rows, :], (((1,), (1,)), ((), ())),
                preferred_element_type=jnp.float32,
            )
            slope = jnp.concatenate(
                [
                    (jnp.tanh(scores[g * TILE : (g + 1) * TILE]) + offset).astype(jnp.bfloat16)
                    for g in range(GROUP)
                ],
                0,
            )
            held_rows[slot] = src_rel
            held_slope[slot] = slope

        def grads(q, slot, dst_rows=dst_rows):
            where, rows = group(q)
            slope = held_slope[slot]
            src_terms = jnp.dot(slope, dst_ref[dst_rows, :], preferred_element_type=jnp.float32)
            dst_grad[...] += lax.dot_general(
                slope, held_rows[slot], (((0,), (0,)), ((), ())), preferred_element_type=jnp.float32
            )
            for g in range(GROUP):
                src_grad[pl.ds(where[g], TILE), :] += src_terms[g * TILE : (g + 1) * TILE] * rows[g]

        @pl.when(steps > 0)
        def _():
            slopes(0, 0)

            def two(p, carry):
                q = p * 2
                slopes(q + 1, 1)
                grads(q, 0)
                slopes(q + 2, 0)
                grads(q + 1, 1)
                return carry

            lax.fori_loop(0, jnp.right_shift(steps, 1), two, 0)

            @pl.when(jnp.bitwise_and(steps, 1) == 1)
            def _():
                grads(steps - 1, 0)

        part[dst_rows, :] = dst_grad[...].astype(jnp.bfloat16)


def tile_work(block, plan, low, rel_rows, shard, src_grad):
    reps = lax.axis_size("rep")
    rows, width = shard.shape
    number = reps * (rows // TILE)
    room = plan.shape[1] // number - 1
    slots = room // reps
    carried = [] if src_grad is None else [src_grad]
    return pl.pallas_call(
        functools.partial(tile_kernel, block, number, room, len(carried)),
        in_specs=[SMEM] + [VMEM] * (3 + len(carried)),
        out_specs=[VMEM] * 2,
        out_shape=[
            jax.ShapeDtypeStruct(low.shape, jnp.float32),
            jax.ShapeDtypeStruct((rows, width), jnp.bfloat16),
        ],
        scratch_shapes=[
            pltpu.VMEM((TILE, width), jnp.float32),
            pltpu.VMEM((2, GROUP * TILE, width), jnp.bfloat16),
            pltpu.VMEM((2, GROUP * TILE, TILE), jnp.bfloat16),
        ],
        input_output_aliases={4: 0} if carried else {},
        cost_estimate=pl.CostEstimate(
            flops=6 * slots * TILE * TILE * width,
            bytes_accessed=4 * low.size,
            transcendentals=slots * TILE * TILE,
        ),
        compiler_params=GRANT,
        name="tile_work",
    )(plan, low, rel_rows, shard, *carried)


def adagrad_kernel(table_ref, state_ref, grad_ref, table_out, state_out, low_out):
    width = table_ref.shape[1]
    row_id = lax.broadcasted_iota(jnp.int32, (TILE, TILE), 0)
    column_id = lax.broadcasted_iota(jnp.int32, (TILE, TILE), 1)
    same = row_id == column_id

    def block(i, carry):
        rows = pl.ds(pl.multiple_of(i * TILE, TILE), TILE)
        grad = grad_ref[rows, :].astype(jnp.float32)
        state = jnp.sum(jnp.where(same, state_ref[pl.ds(i, 1), :], 0.0), axis=1, keepdims=True)
        state = state + jnp.sum(grad * grad, axis=1, keepdims=True) * (1.0 / width)
        state_out[pl.ds(i, 1), :] = jnp.sum(jnp.where(same, state, 0.0), axis=0, keepdims=True)
        table = table_ref[rows, :] - learn_rate * grad / jnp.sqrt(state)
        table_out[rows, :] = table
        low_out[rows, :] = table.astype(jnp.bfloat16).astype(low_out.dtype)
        return carry

    lax.fori_loop(0, table_ref.shape[0] // TILE, block, 0)


def adagrad(table, state, grad, low_type):
    return pl.pallas_call(
        adagrad_kernel,
        in_specs=[VMEM] * 3,
        out_specs=[VMEM] * 3,
        out_shape=[
            jax.ShapeDtypeStruct(table.shape, jnp.float32),
            jax.ShapeDtypeStruct(state.shape, jnp.float32),
            jax.ShapeDtypeStruct(table.shape, low_type),
        ],
        cost_estimate=pl.CostEstimate(
            flops=8 * table.size, bytes_accessed=8 * table.size, transcendentals=table.shape[0]
        ),
        compiler_params=GRANT,
        name="adagrad",
    )(table, state, grad)


def per_device(
    src_table, src_state, dst_table, dst_state, rel_table, partners, tiles, tile_rel, counts
):
    reps = lax.axis_size("rep")
    rounds = partners.shape[0]
    src_state = src_state.reshape(-1, TILE)
    dst_state = dst_state.reshape(-1, TILE)
    shard_blocks = dst_table.shape[0] // TILE
    number = reps * shard_blocks
    room = tiles.shape[-1] + 2 * GROUP
    none_rel = rel_table.shape[0]
    scalars = (
        lax.axis_index("rep").astype(jnp.int32).reshape(1), tiles[0, 0], tile_rel[0, 0], counts[0, 0],
    )
    plan_shape = jax.ShapeDtypeStruct((1, number * (room + 1)), jnp.int32)
    plan, rows, *masks = pl.pallas_call(
        functools.partial(first_kernel, rounds, number, room, none_rel),
        in_specs=[SMEM] * 5 + [VMEM],
        out_specs=[SMEM, VMEM] + [SMEM] * rounds,
        out_shape=[plan_shape, jax.ShapeDtypeStruct(dst_table.shape, jnp.bfloat16)]
        + [jax.ShapeDtypeStruct((1, 1), jnp.int32)] * rounds,
        compiler_params=GRANT,
        name="first",
    )(*scalars, partners, dst_table)
    for k in range(rounds):
        mask = masks[k].reshape(())
        own = bucket_send(rows, mask)
        shards = [own]
        for j in range(1, reps):
            shards.append(rep_send(own, j))
        if k == 0:
            low, rel_rows = round_source(src_table, rel_table)
        src_grad, total = None, None
        for j in [*range(1, reps), 0]:
            src_grad, part = tile_work(j, plan, low, rel_rows, shards[j], src_grad)
            part = rep_send(part, j)
            part = part.astype(jnp.float32)
            total = part if total is None else total + part
        src_table, src_state, low = adagrad(src_table, src_state, src_grad, jnp.float32)
        if k + 1 < rounds:
            plan = pl.pallas_call(
                functools.partial(later_kernel, k + 1, shard_blocks, number, room, none_rel),
                in_specs=[SMEM] * 4,
                out_specs=SMEM,
                out_shape=plan_shape,
                compiler_params=GRANT,
                name="later",
            )(*scalars)
        total = bucket_send(total.astype(jnp.bfloat16), mask)
        dst_table, dst_state, rows = adagrad(dst_table, dst_state, total, jnp.bfloat16)
    return (src_table, src_state.reshape(-1), dst_table, dst_state.reshape(-1))


def solution(mesh):
    table, state = P(AXES, None), P(AXES)
    in_specs = (
        table,
        state,
        table,
        state,
        P(),
        P(),
        P("bucket", "rep", None, None),
        P("bucket", "rep", None, None),
        P("bucket", "rep", None),
    )
    return jax.shard_map(
        per_device,
        mesh=mesh,
        in_specs=in_specs,
        out_specs=(table, state, table, state),
        check_vma=False,
    )
```

profile of v0, /device:TPU:0, one launch (start us, length us, event | category | flops | bytes accessed | tf_op | source)
XLA Modules:
  0.0 70.1 jit_solution(7775621741520258772)
XLA Ops:
  0.7 0.6 copy-done.6
  1.3 0.0 copy-done.9
  1.3 0.0 copy-done.5
  1.4 0.9 %copy-done.2 = f32[128,256]{1,0:T(8,128)S(1)} copy-done((f32[128,256]{1,0:T(8,128)S(1)}, f32[128,256]{1,0:T(8,128)}, u32[]{:S(2)}) %copy-start.2) | copy-done | bytes 131096
  2.3 1.4 %first.1 = (s32[1,292]{1,0:T(1,128)S(1)}, bf16[128,256]{1,0:T(8,128)(2,1)S(1)}, s32[1,1]{1,0:T(1,128)}, s32[1,1]{1,0:T(1,128)}) custom-call(s32[1]{0:T(128)} %bitcast.1.rep, s32[2,64]{1,0:T(2,128)S(1)} %bitcast.10, s32[2,64]{1,0:T(2,128)S(1)} %bitcast.12, s32[2]{0:T(128)S(1)} %bitcast.15, s32[2,8]{1,0:T(2,128)S(1)} %copy-done.9, f32[128,256]{1,0:T(8,128)S(1)} %copy-done.2), custom_call_target="tpu_custom_call" | custom-call | tf_op jit(solution)/shard_map/first/pallas_call | solution.py:264
  4.3 5.6 %conditional.4 = (bf16[128,256]{1,0:T(8,128)(2,1)}) conditional(s32[]{:T(128)} %bitcast.5, bf16[128,256]{1,0:T(8,128)(2,1)S(1)} %get-tuple-element.100, bf16[128,256]{1,0:T(8,128)(2,1)S(1)} %get-tuple-element.100, bf16[128,256]{1,0:T(8,128)(2,1)S(1)} %get-tuple-element.100, ...), branch_computations={%region_0.0_spmd, %region_1.0_spmd, %region_2.0_spmd, %region_3.0_... | conditional | bytes 262192 | solution.py:40
  4.3 3.3 %collective-permute-start.1 = (bf16[128,256]{1,0:T(8,128)(2,1)S(1)}, bf16[128,256]{1,0:T(8,128)(2,1)}, u32[]{:S(2)}, u32[]{:S(2)}) collective-permute-start(bf16[128,256]{1,0:T(8,128)(2,1)S(1)} %param.1), channel_id=1, source_target_pairs={{0,8},{4,12},{8,0},{12,4},{16,24},{20,28},{24,16},{28,20},{1,9},{5... | collective-permute-start | bytes 196616 | tf_op jit(solution)/shard_map/cond/branch_1_fun/ppermute | solution.py:33
  7.6 2.4 %collective-permute-done.1 = bf16[128,256]{1,0:T(8,128)(2,1)} collective-permute-done((bf16[128,256]{1,0:T(8,128)(2,1)S(1)}, bf16[128,256]{1,0:T(8,128)(2,1)}, u32[]{:S(2)}, u32[]{:S(2)}) %collective-permute-start.1) | collective-permute-done | bytes 65568 | tf_op jit(solution)/shard_map/cond/branch_1_fun/ppermute | solution.py:33
  9.9 1.9 %collective-permute-start.30 = (bf16[128,256]{1,0:T(8,128)(2,1)}, bf16[128,256]{1,0:T(8,128)(2,1)S(1)}, u32[]{:S(2)}, u32[]{:S(2)}) collective-permute-start(bf16[128,256]{1,0:T(8,128)(2,1)} %get-tuple-element.128.dst_ref), channel_id=1, source_target_pairs={{0,1},{1,0},{2,3},{3,2},{4,5},{5,4},{6,7},{7,6},{8,9},{9,8},{10,11... | collective-permute-start | bytes 196616 | tf_op jit(solution)/shard_map/ppermute | solution.py:47
  11.9 2.9 %collective-permute-start.29 = (bf16[128,256]{1,0:T(8,128)(2,1)}, bf16[128,256]{1,0:T(8,128)(2,1)S(1)}, u32[]{:S(2)}, u32[]{:S(2)}) collective-permute-start(bf16[128,256]{1,0:T(8,128)(2,1)} %get-tuple-element.128.dst_ref), channel_id=1, source_target_pairs={{0,2},{1,3},{2,0},{3,1},{4,6},{5,7},{6,4},{7,5},{8,10},{9,11},{10,... | collective-permute-start | bytes 196616 | tf_op jit(solution)/shard_map/ppermute | solution.py:47
  14.8 1.0 %copy-done = f32[512,256]{1,0:T(8,128)S(1)} copy-done((f32[512,256]{1,0:T(8,128)S(1)}, f32[512,256]{1,0:T(8,128)}, u32[]{:S(2)}) %copy-start) | copy-done | bytes 524312
  15.9 1.4 %tile_work.8 = (f32[512,256]{1,0:T(8,128)S(1)}, bf16[128,256]{1,0:T(8,128)(2,1)S(1)}) custom-call(s32[1,292]{1,0:T(1,128)S(1)} %get-tuple-element.96.plan, f32[512,256]{1,0:T(8,128)S(1)} %get-tuple-element.97.low_ref, f32[72,256]{1,0:T(8,128)S(1)} %get-tuple-element.98.row_ref, bf16[128,256]{1,0:T(8,128)(2,1)S(1)} %collective-permute-done.30.dst_ref), custom_call_target="tpu_custom_call" | custom-call | flops 452984832 | bytes 524288 | tf_op jit(solution)/shard_map/tile_work/pallas_call | solution.py:187
  17.3 2.1 %collective-permute-done.29.dst_ref = bf16[128,256]{1,0:T(8,128)(2,1)S(1)} collective-permute-done((bf16[128,256]{1,0:T(8,128)(2,1)}, bf16[128,256]{1,0:T(8,128)(2,1)S(1)}, u32[]{:S(2)}, u32[]{:S(2)}) %collective-permute-start.29) | collective-permute-done | bytes 65568 | tf_op jit(solution)/shard_map/ppermute | solution.py:47
  19.4 0.6 tile_work.9
  20.0 1.1 %collective-permute-done.28.dst_ref = bf16[128,256]{1,0:T(8,128)(2,1)S(1)} collective-permute-done((bf16[128,256]{1,0:T(8,128)(2,1)}, bf16[128,256]{1,0:T(8,128)(2,1)S(1)}, u32[]{:S(2)}, u32[]{:S(2)}) %collective-permute-start.28) | collective-permute-done | bytes 65568 | tf_op jit(solution)/shard_map/ppermute | solution.py:47
  21.1 1.1 %tile_work.10 = (f32[512,256]{1,0:T(8,128)S(1)}, bf16[128,256]{1,0:T(8,128)(2,1)S(1)}) custom-call(s32[1,292]{1,0:T(1,128)S(1)} %get-tuple-element.96.plan, f32[512,256]{1,0:T(8,128)S(1)} %get-tuple-element.97.low_ref, f32[72,256]{1,0:T(8,128)S(1)} %get-tuple-element.98.row_ref, ...), custom_call_target="tpu_custom_call", output_to_operand_aliasing={{0}: (4, {})} | custom-call | flops 452984832 | bytes 524288 | tf_op jit(solution)/shard_map/tile_work/pallas_call | solution.py:187
  22.2 2.9 %collective-permute-start.33 = (bf16[128,256]{1,0:T(8,128)(2,1)S(1)}, bf16[128,256]{1,0:T(8,128)(2,1)S(1)}, u32[]{:S(2)}, u32[]{:S(2)}) collective-permute-start(bf16[128,256]{1,0:T(8,128)(2,1)S(1)} %get-tuple-element.111), channel_id=1, source_target_pairs={{0,3},{1,2},{2,1},{3,0},{4,7},{5,6},{6,5},{7,4},{8,11},{9,10},{10,... | collective-permute-start | bytes 196616 | tf_op jit(solution)/shard_map/ppermute | solution.py:47
  25.0 1.6 %collective-permute-start.31 = (bf16[128,256]{1,0:T(8,128)(2,1)S(1)}, bf16[128,256]{1,0:T(8,128)(2,1)S(1)}, u32[]{:S(2)}, u32[]{:S(2)}) collective-permute-start(bf16[128,256]{1,0:T(8,128)(2,1)S(1)} %get-tuple-element.109), channel_id=1, source_target_pairs={{0,1},{1,0},{2,3},{3,2},{4,5},{5,4},{6,7},{7,6},{8,9},{9,8},{10,11... | collective-permute-start | bytes 196616 | tf_op jit(solution)/shard_map/ppermute | solution.py:47
  27.3 0.0 copy-start.3
  27.3 0.0 copy-start.10
  27.3 1.4 %tile_work.11 = (f32[512,256]{1,0:T(8,128)S(1)}, bf16[128,256]{1,0:T(8,128)(2,1)S(1)}) custom-call(s32[1,292]{1,0:T(1,128)S(1)} %get-tuple-element.96.plan, f32[512,256]{1,0:T(8,128)S(1)} %get-tuple-element.97.low_ref, f32[72,256]{1,0:T(8,128)S(1)} %get-tuple-element.98.row_ref, ...), custom_call_target="tpu_custom_call", output_to_operand_aliasing={{0}: (4, {})} | custom-call | flops 452984832 | bytes 524288 | tf_op jit(solution)/shard_map/tile_work/pallas_call | solution.py:187
  28.7 1.7 %collective-permute-done.32 = bf16[128,256]{1,0:T(8,128)(2,1)S(1)} collective-permute-done((bf16[128,256]{1,0:T(8,128)(2,1)S(1)}, bf16[128,256]{1,0:T(8,128)(2,1)S(1)}, u32[]{:S(2)}, u32[]{:S(2)}) %collective-permute-start.32) | collective-permute-done | bytes 65568 | tf_op jit(solution)/shard_map/ppermute | solution.py:47
  30.4 0.5 collective-permute-done.31
  30.9 4.5 %conditional.5 = (bf16[128,256]{1,0:T(8,128)(2,1)}) conditional(s32[]{:T(128)} %bitcast.5, bf16[128,256]{1,0:T(8,128)(2,1)S(1)} %add_convert_fusion.1, bf16[128,256]{1,0:T(8,128)(2,1)S(1)} %add_convert_fusion.1, bf16[128,256]{1,0:T(8,128)(2,1)S(1)} %add_convert_fusion.1, ...), branch_computations={%region_7.0_spmd, %region_8.0_spmd, %region_9.0_spmd, %region_10.0... | conditional | bytes 262192 | solution.py:40
  30.9 0.2 collective-permute-start.8
  31.2 4.2 %collective-permute-done.8 = bf16[128,256]{1,0:T(8,128)(2,1)} collective-permute-done((bf16[128,256]{1,0:T(8,128)(2,1)S(1)}, bf16[128,256]{1,0:T(8,128)(2,1)}, u32[]{:S(2)}, u32[]{:S(2)}) %collective-permute-start.8) | collective-permute-done | bytes 65568 | tf_op jit(solution)/shard_map/cond/branch_1_fun/ppermute | solution.py:33
  35.4 1.0 %adagrad.5 = (f32[128,256]{1,0:T(8,128)S(1)}, f32[1,128]{1,0:T(1,128)S(1)}, bf16[128,256]{1,0:T(8,128)(2,1)S(1)}) custom-call(f32[128,256]{1,0:T(8,128)S(1)} %copy-done.3, f32[1,128]{1,0:T(1,128)S(1)} %bitcast.17, bf16[128,256]{1,0:T(8,128)(2,1)} %get-tuple-element.129.grad_ref), custom_call_target="tpu_custom_call" | custom-call | flops 262144 | bytes 262144 | tf_op jit(solution)/shard_map/adagrad/pallas_call | solution.py:232
  36.4 4.5 %conditional.6 = (bf16[128,256]{1,0:T(8,128)(2,1)}) conditional(s32[]{:T(128)} %bitcast.6, bf16[128,256]{1,0:T(8,128)(2,1)S(1)} %get-tuple-element.113, bf16[128,256]{1,0:T(8,128)(2,1)S(1)} %get-tuple-element.113, bf16[128,256]{1,0:T(8,128)(2,1)S(1)} %get-tuple-element.113, ...), branch_computations={%region_14.0_spmd, %region_15.0_spmd, %region_16.0_spmd, %region_1... | conditional | bytes 262192 | solution.py:40
  36.4 1.9 %collective-permute-start.17 = (bf16[128,256]{1,0:T(8,128)(2,1)S(1)}, bf16[128,256]{1,0:T(8,128)(2,1)}, u32[]{:S(2)}, u32[]{:S(2)}) collective-permute-start(bf16[128,256]{1,0:T(8,128)(2,1)S(1)} %param.17), channel_id=1, source_target_pairs={{0,16},{4,20},{8,24},{12,28},{16,0},{20,4},{24,8},{28,12},{1,17},{... | collective-permute-start | bytes 196616 | tf_op jit(solution)/shard_map/cond/branch_3_fun/ppermute | solution.py:33
  38.3 2.5 %collective-permute-done.17 = bf16[128,256]{1,0:T(8,128)(2,1)} collective-permute-done((bf16[128,256]{1,0:T(8,128)(2,1)S(1)}, bf16[128,256]{1,0:T(8,128)(2,1)}, u32[]{:S(2)}, u32[]{:S(2)}) %collective-permute-start.17) | collective-permute-done | bytes 65568 | tf_op jit(solution)/shard_map/cond/branch_3_fun/ppermute | solution.py:33
  40.8 1.0 %collective-permute-start.36 = (bf16[128,256]{1,0:T(8,128)(2,1)}, bf16[128,256]{1,0:T(8,128)(2,1)S(1)}, u32[]{:S(2)}, u32[]{:S(2)}) collective-permute-start(bf16[128,256]{1,0:T(8,128)(2,1)} %get-tuple-element.130.dst_ref), channel_id=1, source_target_pairs={{0,1},{1,0},{2,3},{3,2},{4,5},{5,4},{6,7},{7,6},{8,9},{9,8},{10,11... | collective-permute-start | bytes 196616 | tf_op jit(solution)/shard_map/ppermute | solution.py:47
  41.8 1.7 %collective-permute-start.35 = (bf16[128,256]{1,0:T(8,128)(2,1)}, bf16[128,256]{1,0:T(8,128)(2,1)S(1)}, u32[]{:S(2)}, u32[]{:S(2)}) collective-permute-start(bf16[128,256]{1,0:T(8,128)(2,1)} %get-tuple-element.130.dst_ref), channel_id=1, source_target_pairs={{0,2},{1,3},{2,0},{3,1},{4,6},{5,7},{6,4},{7,5},{8,10},{9,11},{10,... | collective-permute-start | bytes 196616 | tf_op jit(solution)/shard_map/ppermute | solution.py:47
  43.5 2.3 %later.1.plan = s32[1,292]{1,0:T(1,128)S(1)} custom-call(s32[1]{0:T(128)} %bitcast.1.rep, s32[2,64]{1,0:T(2,128)S(1)} %bitcast.11, s32[2,64]{1,0:T(2,128)S(1)} %bitcast.13, s32[2]{0:T(128)S(1)} %bitcast.16), custom_call_target="tpu_custom_call" | custom-call | tf_op jit(solution)/shard_map/later/pallas_call | solution.py:289
  45.8 0.7 copy-done.7
  46.5 0.6 adagrad.4
  47.1 1.8 %collective-permute-start.34 = (bf16[128,256]{1,0:T(8,128)(2,1)}, bf16[128,256]{1,0:T(8,128)(2,1)S(1)}, u32[]{:S(2)}, u32[]{:S(2)}) collective-permute-start(bf16[128,256]{1,0:T(8,128)(2,1)} %get-tuple-element.130.dst_ref), channel_id=1, source_target_pairs={{0,3},{1,2},{2,1},{3,0},{4,7},{5,6},{6,5},{7,4},{8,11},{9,10},{10,... | collective-permute-start | bytes 196616 | tf_op jit(solution)/shard_map/ppermute | solution.py:47
  48.9 2.3 %tile_work.12 = (f32[512,256]{1,0:T(8,128)S(1)}, bf16[128,256]{1,0:T(8,128)(2,1)S(1)}) custom-call(s32[1,292]{1,0:T(1,128)S(1)} %later.1.plan, f32[512,256]{1,0:T(8,128)S(1)} %get-tuple-element.107.low_ref, f32[72,256]{1,0:T(8,128)S(1)} %get-tuple-element.98.row_ref, bf16[128,256]{1,0:T(8,128)(2,1)S(1)} %collective-permute-done.36.dst_ref), custom_call_target="tpu_custom_call" | custom-call | flops 452984832 | bytes 524288 | tf_op jit(solution)/shard_map/tile_work/pallas_call | solution.py:187
  51.2 1.7 %tile_work.13 = (f32[512,256]{1,0:T(8,128)S(1)}, bf16[128,256]{1,0:T(8,128)(2,1)S(1)}) custom-call(s32[1,292]{1,0:T(1,128)S(1)} %later.1.plan, f32[512,256]{1,0:T(8,128)S(1)} %get-tuple-element.107.low_ref, f32[72,256]{1,0:T(8,128)S(1)} %get-tuple-element.98.row_ref, ...), custom_call_target="tpu_custom_call", output_to_operand_aliasing={{0}: (4, {})} | custom-call | flops 452984832 | bytes 524288 | tf_op jit(solution)/shard_map/tile_work/pallas_call | solution.py:187
  52.9 0.5 collective-permute-done.34.dst_ref
  53.4 2.0 %tile_work.14 = (f32[512,256]{1,0:T(8,128)S(1)}, bf16[128,256]{1,0:T(8,128)(2,1)S(1)}) custom-call(s32[1,292]{1,0:T(1,128)S(1)} %later.1.plan, f32[512,256]{1,0:T(8,128)S(1)} %get-tuple-element.107.low_ref, f32[72,256]{1,0:T(8,128)S(1)} %get-tuple-element.98.row_ref, ...), custom_call_target="tpu_custom_call", output_to_operand_aliasing={{0}: (4, {})} | custom-call | flops 452984832 | bytes 524288 | tf_op jit(solution)/shard_map/tile_work/pallas_call | solution.py:187
  55.4 1.8 %collective-permute-start.39 = (bf16[128,256]{1,0:T(8,128)(2,1)S(1)}, bf16[128,256]{1,0:T(8,128)(2,1)S(1)}, u32[]{:S(2)}, u32[]{:S(2)}) collective-permute-start(bf16[128,256]{1,0:T(8,128)(2,1)S(1)} %get-tuple-element.124), channel_id=1, source_target_pairs={{0,3},{1,2},{2,1},{3,0},{4,7},{5,6},{6,5},{7,4},{8,11},{9,10},{10,... | collective-permute-start | bytes 196616 | tf_op jit(solution)/shard_map/ppermute | solution.py:47
  57.2 2.6 %collective-permute-start.37 = (bf16[128,256]{1,0:T(8,128)(2,1)S(1)}, bf16[128,256]{1,0:T(8,128)(2,1)S(1)}, u32[]{:S(2)}, u32[]{:S(2)}) collective-permute-start(bf16[128,256]{1,0:T(8,128)(2,1)S(1)} %get-tuple-element.122), channel_id=1, source_target_pairs={{0,1},{1,0},{2,3},{3,2},{4,5},{5,4},{6,7},{7,6},{8,9},{9,8},{10,11... | collective-permute-start | bytes 196616 | tf_op jit(solution)/shard_map/ppermute | solution.py:47
  59.8 2.5 %tile_work.15 = (f32[512,256]{1,0:T(8,128)S(1)}, bf16[128,256]{1,0:T(8,128)(2,1)S(1)}) custom-call(s32[1,292]{1,0:T(1,128)S(1)} %later.1.plan, f32[512,256]{1,0:T(8,128)S(1)} %get-tuple-element.107.low_ref, f32[72,256]{1,0:T(8,128)S(1)} %get-tuple-element.98.row_ref, bf16[128,256]{1,0:T(8,128)(2,1)} %get-tuple-element.130.dst_ref, ...), custom_call_target="tpu_custom_call", output_to_operand_aliasing={{0}: (4, {})} | custom-call | flops 452984832 | bytes 524288 | tf_op jit(solution)/shard_map/tile_work/pallas_call | solution.py:187
  62.4 1.6 %adagrad.6 = (f32[512,256]{1,0:T(8,128)}, f32[4,128]{1,0:T(4,128)}, f32[512,256]{1,0:T(8,128)}) custom-call(f32[512,256]{1,0:T(8,128)S(1)} %get-tuple-element.105.table_ref, f32[4,128]{1,0:T(4,128)S(1)} %get-tuple-element.106.state_ref, f32[512,256]{1,0:T(8,128)S(1)} %get-tuple-element.117.grad_ref), custom_call_target="tpu_custom_call" | custom-call | flops 1048576 | bytes 1048576 | tf_op jit(solution)/shard_map/adagrad/pallas_call | solution.py:232
  64.0 4.5 %conditional.7 = (bf16[128,256]{1,0:T(8,128)(2,1)}) conditional(s32[]{:T(128)} %bitcast.6, bf16[128,256]{1,0:T(8,128)(2,1)S(1)} %add_convert_fusion, bf16[128,256]{1,0:T(8,128)(2,1)S(1)} %add_convert_fusion, bf16[128,256]{1,0:T(8,128)(2,1)S(1)} %add_convert_fusion, bf16[128,256]{1,0:T(8,128)(2,1)S(1)} %add_convert_fusion, ...), branch_computations={%region_21.0_spmd, %region_22.0_spmd, %region_23.0_spmd, %region_2... | conditional | bytes 262192 | solution.py:40
  64.0 0.1 collective-permute-start.24
  64.1 4.4 %collective-permute-done.24 = bf16[128,256]{1,0:T(8,128)(2,1)} collective-permute-done((bf16[128,256]{1,0:T(8,128)(2,1)S(1)}, bf16[128,256]{1,0:T(8,128)(2,1)}, u32[]{:S(2)}, u32[]{:S(2)}) %collective-permute-start.24) | collective-permute-done | bytes 65568 | tf_op jit(solution)/shard_map/cond/branch_3_fun/ppermute | solution.py:33
  68.5 1.6 %adagrad.7 = (f32[128,256]{1,0:T(8,128)}, f32[1,128]{1,0:T(1,128)}, bf16[128,256]{1,0:T(8,128)(2,1)}) custom-call(f32[128,256]{1,0:T(8,128)S(1)} %get-tuple-element.120.table_ref, f32[1,128]{1,0:T(1,128)S(1)} %get-tuple-element.121.state_ref, bf16[128,256]{1,0:T(8,128)(2,1)} %get-tuple-element.131.grad_ref), custom_call_target="tpu_custom_call" | custom-call | flops 262144 | bytes 262144 | tf_op jit(solution)/shard_map/adagrad/pallas_call | solution.py:232
  (27 shorter events, 0.2 us)
Async XLA Ops:
  0.6 0.7 copy-start.6
  0.6 0.7 copy-start.9
  0.7 0.7 copy-start.5
  0.7 0.7 copy-start.8
  1.4 0.9 %copy-start.2 = (f32[128,256]{1,0:T(8,128)S(1)}, f32[128,256]{1,0:T(8,128)}, u32[]{:S(2)}) copy-start(f32[128,256]{1,0:T(8,128)} %table_ref.3) | copy-start | bytes 393220
  2.3 12.5 %copy-start.4 = (f32[64,256]{1,0:T(8,128)S(1)}, f32[64,256]{1,0:T(8,128)}, u32[]{:S(2)}) copy-start(f32[64,256]{1,0:T(8,128)} %rel_ref.1) | copy-start | bytes 196612
  4.3 5.6 %collective-permute-start.1 = (bf16[128,256]{1,0:T(8,128)(2,1)S(1)}, bf16[128,256]{1,0:T(8,128)(2,1)}, u32[]{:S(2)}, u32[]{:S(2)}) collective-permute-start(bf16[128,256]{1,0:T(8,128)(2,1)S(1)} %param.1), channel_id=1, source_target_pairs={{0,8},{4,12},{8,0},{12,4},{16,24},{20,28},{24,16},{28,20},{1,9},{5... | collective-permute-start | bytes 196616 | tf_op jit(solution)/shard_map/cond/branch_1_fun/ppermute | solution.py:33
  9.9 6.0 %collective-permute-start.30 = (bf16[128,256]{1,0:T(8,128)(2,1)}, bf16[128,256]{1,0:T(8,128)(2,1)S(1)}, u32[]{:S(2)}, u32[]{:S(2)}) collective-permute-start(bf16[128,256]{1,0:T(8,128)(2,1)} %get-tuple-element.128.dst_ref), channel_id=1, source_target_pairs={{0,1},{1,0},{2,3},{3,2},{4,5},{5,4},{6,7},{7,6},{8,9},{9,8},{10,11... | collective-permute-start | bytes 196616 | tf_op jit(solution)/shard_map/ppermute | solution.py:47
  11.9 7.5 %collective-permute-start.29 = (bf16[128,256]{1,0:T(8,128)(2,1)}, bf16[128,256]{1,0:T(8,128)(2,1)S(1)}, u32[]{:S(2)}, u32[]{:S(2)}) collective-permute-start(bf16[128,256]{1,0:T(8,128)(2,1)} %get-tuple-element.128.dst_ref), channel_id=1, source_target_pairs={{0,2},{1,3},{2,0},{3,1},{4,6},{5,7},{6,4},{7,5},{8,10},{9,11},{10,... | collective-permute-start | bytes 196616 | tf_op jit(solution)/shard_map/ppermute | solution.py:47
  14.8 6.3 %collective-permute-start.28 = (bf16[128,256]{1,0:T(8,128)(2,1)}, bf16[128,256]{1,0:T(8,128)(2,1)S(1)}, u32[]{:S(2)}, u32[]{:S(2)}) collective-permute-start(bf16[128,256]{1,0:T(8,128)(2,1)} %get-tuple-element.128.dst_ref), channel_id=1, source_target_pairs={{0,3},{1,2},{2,1},{3,0},{4,7},{5,6},{6,5},{7,4},{8,11},{9,10},{10,... | collective-permute-start | bytes 196616 | tf_op jit(solution)/shard_map/ppermute | solution.py:47
  14.8 1.0 %copy-start = (f32[512,256]{1,0:T(8,128)S(1)}, f32[512,256]{1,0:T(8,128)}, u32[]{:S(2)}) copy-start(f32[512,256]{1,0:T(8,128)} %table_ref.2) | copy-start | bytes 1572868
  22.2 6.6 %collective-permute-start.33 = (bf16[128,256]{1,0:T(8,128)(2,1)S(1)}, bf16[128,256]{1,0:T(8,128)(2,1)S(1)}, u32[]{:S(2)}, u32[]{:S(2)}) collective-permute-start(bf16[128,256]{1,0:T(8,128)(2,1)S(1)} %get-tuple-element.111), channel_id=1, source_target_pairs={{0,3},{1,2},{2,1},{3,0},{4,7},{5,6},{6,5},{7,4},{8,11},{9,10},{10,... | collective-permute-start | bytes 196616 | tf_op jit(solution)/shard_map/ppermute | solution.py:47
  25.0 5.4 %collective-permute-start.32 = (bf16[128,256]{1,0:T(8,128)(2,1)S(1)}, bf16[128,256]{1,0:T(8,128)(2,1)S(1)}, u32[]{:S(2)}, u32[]{:S(2)}) collective-permute-start(bf16[128,256]{1,0:T(8,128)(2,1)S(1)} %get-tuple-element.110), channel_id=1, source_target_pairs={{0,2},{1,3},{2,0},{3,1},{4,6},{5,7},{6,4},{7,5},{8,10},{9,11},{10,... | collective-permute-start | bytes 196616 | tf_op jit(solution)/shard_map/ppermute | solution.py:47
  25.0 5.9 %collective-permute-start.31 = (bf16[128,256]{1,0:T(8,128)(2,1)S(1)}, bf16[128,256]{1,0:T(8,128)(2,1)S(1)}, u32[]{:S(2)}, u32[]{:S(2)}) collective-permute-start(bf16[128,256]{1,0:T(8,128)(2,1)S(1)} %get-tuple-element.109), channel_id=1, source_target_pairs={{0,1},{1,0},{2,3},{3,2},{4,5},{5,4},{6,7},{7,6},{8,9},{9,8},{10,11... | collective-permute-start | bytes 196616 | tf_op jit(solution)/shard_map/ppermute | solution.py:47
  27.3 8.1 %copy-start.3 = (f32[128,256]{1,0:T(8,128)S(1)}, f32[128,256]{1,0:T(8,128)}, u32[]{:S(2)}) copy-start(f32[128,256]{1,0:T(8,128)} %table_ref.3) | copy-start | bytes 393220
  27.3 8.1 %copy-start.10 = (f32[128]{0:T(128)S(1)}, f32[128]{0:T(128)}, u32[]{:S(2)}) copy-start(f32[128]{0:T(128)} %param.40) | copy-start | bytes 1540
  28.7 17.1 %copy-start.1 = (f32[512,256]{1,0:T(8,128)S(1)}, f32[512,256]{1,0:T(8,128)}, u32[]{:S(2)}) copy-start(f32[512,256]{1,0:T(8,128)} %table_ref.2) | copy-start | bytes 1572868
  30.9 4.4 %collective-permute-start.8 = (bf16[128,256]{1,0:T(8,128)(2,1)S(1)}, bf16[128,256]{1,0:T(8,128)(2,1)}, u32[]{:S(2)}, u32[]{:S(2)}) collective-permute-start(bf16[128,256]{1,0:T(8,128)(2,1)S(1)} %param.8), channel_id=1, source_target_pairs={{0,8},{4,12},{8,0},{12,4},{16,24},{20,28},{24,16},{28,20},{1,9},{5... | collective-permute-start | bytes 196616 | tf_op jit(solution)/shard_map/cond/branch_1_fun/ppermute | solution.py:33
  36.4 4.4 %collective-permute-start.17 = (bf16[128,256]{1,0:T(8,128)(2,1)S(1)}, bf16[128,256]{1,0:T(8,128)(2,1)}, u32[]{:S(2)}, u32[]{:S(2)}) collective-permute-start(bf16[128,256]{1,0:T(8,128)(2,1)S(1)} %param.17), channel_id=1, source_target_pairs={{0,16},{4,20},{8,24},{12,28},{16,0},{20,4},{24,8},{28,12},{1,17},{... | collective-permute-start | bytes 196616 | tf_op jit(solution)/shard_map/cond/branch_3_fun/ppermute | solution.py:33
  40.8 8.0 %collective-permute-start.36 = (bf16[128,256]{1,0:T(8,128)(2,1)}, bf16[128,256]{1,0:T(8,128)(2,1)S(1)}, u32[]{:S(2)}, u32[]{:S(2)}) collective-permute-start(bf16[128,256]{1,0:T(8,128)(2,1)} %get-tuple-element.130.dst_ref), channel_id=1, source_target_pairs={{0,1},{1,0},{2,3},{3,2},{4,5},{5,4},{6,7},{7,6},{8,9},{9,8},{10,11... | collective-permute-start | bytes 196616 | tf_op jit(solution)/shard_map/ppermute | solution.py:47
  41.8 9.4 %collective-permute-start.35 = (bf16[128,256]{1,0:T(8,128)(2,1)}, bf16[128,256]{1,0:T(8,128)(2,1)S(1)}, u32[]{:S(2)}, u32[]{:S(2)}) collective-permute-start(bf16[128,256]{1,0:T(8,128)(2,1)} %get-tuple-element.130.dst_ref), channel_id=1, source_target_pairs={{0,2},{1,3},{2,0},{3,1},{4,6},{5,7},{6,4},{7,5},{8,10},{9,11},{10,... | collective-permute-start | bytes 196616 | tf_op jit(solution)/shard_map/ppermute | solution.py:47
  45.8 0.7 copy-start.7
  47.1 6.3 %collective-permute-start.34 = (bf16[128,256]{1,0:T(8,128)(2,1)}, bf16[128,256]{1,0:T(8,128)(2,1)S(1)}, u32[]{:S(2)}, u32[]{:S(2)}) collective-permute-start(bf16[128,256]{1,0:T(8,128)(2,1)} %get-tuple-element.130.dst_ref), channel_id=1, source_target_pairs={{0,3},{1,2},{2,1},{3,0},{4,7},{5,6},{6,5},{7,4},{8,11},{9,10},{10,... | collective-permute-start | bytes 196616 | tf_op jit(solution)/shard_map/ppermute | solution.py:47
  55.4 8.6 %collective-permute-start.39 = (bf16[128,256]{1,0:T(8,128)(2,1)S(1)}, bf16[128,256]{1,0:T(8,128)(2,1)S(1)}, u32[]{:S(2)}, u32[]{:S(2)}) collective-permute-start(bf16[128,256]{1,0:T(8,128)(2,1)S(1)} %get-tuple-element.124), channel_id=1, source_target_pairs={{0,3},{1,2},{2,1},{3,0},{4,7},{5,6},{6,5},{7,4},{8,11},{9,10},{10,... | collective-permute-start | bytes 196616 | tf_op jit(solution)/shard_map/ppermute | solution.py:47
  57.2 6.8 %collective-permute-start.38 = (bf16[128,256]{1,0:T(8,128)(2,1)S(1)}, bf16[128,256]{1,0:T(8,128)(2,1)S(1)}, u32[]{:S(2)}, u32[]{:S(2)}) collective-permute-start(bf16[128,256]{1,0:T(8,128)(2,1)S(1)} %get-tuple-element.123), channel_id=1, source_target_pairs={{0,2},{1,3},{2,0},{3,1},{4,6},{5,7},{6,4},{7,5},{8,10},{9,11},{10,... | collective-permute-start | bytes 196616 | tf_op jit(solution)/shard_map/ppermute | solution.py:47
  57.2 6.8 %collective-permute-start.37 = (bf16[128,256]{1,0:T(8,128)(2,1)S(1)}, bf16[128,256]{1,0:T(8,128)(2,1)S(1)}, u32[]{:S(2)}, u32[]{:S(2)}) collective-permute-start(bf16[128,256]{1,0:T(8,128)(2,1)S(1)} %get-tuple-element.122), channel_id=1, source_target_pairs={{0,1},{1,0},{2,3},{3,2},{4,5},{5,4},{6,7},{7,6},{8,9},{9,8},{10,11... | collective-permute-start | bytes 196616 | tf_op jit(solution)/shard_map/ppermute | solution.py:47
  64.0 4.4 %collective-permute-start.24 = (bf16[128,256]{1,0:T(8,128)(2,1)S(1)}, bf16[128,256]{1,0:T(8,128)(2,1)}, u32[]{:S(2)}, u32[]{:S(2)}) collective-permute-start(bf16[128,256]{1,0:T(8,128)(2,1)S(1)} %param.24), channel_id=1, source_target_pairs={{0,16},{4,20},{8,24},{12,28},{16,0},{20,4},{24,8},{28,12},{1,17},{... | collective-permute-start | bytes 196616 | tf_op jit(solution)/shard_map/cond/branch_3_fun/ppermute | solution.py:33
where the time goes:
time: 70.5 us; the launch traced here: 70.1 us
  starting transfers between devices  23.7 us (34%)
  Pallas kernels  21.5 us (30%)
  waiting for transfers between devices  19.3 us (27%)
  local copies, waits for them, and re-layouts  3.32 us (5%)
  between operations  2.17 us (3%)
    ppermute x12, starting transfers between devices, rep_send(): lax.ppermute(rows, 'rep', [(r, r ^ offset) for r in range(lax.axis_size('...  18.2 us
    ppermute x4, waiting for transfers between devices, branch(): lax.ppermute(x, 'bucket', [(b, b ^ value << first) for b in range(buckets)])  13.4 us
    pallas_call x8, Pallas kernels, tile_work(): pl.pallas_call(functools.partial(tile_kernel, block, number, room, len(ca...  13 us
    ppermute x12, waiting for transfers between devices, rep_send(): lax.ppermute(rows, 'rep', [(r, r ^ offset) for r in range(lax.axis_size('...  5.83 us
    ppermute x4, starting transfers between devices, branch(): lax.ppermute(x, 'bucket', [(b, b ^ value << first) for b in range(buckets)])  5.48 us
    pallas_call x4, Pallas kernels, adagrad(): pl.pallas_call(adagrad_kernel, in_specs=[VMEM] * 3, out_specs=[VMEM] * 3,...  4.75 us
    unnamed x22, local copies, waits for them, and re-layouts  3.32 us
    pallas_call x1, Pallas kernels, per_device(): pl.pallas_call(functools.partial(later_kernel, k + 1, shard_blocks, numbe...  2.32 us
  transfers between devices with their start and end apart: 16, of which 9 were waited for; matrix products, arithmetic and copies ran while one was open for 0% of the time, Pallas kernels for 21%

commit v1 on v0

v1 whole, which is shorter than its diff:
```python
import functools

import jax
import jax.numpy as jnp
from jax import lax
from jax.experimental import pallas as pl
from jax.experimental.pallas import tpu as pltpu
from jax.sharding import PartitionSpec as P

TILE = 128
GROUP = 4
LOW_BITS = 3
SHIFT = 16

learn_rate = 0.1

AXES = ("bucket", "rep")
SMEM = pl.BlockSpec(memory_space=pltpu.SMEM)
VMEM = pl.BlockSpec(memory_space=pltpu.VMEM)
FIRST_GRANT = 60 * 1024 * 1024
GRANT = pltpu.CompilerParams(vmem_limit_bytes=12 * 1024 * 1024)


def bucket_send(rows, mask):
    buckets = lax.axis_size("bucket")
    bits = buckets.bit_length() - 1
    for first in range(0, bits, LOW_BITS):
        width = min(LOW_BITS, bits - first)
        least = 1 if width == bits else 0

        def branch(value, x, first=first):
            if value == 0:
                return x
            return lax.ppermute(x, "bucket", [(b, b ^ (value << first)) for b in range(buckets)])

        if width == bits:
            index = mask - 1
        else:
            index = jnp.bitwise_and(jnp.right_shift(mask, first), (1 << width) - 1)
        branches = [functools.partial(branch, value) for value in range(least, 1 << width)]
        rows = lax.switch(index, branches, rows)
    return rows


def rep_send(rows, offset):
    if offset == 0:
        return rows
    return lax.ppermute(rows, "rep", [(r, r ^ offset) for r in range(lax.axis_size("rep"))])


def layout(number, slots):
    most = slots // GROUP + number + 3
    first = 2
    second = first + most
    start = second + most
    room = 1 << (slots + 2 * GROUP - 1).bit_length()
    return first, second, start, room, start + number * room


def sort_tiles(k, own, none_rel, flip, number, tiles, rel, counts, plan):
    bits = number.bit_length() - 1
    first, second, start, room, _ = layout(number, tiles.shape[1])

    def place(t, ends):
        code = tiles[k, t]
        e = jnp.bitwise_xor(jnp.bitwise_and(code, number - 1), flip)
        p = ends[0]
        for i in range(1, number):
            p = jnp.where(e == i, ends[i], p)
        plan[0, start + e * room + p] = jnp.bitwise_or(
            jnp.left_shift(jnp.right_shift(code, bits), SHIFT), rel[k, t]
        )
        return tuple(ends[i] + jnp.where(e == i, 1, 0) for i in range(number))

    ends = lax.fori_loop(0, counts[k], place, (jnp.int32(0),) * number)
    for i in range(number):
        for extra in range(2 * GROUP):
            plan[0, start + i * room + ends[i] + extra] = jnp.int32(none_rel)
    for index, at, blocks in ((0, first, range(own, number)), (1, second, range(own))):
        q = jnp.int32(0)
        for i in blocks:
            amount = jnp.right_shift(ends[i] + (GROUP - 1), GROUP.bit_length() - 1)

            def name(g, carry, i=i, q=q, at=at):
                plan[0, at + q + g] = i * room + g * GROUP
                return carry

            lax.fori_loop(0, amount, name, 0)
            q = q + amount
        plan[0, index] = q
        for extra in range(3):
            plan[0, at + q + extra] = blocks[0] * room


def first_kernel(rounds, number, none_rel, rep, tiles, rel, counts, partners, dst_ref, plan, rows_ref, *masks):
    own = dst_ref.shape[0] // TILE
    rows_ref[...] = dst_ref[...].astype(jnp.bfloat16)
    for k in range(rounds):
        masks[k][0, 0] = partners[k, 0]
    sort_tiles(0, own, none_rel, rep[0] * own, number, tiles, rel, counts, plan)


def later_kernel(k, own, number, none_rel, rep, tiles, rel, counts, after, plan):
    sort_tiles(k, own, none_rel, rep[0] * own, number, tiles, rel, counts, plan)


def round_kernel(src_ref, rel_ref, low_ref, row_ref):
    rels, width = rel_ref.shape
    low_ref[...] = src_ref[...].astype(jnp.bfloat16).astype(jnp.float32)
    row_ref[pl.ds(0, rels), :] = rel_ref[...] * (0.5 * width**-0.5)
    row_ref[pl.ds(rels, 8), :] = jnp.zeros((8, width), jnp.float32)


def round_source(src_table, rel_table):
    return pl.pallas_call(
        round_kernel,
        in_specs=[VMEM] * 2,
        out_specs=[VMEM] * 2,
        out_shape=[
            jax.ShapeDtypeStruct(src_table.shape, jnp.float32),
            jax.ShapeDtypeStruct((rel_table.shape[0] + 8, rel_table.shape[1]), jnp.float32),
        ],
        cost_estimate=pl.CostEstimate(
            flops=src_table.size, bytes_accessed=8 * src_table.size, transcendentals=0
        ),
        compiler_params=GRANT,
        name="round_source",
    )(src_table, rel_table)


def tile_kernel(index, lists, shards, carried, plan, low_ref, row_ref, *refs):
    dst_refs, refs = refs[:shards], refs[shards + carried :]
    src_grad, parts, refs = refs[0], refs[1 : 1 + shards], refs[1 + shards :]
    dst_all, dst_grad, held_rows, held_slope = refs
    _, _, start, room, _ = lists
    at_list = lists[index]
    rows_of_shard = dst_refs[0].shape[0]
    first_row = rows_of_shard if index == 0 else 0
    if not carried:
        src_grad[...] = jnp.zeros_like(src_grad)
    for i in range(shards):
        dst_all[pl.ds(i * rows_of_shard, rows_of_shard), :] = dst_refs[i][...]
    dst_grad[...] = jnp.zeros_like(dst_grad)
    row_id = lax.broadcasted_iota(jnp.int32, (TILE, TILE), 0)
    column_id = lax.broadcasted_iota(jnp.int32, (TILE, TILE), 1)
    offset = jnp.where(row_id == column_id, -1.0, 1.0).astype(jnp.float32)
    steps = plan[0, index]

    def group(q):
        at = plan[0, at_list + q]
        block = jnp.right_shift(at, room.bit_length() - 1)
        where, rows = [], []
        for g in range(GROUP):
            code = plan[0, start + at + g]
            where.append(pl.multiple_of(jnp.right_shift(code, SHIFT) * TILE, TILE))
            rows.append(row_ref[pl.ds(jnp.bitwise_and(code, (1 << SHIFT) - 1), 1), :])
        return pl.ds(pl.multiple_of(block * TILE - first_row, TILE), TILE), where, rows

    def slopes(q, slot):
        dst_rows, where, rows = group(q)
        src_rel = jnp.concatenate(
            [(low_ref[pl.ds(s, TILE), :] * row).astype(jnp.bfloat16) for s, row in zip(where, rows)], 0
        )
        scores = lax.dot_general(
            src_rel, dst_all[dst_rows, :], (((1,), (1,)), ((), ())), preferred_element_type=jnp.float32
        )
        slope = jnp.concatenate(
            [
                (jnp.tanh(scores[g * TILE : (g + 1) * TILE]) + offset).astype(jnp.bfloat16)
                for g in range(GROUP)
            ],
            0,
        )
        held_rows[slot] = src_rel
        held_slope[slot] = slope

    def grads(q, slot):
        dst_rows, where, rows = group(q)
        slope = held_slope[slot]
        src_terms = jnp.dot(slope, dst_all[dst_rows, :], preferred_element_type=jnp.float32)
        dst_grad[dst_rows, :] += lax.dot_general(
            slope, held_rows[slot], (((0,), (0,)), ((), ())), preferred_element_type=jnp.float32
        )
        for g in range(GROUP):
            src_grad[pl.ds(where[g], TILE), :] += src_terms[g * TILE : (g + 1) * TILE] * rows[g]

    @pl.when(steps > 0)
    def _():
        slopes(0, 0)

        def two(p, carry):
            q = p * 2
            slopes(q + 1, 1)
            grads(q, 0)
            slopes(q + 2, 0)
            grads(q + 1, 1)
            return carry

        lax.fori_loop(0, jnp.right_shift(steps, 1), two, 0)

        @pl.when(jnp.bitwise_and(steps, 1) == 1)
        def _():
            grads(steps - 1, 0)

    for i in range(shards):
        parts[i][...] = dst_grad[pl.ds(i * rows_of_shard, rows_of_shard), :].astype(jnp.bfloat16)


def tile_work(index, lists, slots, plan, low, rel_rows, shards, src_grad):
    rows, width = shards[0].shape
    carried = [] if src_grad is None else [src_grad]
    out = pl.pallas_call(
        functools.partial(tile_kernel, index, lists, len(shards), len(carried)),
        in_specs=[SMEM] + [VMEM] * (2 + len(shards) + len(carried)),
        out_specs=[VMEM] * (1 + len(shards)),
        out_shape=[jax.ShapeDtypeStruct(low.shape, jnp.float32)]
        + [jax.ShapeDtypeStruct((rows, width), jnp.bfloat16)] * len(shards),
        scratch_shapes=[
            pltpu.VMEM((len(shards) * rows, width), jnp.bfloat16),
            pltpu.VMEM((len(shards) * rows, width), jnp.float32),
            pltpu.VMEM((2, GROUP * TILE, width), jnp.bfloat16),
            pltpu.VMEM((2, GROUP * TILE, TILE), jnp.bfloat16),
        ],
        input_output_aliases={3 + len(shards): 0} if carried else {},
        cost_estimate=pl.CostEstimate(
            flops=6 * slots * TILE * TILE * width,
            bytes_accessed=4 * low.size,
            transcendentals=slots * TILE * TILE,
        ),
        compiler_params=GRANT,
        name="tile_work",
    )(plan, low, rel_rows, *shards, *carried)
    return out[0], list(out[1:])


def adagrad_kernel(table_ref, state_ref, grad_ref, table_out, state_out, low_out):
    width = table_ref.shape[1]
    row_id = lax.broadcasted_iota(jnp.int32, (TILE, TILE), 0)
    column_id = lax.broadcasted_iota(jnp.int32, (TILE, TILE), 1)
    same = row_id == column_id

    def block(i, carry):
        rows = pl.ds(pl.multiple_of(i * TILE, TILE), TILE)
        grad = grad_ref[rows, :].astype(jnp.float32)
        state = jnp.sum(jnp.where(same, state_ref[pl.ds(i, 1), :], 0.0), axis=1, keepdims=True)
        state = state + jnp.sum(grad * grad, axis=1, keepdims=True) * (1.0 / width)
        state_out[pl.ds(i, 1), :] = jnp.sum(jnp.where(same, state, 0.0), axis=0, keepdims=True)
        table = table_ref[rows, :] - learn_rate * grad / jnp.sqrt(state)
        table_out[rows, :] = table
        low_out[rows, :] = table.astype(jnp.bfloat16).astype(low_out.dtype)
        return carry

    lax.fori_loop(0, table_ref.shape[0] // TILE, block, 0)


def adagrad(table, state, grad, low_type):
    return pl.pallas_call(
        adagrad_kernel,
        in_specs=[VMEM] * 3,
        out_specs=[VMEM] * 3,
        out_shape=[
            jax.ShapeDtypeStruct(table.shape, jnp.float32),
            jax.ShapeDtypeStruct(state.shape, jnp.float32),
            jax.ShapeDtypeStruct(table.shape, low_type),
        ],
        cost_estimate=pl.CostEstimate(
            flops=8 * table.size, bytes_accessed=8 * table.size, transcendentals=table.shape[0]
        ),
        compiler_params=GRANT,
        name="adagrad",
    )(table, state, grad)


def per_device(
    src_table, src_state, dst_table, dst_state, rel_table, partners, tiles, tile_rel, counts
):
    reps = lax.axis_size("rep")
    rounds = partners.shape[0]
    src_state = src_state.reshape(-1, TILE)
    dst_state = dst_state.reshape(-1, TILE)
    shard_blocks = dst_table.shape[0] // TILE
    number = reps * shard_blocks
    slots = tiles.shape[-1]
    lists = layout(number, slots)
    none_rel = rel_table.shape[0]
    scalars = (
        lax.axis_index("rep").astype(jnp.int32).reshape(1), tiles[0, 0], tile_rel[0, 0], counts[0, 0],
    )
    plan_shape = jax.ShapeDtypeStruct((1, lists[-1]), jnp.int32)
    plan, rows, *masks = pl.pallas_call(
        functools.partial(first_kernel, rounds, number, none_rel),
        in_specs=[SMEM] * 5 + [VMEM],
        out_specs=[SMEM, VMEM] + [SMEM] * rounds,
        out_shape=[plan_shape, jax.ShapeDtypeStruct(dst_table.shape, jnp.bfloat16)]
        + [jax.ShapeDtypeStruct((1, 1), jnp.int32)] * rounds,
        compiler_params=pltpu.CompilerParams(vmem_limit_bytes=FIRST_GRANT),
        name="first",
    )(*scalars, partners, dst_table)
    for k in range(rounds):
        mask = masks[k].reshape(())
        own = bucket_send(rows, mask)
        others = []
        for j in range(1, reps):
            others.append(rep_send(own, j))
        if k == 0:
            low, rel_rows = round_source(src_table, rel_table)
        src_grad, parts = tile_work(0, lists, slots, plan, low, rel_rows, others, None)
        for j in range(1, reps):
            parts[j - 1] = rep_send(parts[j - 1], j)
        src_grad, mine = tile_work(
            1, lists, slots // reps, plan, low, rel_rows, [own], src_grad
        )
        total = functools.reduce(jnp.add, [x.astype(jnp.float32) for x in mine + parts])
        if k + 1 < rounds:
            plan = pl.pallas_call(
                functools.partial(later_kernel, k + 1, shard_blocks, number, none_rel),
                in_specs=[SMEM] * 4 + [pl.BlockSpec(memory_space=pl.ANY)],
                out_specs=SMEM,
                out_shape=plan_shape,
                compiler_params=GRANT,
                name="later",
            )(*scalars, src_grad)
        src_table, src_state, low = adagrad(src_table, src_state, src_grad, jnp.float32)
        total = bucket_send(total.astype(jnp.bfloat16), mask)
        dst_table, dst_state, rows = adagrad(dst_table, dst_state, total, jnp.bfloat16)
    return (src_table, src_state.reshape(-1), dst_table, dst_state.reshape(-1))


def solution(mesh):
    table, state = P(AXES, None), P(AXES)
    in_specs = (
        table,
        state,
        table,
        state,
        P(),
        P(),
        P("bucket", "rep", None, None),
        P("bucket", "rep", None, None),
        P("bucket", "rep", None),
    )
    return jax.shard_map(
        per_device,
        mesh=mesh,
        in_specs=in_specs,
        out_specs=(table, state, table, state),
        check_vma=False,
    )
```

time: 70.5 us -> 68.8 us (0.976)
  waiting for transfers between devices: 19.3 us -> 22.6 us
  Pallas kernels: 21.5 us -> 19 us
  local copies, waits for them, and re-layouts: 3.32 us -> 1.08 us
    ppermute x12, waiting for transfers between devices: 5.83 us -> 8.87 us  [rep_send(): lax.ppermute(rows, 'rep', [(r, r ^ offset) for r in range(lax.axis_size('...]
    pallas_call x9 -> x5, Pallas kernels: 14.4 us -> 11.8 us  [the longest x4 10 us: tile_work(): pl.pallas_call(functools.partial(tile_kernel, index, lists, len(shards),...]
    unnamed x22 -> x20, local copies, waits for them, and re-layouts: 3.32 us -> 1.08 us
  transfers between devices with their start and end apart: 16 -> 16, of which waited for: 9 -> 10; matrix products, arithmetic and copies ran while one was open for 0% -> 0% of each run, Pallas kernels for 21% -> 13%
where the time goes in v1:
time: 68.8 us; the launch traced here: 68.4 us
  starting transfers between devices  23.5 us (34%)
  waiting for transfers between devices  22.6 us (33%)
  Pallas kernels  19 us (28%)
  between operations  2.11 us (3%)
  local copies, waits for them, and re-layouts  1.08 us (2%)
    ppermute x12, starting transfers between devices, rep_send(): lax.ppermute(rows, 'rep', [(r, r ^ offset) for r in range(lax.axis_size('...  18.2 us
    ppermute x4, waiting for transfers between devices, branch(): lax.ppermute(x, 'bucket', [(b, b ^ value << first) for b in range(buckets)])  13.7 us
    pallas_call x4, Pallas kernels, tile_work(): pl.pallas_call(functools.partial(tile_kernel, index, lists, len(shards),...  10 us
    ppermute x12, waiting for transfers between devices, rep_send(): lax.ppermute(rows, 'rep', [(r, r ^ offset) for r in range(lax.axis_size('...  8.87 us
    ppermute x4, starting transfers between devices, branch(): lax.ppermute(x, 'bucket', [(b, b ^ value << first) for b in range(buckets)])  5.25 us
    pallas_call x4, Pallas kernels, adagrad(): pl.pallas_call(adagrad_kernel, in_specs=[VMEM] * 3, out_specs=[VMEM] * 3,...  4.76 us
    pallas_call x1, Pallas kernels, per_device(): pl.pallas_call(functools.partial(later_kernel, k + 1, shard_blocks, numbe...  2.44 us
    pallas_call x1, Pallas kernels, per_device(): pl.pallas_call(functools.partial(first_kernel, rounds, number, none_rel),...  1.75 us
  transfers between devices with their start and end apart: 16, of which 10 were waited for; matrix products, arithmetic and copies ran while one was open for 0% of the time, Pallas kernels for 13%

profile of v1, /device:TPU:0, one launch (start us, length us, event | category | flops | bytes accessed | tf_op | source)
XLA Modules:
  0.0 68.4 jit_solution(8014339772521862532)
XLA Ops:
  0.6 1.7 %first.1 = (s32[1,560]{1,0:T(1,128)}, bf16[128,256]{1,0:T(8,128)(2,1)S(1)}, s32[1,1]{1,0:T(1,128)}, s32[1,1]{1,0:T(1,128)}) custom-call(s32[1]{0:T(128)} %bitcast.1.rep, s32[2,64]{1,0:T(2,128)} %bitcast.10, s32[2,64]{1,0:T(2,128)} %bitcast.12, s32[2]{0:T(128)} %bitcast.15, s32[2,8]{1,0:T(2,128)} %partners.1, f32[128,256]{1,0:T(8,128)} %table_ref.3), custom_call_target="tpu_custom_call" | custom-call | tf_op jit(solution)/shard_map/first/pallas_call | solution.py:290
  3.0 5.7 %conditional.4 = (bf16[128,256]{1,0:T(8,128)(2,1)}) conditional(s32[]{:T(128)} %bitcast.5, bf16[128,256]{1,0:T(8,128)(2,1)S(1)} %get-tuple-element.96, bf16[128,256]{1,0:T(8,128)(2,1)S(1)} %get-tuple-element.96, bf16[128,256]{1,0:T(8,128)(2,1)S(1)} %get-tuple-element.96, ...), branch_computations={%region_0.0_spmd, %region_1.0_spmd, %region_2.0_spmd, %region_3.0_... | conditional | bytes 262192 | solution.py:41
  3.1 3.3 %collective-permute-start.1 = (bf16[128,256]{1,0:T(8,128)(2,1)S(1)}, bf16[128,256]{1,0:T(8,128)(2,1)}, u32[]{:S(2)}, u32[]{:S(2)}) collective-permute-start(bf16[128,256]{1,0:T(8,128)(2,1)S(1)} %param.1), channel_id=1, source_target_pairs={{0,8},{4,12},{8,0},{12,4},{16,24},{20,28},{24,16},{28,20},{1,9},{5... | collective-permute-start | bytes 196616 | tf_op jit(solution)/shard_map/cond/branch_1_fun/ppermute | solution.py:34
  6.4 2.4 %collective-permute-done.1 = bf16[128,256]{1,0:T(8,128)(2,1)} collective-permute-done((bf16[128,256]{1,0:T(8,128)(2,1)S(1)}, bf16[128,256]{1,0:T(8,128)(2,1)}, u32[]{:S(2)}, u32[]{:S(2)}) %collective-permute-start.1) | collective-permute-done | bytes 65568 | tf_op jit(solution)/shard_map/cond/branch_1_fun/ppermute | solution.py:34
  8.7 4.4 %collective-permute-start.30 = (bf16[128,256]{1,0:T(8,128)(2,1)}, bf16[128,256]{1,0:T(8,128)(2,1)S(1)}, u32[]{:S(2)}, u32[]{:S(2)}) collective-permute-start(bf16[128,256]{1,0:T(8,128)(2,1)} %get-tuple-element.120.refs_0_), channel_id=1, source_target_pairs={{0,3},{1,2},{2,1},{3,0},{4,7},{5,6},{6,5},{7,4},{8,11},{9,10},{10,... | collective-permute-start | bytes 196616 | tf_op jit(solution)/shard_map/ppermute | solution.py:48
  13.1 0.0 collective-permute-start.29
  13.1 0.6 collective-permute-start.28
  13.6 1.0 %copy-done = f32[512,256]{1,0:T(8,128)S(1)} copy-done((f32[512,256]{1,0:T(8,128)S(1)}, f32[512,256]{1,0:T(8,128)}, u32[]{:S(2)}) %copy-start) | copy-done | bytes 524312
  14.7 0.0 copy-start.9
  14.7 1.4 %collective-permute-done.30.refs_2_ = bf16[128,256]{1,0:T(8,128)(2,1)S(1)} collective-permute-done((bf16[128,256]{1,0:T(8,128)(2,1)}, bf16[128,256]{1,0:T(8,128)(2,1)S(1)}, u32[]{:S(2)}, u32[]{:S(2)}) %collective-permute-start.30) | collective-permute-done | bytes 65568 | tf_op jit(solution)/shard_map/ppermute | solution.py:48
  16.1 2.7 %collective-permute-done.29.refs_1_ = bf16[128,256]{1,0:T(8,128)(2,1)S(1)} collective-permute-done((bf16[128,256]{1,0:T(8,128)(2,1)}, bf16[128,256]{1,0:T(8,128)(2,1)S(1)}, u32[]{:S(2)}, u32[]{:S(2)}) %collective-permute-start.29) | collective-permute-done | bytes 65568 | tf_op jit(solution)/shard_map/ppermute | solution.py:48
  18.8 0.1 collective-permute-done.28.refs_0_
  19.0 1.7 %tile_work.4 = (f32[512,256]{1,0:T(8,128)S(1)}, bf16[128,256]{1,0:T(8,128)(2,1)S(1)}, bf16[128,256]{1,0:T(8,128)(2,1)S(1)}, bf16[128,256]{1,0:T(8,128)(2,1)S(1)}) custom-call(s32[1,560]{1,0:T(1,128)S(1)} %copy-done.9, f32[512,256]{1,0:T(8,128)S(1)} %get-tuple-element.93.low_ref, f32[72,256]{1,0:T(8,128)S(1)} %get-tuple-element.94.row_ref, ...), custom_call_target="tpu_custom_call" | custom-call | flops 1610612736 | bytes 524288 | tf_op jit(solution)/shard_map/tile_work/pallas_call | solution.py:212
  20.7 1.5 %collective-permute-start.31 = (bf16[128,256]{1,0:T(8,128)(2,1)S(1)}, bf16[128,256]{1,0:T(8,128)(2,1)S(1)}, u32[]{:S(2)}, u32[]{:S(2)}) collective-permute-start(bf16[128,256]{1,0:T(8,128)(2,1)S(1)} %get-tuple-element.104), channel_id=1, source_target_pairs={{0,1},{1,0},{2,3},{3,2},{4,5},{5,4},{6,7},{7,6},{8,9},{9,8},{10,11... | collective-permute-start | bytes 196616 | tf_op jit(solution)/shard_map/ppermute | solution.py:48
  22.2 1.8 %collective-permute-start.32 = (bf16[128,256]{1,0:T(8,128)(2,1)S(1)}, bf16[128,256]{1,0:T(8,128)(2,1)S(1)}, u32[]{:S(2)}, u32[]{:S(2)}) collective-permute-start(bf16[128,256]{1,0:T(8,128)(2,1)S(1)} %get-tuple-element.105), channel_id=1, source_target_pairs={{0,2},{1,3},{2,0},{3,1},{4,6},{5,7},{6,4},{7,5},{8,10},{9,11},{10,... | collective-permute-start | bytes 196616 | tf_op jit(solution)/shard_map/ppermute | solution.py:48
  24.0 1.1 %collective-permute-start.33 = (bf16[128,256]{1,0:T(8,128)(2,1)S(1)}, bf16[128,256]{1,0:T(8,128)(2,1)S(1)}, u32[]{:S(2)}, u32[]{:S(2)}) collective-permute-start(bf16[128,256]{1,0:T(8,128)(2,1)S(1)} %get-tuple-element.106), channel_id=1, source_target_pairs={{0,3},{1,2},{2,1},{3,0},{4,7},{5,6},{6,5},{7,4},{8,11},{9,10},{10,... | collective-permute-start | bytes 196616 | tf_op jit(solution)/shard_map/ppermute | solution.py:48
  25.8 0.0 copy-start.2
  25.8 0.0 copy-start.8
  25.8 1.4 %tile_work.5 = (f32[512,256]{1,0:T(8,128)S(1)}, bf16[128,256]{1,0:T(8,128)(2,1)S(1)}) custom-call(s32[1,560]{1,0:T(1,128)S(1)} %copy-done.9, f32[512,256]{1,0:T(8,128)S(1)} %get-tuple-element.93.low_ref, f32[72,256]{1,0:T(8,128)S(1)} %get-tuple-element.94.row_ref, bf16[128,256]{1,0:T(8,128)(2,1)} %get-tuple-element.120.refs_0_, ...), custom_call_target="tpu_custom_call", output_to_operand_aliasing={{0}: (4, {})} | custom-call | flops 402653184 | bytes 524288 | tf_op jit(solution)/shard_map/tile_work/pallas_call | solution.py:212
  27.3 0.0 collective-permute-done.31
  27.3 3.6 %collective-permute-done.32 = bf16[128,256]{1,0:T(8,128)(2,1)S(1)} collective-permute-done((bf16[128,256]{1,0:T(8,128)(2,1)S(1)}, bf16[128,256]{1,0:T(8,128)(2,1)S(1)}, u32[]{:S(2)}, u32[]{:S(2)}) %collective-permute-start.32) | collective-permute-done | bytes 65568 | tf_op jit(solution)/shard_map/ppermute | solution.py:48
  30.9 0.0 collective-permute-done.33
  30.9 4.5 %conditional.5 = (bf16[128,256]{1,0:T(8,128)(2,1)}) conditional(s32[]{:T(128)} %bitcast.5, bf16[128,256]{1,0:T(8,128)(2,1)S(1)} %add_convert_fusion.1, bf16[128,256]{1,0:T(8,128)(2,1)S(1)} %add_convert_fusion.1, bf16[128,256]{1,0:T(8,128)(2,1)S(1)} %add_convert_fusion.1, ...), branch_computations={%region_7.0_spmd, %region_8.0_spmd, %region_9.0_spmd, %region_10.0... | conditional | bytes 262192 | solution.py:41
  30.9 0.1 collective-permute-start.8
  31.0 4.4 %collective-permute-done.8 = bf16[128,256]{1,0:T(8,128)(2,1)} collective-permute-done((bf16[128,256]{1,0:T(8,128)(2,1)S(1)}, bf16[128,256]{1,0:T(8,128)(2,1)}, u32[]{:S(2)}, u32[]{:S(2)}) %collective-permute-start.8) | collective-permute-done | bytes 65568 | tf_op jit(solution)/shard_map/cond/branch_1_fun/ppermute | solution.py:34
  35.4 1.0 %adagrad.5 = (f32[128,256]{1,0:T(8,128)S(1)}, f32[1,128]{1,0:T(1,128)S(1)}, bf16[128,256]{1,0:T(8,128)(2,1)S(1)}) custom-call(f32[128,256]{1,0:T(8,128)S(1)} %copy-done.2, f32[1,128]{1,0:T(1,128)S(1)} %bitcast.17, bf16[128,256]{1,0:T(8,128)(2,1)} %get-tuple-element.121.grad_ref), custom_call_target="tpu_custom_call" | custom-call | flops 262144 | bytes 262144 | tf_op jit(solution)/shard_map/adagrad/pallas_call | solution.py:257
  36.4 4.5 %conditional.6 = (bf16[128,256]{1,0:T(8,128)(2,1)}) conditional(s32[]{:T(128)} %bitcast.6, bf16[128,256]{1,0:T(8,128)(2,1)S(1)} %get-tuple-element.107, bf16[128,256]{1,0:T(8,128)(2,1)S(1)} %get-tuple-element.107, bf16[128,256]{1,0:T(8,128)(2,1)S(1)} %get-tuple-element.107, ...), branch_computations={%region_14.0_spmd, %region_15.0_spmd, %region_16.0_spmd, %region_1... | conditional | bytes 262192 | solution.py:41
  36.4 1.8 %collective-permute-start.17 = (bf16[128,256]{1,0:T(8,128)(2,1)S(1)}, bf16[128,256]{1,0:T(8,128)(2,1)}, u32[]{:S(2)}, u32[]{:S(2)}) collective-permute-start(bf16[128,256]{1,0:T(8,128)(2,1)S(1)} %param.17), channel_id=1, source_target_pairs={{0,16},{4,20},{8,24},{12,28},{16,0},{20,4},{24,8},{28,12},{1,17},{... | collective-permute-start | bytes 196616 | tf_op jit(solution)/shard_map/cond/branch_3_fun/ppermute | solution.py:34
  38.2 2.6 %collective-permute-done.17 = bf16[128,256]{1,0:T(8,128)(2,1)} collective-permute-done((bf16[128,256]{1,0:T(8,128)(2,1)S(1)}, bf16[128,256]{1,0:T(8,128)(2,1)}, u32[]{:S(2)}, u32[]{:S(2)}) %collective-permute-start.17) | collective-permute-done | bytes 65568 | tf_op jit(solution)/shard_map/cond/branch_3_fun/ppermute | solution.py:34
  40.8 1.3 %collective-permute-start.36 = (bf16[128,256]{1,0:T(8,128)(2,1)}, bf16[128,256]{1,0:T(8,128)(2,1)S(1)}, u32[]{:S(2)}, u32[]{:S(2)}) collective-permute-start(bf16[128,256]{1,0:T(8,128)(2,1)} %get-tuple-element.122.refs_0_), channel_id=1, source_target_pairs={{0,3},{1,2},{2,1},{3,0},{4,7},{5,6},{6,5},{7,4},{8,11},{9,10},{10,... | collective-permute-start | bytes 196616 | tf_op jit(solution)/shard_map/ppermute | solution.py:48
  42.1 2.1 %collective-permute-start.35 = (bf16[128,256]{1,0:T(8,128)(2,1)}, bf16[128,256]{1,0:T(8,128)(2,1)S(1)}, u32[]{:S(2)}, u32[]{:S(2)}) collective-permute-start(bf16[128,256]{1,0:T(8,128)(2,1)} %get-tuple-element.122.refs_0_), channel_id=1, source_target_pairs={{0,2},{1,3},{2,0},{3,1},{4,6},{5,7},{6,4},{7,5},{8,10},{9,11},{10,... | collective-permute-start | bytes 196616 | tf_op jit(solution)/shard_map/ppermute | solution.py:48
  44.2 1.0 %collective-permute-start.34 = (bf16[128,256]{1,0:T(8,128)(2,1)}, bf16[128,256]{1,0:T(8,128)(2,1)S(1)}, u32[]{:S(2)}, u32[]{:S(2)}) collective-permute-start(bf16[128,256]{1,0:T(8,128)(2,1)} %get-tuple-element.122.refs_0_), channel_id=1, source_target_pairs={{0,1},{1,0},{2,3},{3,2},{4,5},{5,4},{6,7},{7,6},{8,9},{9,8},{10,11... | collective-permute-start | bytes 196616 | tf_op jit(solution)/shard_map/ppermute | solution.py:48
  45.2 2.4 %later.1.plan = s32[1,560]{1,0:T(1,128)S(1)} custom-call(s32[1]{0:T(128)} %bitcast.1.rep, s32[2,64]{1,0:T(2,128)S(1)} %bitcast.11, s32[2,64]{1,0:T(2,128)S(1)} %bitcast.13, s32[2]{0:T(128)S(1)} %bitcast.16, f32[512,256]{1,0:T(8,128)S(1)} %get-tuple-element.98.grad_ref.after), custom_call_target="tpu_custom_call" | custom-call | tf_op jit(solution)/shard_map/later/pallas_call | solution.py:315
  47.7 0.6 adagrad.4
  48.3 0.0 collective-permute-done.36.refs_2_
  48.3 0.6 collective-permute-done.35.refs_1_
  48.9 0.5 collective-permute-done.34.refs_0_
  49.4 4.3 %tile_work.6 = (f32[512,256]{1,0:T(8,128)S(1)}, bf16[128,256]{1,0:T(8,128)(2,1)S(1)}, bf16[128,256]{1,0:T(8,128)(2,1)S(1)}, bf16[128,256]{1,0:T(8,128)(2,1)S(1)}) custom-call(s32[1,560]{1,0:T(1,128)S(1)} %later.1.plan, f32[512,256]{1,0:T(8,128)S(1)} %get-tuple-element.101.low_ref, f32[72,256]{1,0:T(8,128)S(1)} %get-tuple-element.94.row_ref, ...), custom_call_target="tpu_custom_call" | custom-call | flops 1610612736 | bytes 524288 | tf_op jit(solution)/shard_map/tile_work/pallas_call | solution.py:212
  53.7 0.1 collective-permute-start.37
  53.8 1.9 %collective-permute-start.38 = (bf16[128,256]{1,0:T(8,128)(2,1)S(1)}, bf16[128,256]{1,0:T(8,128)(2,1)S(1)}, u32[]{:S(2)}, u32[]{:S(2)}) collective-permute-start(bf16[128,256]{1,0:T(8,128)(2,1)S(1)} %get-tuple-element.116), channel_id=1, source_target_pairs={{0,2},{1,3},{2,0},{3,1},{4,6},{5,7},{6,4},{7,5},{8,10},{9,11},{10,... | collective-permute-start | bytes 196616 | tf_op jit(solution)/shard_map/ppermute | solution.py:48
  55.7 2.5 %collective-permute-start.39 = (bf16[128,256]{1,0:T(8,128)(2,1)S(1)}, bf16[128,256]{1,0:T(8,128)(2,1)S(1)}, u32[]{:S(2)}, u32[]{:S(2)}) collective-permute-start(bf16[128,256]{1,0:T(8,128)(2,1)S(1)} %get-tuple-element.117), channel_id=1, source_target_pairs={{0,3},{1,2},{2,1},{3,0},{4,7},{5,6},{6,5},{7,4},{8,11},{9,10},{10,... | collective-permute-start | bytes 196616 | tf_op jit(solution)/shard_map/ppermute | solution.py:48
  58.2 2.5 %tile_work.7 = (f32[512,256]{1,0:T(8,128)S(1)}, bf16[128,256]{1,0:T(8,128)(2,1)S(1)}) custom-call(s32[1,560]{1,0:T(1,128)S(1)} %later.1.plan, f32[512,256]{1,0:T(8,128)S(1)} %get-tuple-element.101.low_ref, f32[72,256]{1,0:T(8,128)S(1)} %get-tuple-element.94.row_ref, bf16[128,256]{1,0:T(8,128)(2,1)} %get-tuple-element.122.refs_0_, ...), custom_call_target="tpu_custom_call", output_to_operand_aliasing={{0}: (4, {})} | custom-call | flops 402653184 | bytes 524288 | tf_op jit(solution)/shard_map/tile_work/pallas_call | solution.py:212
  60.7 1.6 %adagrad.6 = (f32[512,256]{1,0:T(8,128)}, f32[4,128]{1,0:T(4,128)}, f32[512,256]{1,0:T(8,128)}) custom-call(f32[512,256]{1,0:T(8,128)S(1)} %get-tuple-element.99.table_ref, f32[4,128]{1,0:T(4,128)S(1)} %get-tuple-element.100.state_ref, f32[512,256]{1,0:T(8,128)S(1)} %get-tuple-element.109.grad_ref), custom_call_target="tpu_custom_call" | custom-call | flops 1048576 | bytes 1048576 | tf_op jit(solution)/shard_map/adagrad/pallas_call | solution.py:257
  62.3 0.0 collective-permute-done.37
  62.3 4.5 %conditional.7 = (bf16[128,256]{1,0:T(8,128)(2,1)}) conditional(s32[]{:T(128)} %bitcast.6, bf16[128,256]{1,0:T(8,128)(2,1)S(1)} %add_convert_fusion, bf16[128,256]{1,0:T(8,128)(2,1)S(1)} %add_convert_fusion, bf16[128,256]{1,0:T(8,128)(2,1)S(1)} %add_convert_fusion, bf16[128,256]{1,0:T(8,128)(2,1)S(1)} %add_convert_fusion, ...), branch_computations={%region_21.0_spmd, %region_22.0_spmd, %region_23.0_spmd, %region_2... | conditional | bytes 262192 | solution.py:41
  62.4 0.1 collective-permute-start.24
  62.4 4.4 %collective-permute-done.24 = bf16[128,256]{1,0:T(8,128)(2,1)} collective-permute-done((bf16[128,256]{1,0:T(8,128)(2,1)S(1)}, bf16[128,256]{1,0:T(8,128)(2,1)}, u32[]{:S(2)}, u32[]{:S(2)}) %collective-permute-start.24) | collective-permute-done | bytes 65568 | tf_op jit(solution)/shard_map/cond/branch_3_fun/ppermute | solution.py:34
  66.8 1.6 %adagrad.7 = (f32[128,256]{1,0:T(8,128)}, f32[1,128]{1,0:T(1,128)}, bf16[128,256]{1,0:T(8,128)(2,1)}) custom-call(f32[128,256]{1,0:T(8,128)S(1)} %get-tuple-element.112.table_ref, f32[1,128]{1,0:T(1,128)S(1)} %get-tuple-element.113.state_ref, bf16[128,256]{1,0:T(8,128)(2,1)} %get-tuple-element.123.grad_ref), custom_call_target="tpu_custom_call" | custom-call | flops 262144 | bytes 262144 | tf_op jit(solution)/shard_map/adagrad/pallas_call | solution.py:257
  (21 shorter events, 0.2 us)
Async XLA Ops:
  0.6 13.0 %copy-start.3 = (f32[64,256]{1,0:T(8,128)S(1)}, f32[64,256]{1,0:T(8,128)}, u32[]{:S(2)}) copy-start(f32[64,256]{1,0:T(8,128)} %rel_ref.1) | copy-start | bytes 196612
  3.1 5.6 %collective-permute-start.1 = (bf16[128,256]{1,0:T(8,128)(2,1)S(1)}, bf16[128,256]{1,0:T(8,128)(2,1)}, u32[]{:S(2)}, u32[]{:S(2)}) collective-permute-start(bf16[128,256]{1,0:T(8,128)(2,1)S(1)} %param.1), channel_id=1, source_target_pairs={{0,8},{4,12},{8,0},{12,4},{16,24},{20,28},{24,16},{28,20},{1,9},{5... | collective-permute-start | bytes 196616 | tf_op jit(solution)/shard_map/cond/branch_1_fun/ppermute | solution.py:34
  8.7 7.4 %collective-permute-start.30 = (bf16[128,256]{1,0:T(8,128)(2,1)}, bf16[128,256]{1,0:T(8,128)(2,1)S(1)}, u32[]{:S(2)}, u32[]{:S(2)}) collective-permute-start(bf16[128,256]{1,0:T(8,128)(2,1)} %get-tuple-element.120.refs_0_), channel_id=1, source_target_pairs={{0,3},{1,2},{2,1},{3,0},{4,7},{5,6},{6,5},{7,4},{8,11},{9,10},{10,... | collective-permute-start | bytes 196616 | tf_op jit(solution)/shard_map/ppermute | solution.py:48
  13.1 5.7 %collective-permute-start.29 = (bf16[128,256]{1,0:T(8,128)(2,1)}, bf16[128,256]{1,0:T(8,128)(2,1)S(1)}, u32[]{:S(2)}, u32[]{:S(2)}) collective-permute-start(bf16[128,256]{1,0:T(8,128)(2,1)} %get-tuple-element.120.refs_0_), channel_id=1, source_target_pairs={{0,2},{1,3},{2,0},{3,1},{4,6},{5,7},{6,4},{7,5},{8,10},{9,11},{10,... | collective-permute-start | bytes 196616 | tf_op jit(solution)/shard_map/ppermute | solution.py:48
  13.1 5.9 %collective-permute-start.28 = (bf16[128,256]{1,0:T(8,128)(2,1)}, bf16[128,256]{1,0:T(8,128)(2,1)S(1)}, u32[]{:S(2)}, u32[]{:S(2)}) collective-permute-start(bf16[128,256]{1,0:T(8,128)(2,1)} %get-tuple-element.120.refs_0_), channel_id=1, source_target_pairs={{0,1},{1,0},{2,3},{3,2},{4,5},{5,4},{6,7},{7,6},{8,9},{9,8},{10,11... | collective-permute-start | bytes 196616 | tf_op jit(solution)/shard_map/ppermute | solution.py:48
  13.6 1.0 %copy-start = (f32[512,256]{1,0:T(8,128)S(1)}, f32[512,256]{1,0:T(8,128)}, u32[]{:S(2)}) copy-start(f32[512,256]{1,0:T(8,128)} %table_ref.2) | copy-start | bytes 1572868
  14.7 4.2 %copy-start.9 = (s32[1,560]{1,0:T(1,128)S(1)}, s32[1,560]{1,0:T(1,128)}, u32[]{:S(2)}) copy-start(s32[1,560]{1,0:T(1,128)} %get-tuple-element.92.plan) | copy-start | bytes 6724
  20.7 6.6 %collective-permute-start.31 = (bf16[128,256]{1,0:T(8,128)(2,1)S(1)}, bf16[128,256]{1,0:T(8,128)(2,1)S(1)}, u32[]{:S(2)}, u32[]{:S(2)}) collective-permute-start(bf16[128,256]{1,0:T(8,128)(2,1)S(1)} %get-tuple-element.104), channel_id=1, source_target_pairs={{0,1},{1,0},{2,3},{3,2},{4,5},{5,4},{6,7},{7,6},{8,9},{9,8},{10,11... | collective-permute-start | bytes 196616 | tf_op jit(solution)/shard_map/ppermute | solution.py:48
  22.2 8.7 %collective-permute-start.32 = (bf16[128,256]{1,0:T(8,128)(2,1)S(1)}, bf16[128,256]{1,0:T(8,128)(2,1)S(1)}, u32[]{:S(2)}, u32[]{:S(2)}) collective-permute-start(bf16[128,256]{1,0:T(8,128)(2,1)S(1)} %get-tuple-element.105), channel_id=1, source_target_pairs={{0,2},{1,3},{2,0},{3,1},{4,6},{5,7},{6,4},{7,5},{8,10},{9,11},{10,... | collective-permute-start | bytes 196616 | tf_op jit(solution)/shard_map/ppermute | solution.py:48
  24.0 6.8 %collective-permute-start.33 = (bf16[128,256]{1,0:T(8,128)(2,1)S(1)}, bf16[128,256]{1,0:T(8,128)(2,1)S(1)}, u32[]{:S(2)}, u32[]{:S(2)}) collective-permute-start(bf16[128,256]{1,0:T(8,128)(2,1)S(1)} %get-tuple-element.106), channel_id=1, source_target_pairs={{0,3},{1,2},{2,1},{3,0},{4,7},{5,6},{6,5},{7,4},{8,11},{9,10},{10,... | collective-permute-start | bytes 196616 | tf_op jit(solution)/shard_map/ppermute | solution.py:48
  25.8 9.6 %copy-start.2 = (f32[128,256]{1,0:T(8,128)S(1)}, f32[128,256]{1,0:T(8,128)}, u32[]{:S(2)}) copy-start(f32[128,256]{1,0:T(8,128)} %table_ref.3) | copy-start | bytes 393220
  25.8 9.5 %copy-start.8 = (f32[128]{0:T(128)S(1)}, f32[128]{0:T(128)}, u32[]{:S(2)}) copy-start(f32[128]{0:T(128)} %param.40) | copy-start | bytes 1540
  30.9 16.8 %copy-start.1 = (f32[512,256]{1,0:T(8,128)S(1)}, f32[512,256]{1,0:T(8,128)}, u32[]{:S(2)}) copy-start(f32[512,256]{1,0:T(8,128)} %table_ref.2) | copy-start | bytes 1572868
  30.9 4.4 %collective-permute-start.8 = (bf16[128,256]{1,0:T(8,128)(2,1)S(1)}, bf16[128,256]{1,0:T(8,128)(2,1)}, u32[]{:S(2)}, u32[]{:S(2)}) collective-permute-start(bf16[128,256]{1,0:T(8,128)(2,1)S(1)} %param.8), channel_id=1, source_target_pairs={{0,8},{4,12},{8,0},{12,4},{16,24},{20,28},{24,16},{28,20},{1,9},{5... | collective-permute-start | bytes 196616 | tf_op jit(solution)/shard_map/cond/branch_1_fun/ppermute | solution.py:34
  36.4 4.4 %collective-permute-start.17 = (bf16[128,256]{1,0:T(8,128)(2,1)S(1)}, bf16[128,256]{1,0:T(8,128)(2,1)}, u32[]{:S(2)}, u32[]{:S(2)}) collective-permute-start(bf16[128,256]{1,0:T(8,128)(2,1)S(1)} %param.17), channel_id=1, source_target_pairs={{0,16},{4,20},{8,24},{12,28},{16,0},{20,4},{24,8},{28,12},{1,17},{... | collective-permute-start | bytes 196616 | tf_op jit(solution)/shard_map/cond/branch_3_fun/ppermute | solution.py:34
  40.8 4.4 %copy-start.5 = (s32[1,1,2,64]{3,2,1,0:T(2,128)S(1)}, s32[1,1,2,64]{3,2,1,0:T(2,128)}, u32[]{:S(2)}) copy-start(s32[1,1,2,64]{3,2,1,0:T(2,128)} %param.44) | copy-start | bytes 1540
  40.8 4.4 %copy-start.4 = (s32[1,1,2,64]{3,2,1,0:T(2,128)S(1)}, s32[1,1,2,64]{3,2,1,0:T(2,128)}, u32[]{:S(2)}) copy-start(s32[1,1,2,64]{3,2,1,0:T(2,128)} %param.43) | copy-start | bytes 1540
  40.8 4.4 %copy-start.7 = (s32[1,1,2]{2,1,0:T(1,128)S(1)}, s32[1,1,2]{2,1,0:T(1,128)}, u32[]{:S(2)}) copy-start(s32[1,1,2]{2,1,0:T(1,128)} %param.45) | copy-start | bytes 28
  40.8 7.5 %collective-permute-start.36 = (bf16[128,256]{1,0:T(8,128)(2,1)}, bf16[128,256]{1,0:T(8,128)(2,1)S(1)}, u32[]{:S(2)}, u32[]{:S(2)}) collective-permute-start(bf16[128,256]{1,0:T(8,128)(2,1)} %get-tuple-element.122.refs_0_), channel_id=1, source_target_pairs={{0,3},{1,2},{2,1},{3,0},{4,7},{5,6},{6,5},{7,4},{8,11},{9,10},{10,... | collective-permute-start | bytes 196616 | tf_op jit(solution)/shard_map/ppermute | solution.py:48
  42.1 6.8 %collective-permute-start.35 = (bf16[128,256]{1,0:T(8,128)(2,1)}, bf16[128,256]{1,0:T(8,128)(2,1)S(1)}, u32[]{:S(2)}, u32[]{:S(2)}) collective-permute-start(bf16[128,256]{1,0:T(8,128)(2,1)} %get-tuple-element.122.refs_0_), channel_id=1, source_target_pairs={{0,2},{1,3},{2,0},{3,1},{4,6},{5,7},{6,4},{7,5},{8,10},{9,11},{10,... | collective-permute-start | bytes 196616 | tf_op jit(solution)/shard_map/ppermute | solution.py:48
  44.2 5.2 %collective-permute-start.34 = (bf16[128,256]{1,0:T(8,128)(2,1)}, bf16[128,256]{1,0:T(8,128)(2,1)S(1)}, u32[]{:S(2)}, u32[]{:S(2)}) collective-permute-start(bf16[128,256]{1,0:T(8,128)(2,1)} %get-tuple-element.122.refs_0_), channel_id=1, source_target_pairs={{0,1},{1,0},{2,3},{3,2},{4,5},{5,4},{6,7},{7,6},{8,9},{9,8},{10,11... | collective-permute-start | bytes 196616 | tf_op jit(solution)/shard_map/ppermute | solution.py:48
  45.2 2.5 %copy-start.6 = (f32[512]{0:T(512)S(1)}, f32[512]{0:T(512)}, u32[]{:S(2)}) copy-start(f32[512]{0:T(512)} %param.38) | copy-start | bytes 6148
  53.7 8.5 %collective-permute-start.37 = (bf16[128,256]{1,0:T(8,128)(2,1)S(1)}, bf16[128,256]{1,0:T(8,128)(2,1)S(1)}, u32[]{:S(2)}, u32[]{:S(2)}) collective-permute-start(bf16[128,256]{1,0:T(8,128)(2,1)S(1)} %get-tuple-element.115), channel_id=1, source_target_pairs={{0,1},{1,0},{2,3},{3,2},{4,5},{5,4},{6,7},{7,6},{8,9},{9,8},{10,11... | collective-permute-start | bytes 196616 | tf_op jit(solution)/shard_map/ppermute | solution.py:48
  53.8 8.5 %collective-permute-start.38 = (bf16[128,256]{1,0:T(8,128)(2,1)S(1)}, bf16[128,256]{1,0:T(8,128)(2,1)S(1)}, u32[]{:S(2)}, u32[]{:S(2)}) collective-permute-start(bf16[128,256]{1,0:T(8,128)(2,1)S(1)} %get-tuple-element.116), channel_id=1, source_target_pairs={{0,2},{1,3},{2,0},{3,1},{4,6},{5,7},{6,4},{7,5},{8,10},{9,11},{10,... | collective-permute-start | bytes 196616 | tf_op jit(solution)/shard_map/ppermute | solution.py:48
  55.7 6.6 %collective-permute-start.39 = (bf16[128,256]{1,0:T(8,128)(2,1)S(1)}, bf16[128,256]{1,0:T(8,128)(2,1)S(1)}, u32[]{:S(2)}, u32[]{:S(2)}) collective-permute-start(bf16[128,256]{1,0:T(8,128)(2,1)S(1)} %get-tuple-element.117), channel_id=1, source_target_pairs={{0,3},{1,2},{2,1},{3,0},{4,7},{5,6},{6,5},{7,4},{8,11},{9,10},{10,... | collective-permute-start | bytes 196616 | tf_op jit(solution)/shard_map/ppermute | solution.py:48
  62.4 4.4 %collective-permute-start.24 = (bf16[128,256]{1,0:T(8,128)(2,1)S(1)}, bf16[128,256]{1,0:T(8,128)(2,1)}, u32[]{:S(2)}, u32[]{:S(2)}) collective-permute-start(bf16[128,256]{1,0:T(8,128)(2,1)S(1)} %param.24), channel_id=1, source_target_pairs={{0,16},{4,20},{8,24},{12,28},{16,0},{20,4},{24,8},{28,12},{1,17},{... | collective-permute-start | bytes 196616 | tf_op jit(solution)/shard_map/cond/branch_3_fun/ppermute | solution.py:34

commit v2 on v1

v2 whole, which is shorter than its diff:
```python
import functools

import jax
import jax.numpy as jnp
from jax import lax
from jax.experimental import pallas as pl
from jax.experimental.pallas import tpu as pltpu
from jax.sharding import PartitionSpec as P

TILE = 128
GROUP = 4
LOW_BITS = 3
SHIFT = 16

learn_rate = 0.1

AXES = ("bucket", "rep")
SMEM = pl.BlockSpec(memory_space=pltpu.SMEM)
VMEM = pl.BlockSpec(memory_space=pltpu.VMEM)
FIRST_GRANT = 60 * 1024 * 1024
GRANT = pltpu.CompilerParams(vmem_limit_bytes=12 * 1024 * 1024)


def send(rows, bucket_xor, rep_xor):
    if bucket_xor == 0 and rep_xor == 0:
        return rows
    buckets, reps = lax.axis_size("bucket"), lax.axis_size("rep")
    pairs = [
        (b * reps + r, (b ^ bucket_xor) * reps + (r ^ rep_xor))
        for b in range(buckets)
        for r in range(reps)
    ]
    return lax.ppermute(rows, AXES, pairs)


def bit_chunks():
    bits = lax.axis_size("bucket").bit_length() - 1
    return [(at, min(LOW_BITS, bits - at)) for at in range(0, bits, LOW_BITS)]


def by_mask(mask, chunk, branch, operands):
    first, width = chunk
    if (1 << width) == lax.axis_size("bucket"):
        least, index = 1, mask - 1
    else:
        least, index = 0, jnp.bitwise_and(jnp.right_shift(mask, first), (1 << width) - 1)
    branches = [functools.partial(branch, value << first) for value in range(least, 1 << width)]
    return lax.switch(index, branches, operands)


def send_high(rows, mask):
    for chunk in bit_chunks()[1:]:
        rows = by_mask(mask, chunk, lambda value, x: send(x, value, 0), rows)
    return rows


def layout(number, slots):
    most = slots // GROUP + number + 3
    first = 2
    second = first + most
    start = second + most
    room = 1 << (slots + 2 * GROUP - 1).bit_length()
    return first, second, start, room, start + number * room


def sort_tiles(k, cut, none_rel, flip, number, tiles, rel, counts, plan):
    bits = number.bit_length() - 1
    first, second, start, room, _ = layout(number, tiles.shape[1])

    def place(t, ends):
        code = tiles[k, t]
        e = jnp.bitwise_xor(jnp.bitwise_and(code, number - 1), flip)
        p = ends[0]
        for i in range(1, number):
            p = jnp.where(e == i, ends[i], p)
        plan[0, start + e * room + p] = jnp.bitwise_or(
            jnp.left_shift(jnp.right_shift(code, bits), SHIFT), rel[k, t]
        )
        return tuple(ends[i] + jnp.where(e == i, 1, 0) for i in range(number))

    ends = lax.fori_loop(0, counts[k], place, (jnp.int32(0),) * number)
    for i in range(number):
        for extra in range(2 * GROUP):
            plan[0, start + i * room + ends[i] + extra] = jnp.int32(none_rel)
    for index, at, blocks in ((0, first, range(cut)), (1, second, range(cut, number))):
        q = jnp.int32(0)
        for i in blocks:
            amount = jnp.right_shift(ends[i] + (GROUP - 1), GROUP.bit_length() - 1)

            def name(g, carry, i=i, q=q, at=at):
                plan[0, at + q + g] = i * room + g * GROUP
                return carry

            lax.fori_loop(0, amount, name, 0)
            q = q + amount
        plan[0, index] = jnp.right_shift(q + 1, 1)
        for extra in range(3):
            plan[0, at + q + extra] = blocks[0] * room + ends[blocks[0]]


def first_kernel(rounds, number, cut, none_rel, rep, tiles, rel, counts, partners, dst_ref, rel_ref, plan, rows_ref, row_ref, *masks):
    rows_ref[...] = dst_ref[...].astype(jnp.bfloat16)
    row_ref[pl.ds(0, none_rel), :] = rel_ref[...] * (0.5 * rel_ref.shape[1] ** -0.5)
    row_ref[pl.ds(none_rel, 8), :] = jnp.zeros((8, rel_ref.shape[1]), jnp.float32)
    for k in range(rounds):
        masks[k][0, 0] = partners[k, 0]
    flip = rep[0] * (dst_ref.shape[0] // TILE)
    sort_tiles(0, cut, none_rel, flip, number, tiles, rel, counts, plan)


def later_kernel(k, shard_blocks, number, cut, none_rel, rep, tiles, rel, counts, after, plan):
    sort_tiles(k, cut, none_rel, rep[0] * shard_blocks, number, tiles, rel, counts, plan)


def tile_kernel(index, lists, cut, shards, carried, plan, src_ref, row_ref, *refs):
    dst_refs, refs = refs[:shards], refs[shards + carried :]
    src_grad, parts, refs = refs[0], refs[1 : 1 + shards], refs[1 + shards :]
    low_ref, dst_all, dst_grad, held_rows, held_slope = refs
    _, _, start, room, _ = lists
    at_list = lists[index]
    rows_of_shard = dst_refs[0].shape[0]
    first_row = cut * TILE if index == 1 else 0

    def begin(i, carry):
        rows = pl.ds(pl.multiple_of(i * TILE, TILE), TILE)
        low_ref[rows, :] = src_ref[rows, :].astype(jnp.bfloat16).astype(jnp.float32)
        if not carried:
            src_grad[rows, :] = jnp.zeros((TILE, src_grad.shape[1]), jnp.float32)
        return carry

    lax.fori_loop(0, src_ref.shape[0] // TILE, begin, 0)
    for i in range(shards):
        dst_all[pl.ds(i * rows_of_shard, rows_of_shard), :] = dst_refs[i][...]
    dst_grad[...] = jnp.zeros_like(dst_grad)
    row_id = lax.broadcasted_iota(jnp.int32, (TILE, TILE), 0)
    column_id = lax.broadcasted_iota(jnp.int32, (TILE, TILE), 1)
    offset = jnp.where(row_id == column_id, -1.0, 1.0).astype(jnp.float32)
    pairs = plan[0, index]

    def group(q):
        at = plan[0, at_list + q]
        block = jnp.right_shift(at, room.bit_length() - 1)
        where, rows = [], []
        for g in range(GROUP):
            code = plan[0, start + at + g]
            where.append(pl.multiple_of(jnp.right_shift(code, SHIFT) * TILE, TILE))
            rows.append(row_ref[pl.ds(jnp.bitwise_and(code, (1 << SHIFT) - 1), 1), :])
        return pl.ds(pl.multiple_of(block * TILE - first_row, TILE), TILE), where, rows

    def slopes(q, slot):
        dst_rows, where, rows = group(q)
        src_rel = jnp.concatenate(
            [(low_ref[pl.ds(s, TILE), :] * row).astype(jnp.bfloat16) for s, row in zip(where, rows)], 0
        )
        scores = lax.dot_general(
            src_rel, dst_all[dst_rows, :], (((1,), (1,)), ((), ())), preferred_element_type=jnp.float32
        )
        slope = jnp.concatenate(
            [
                (jnp.tanh(scores[g * TILE : (g + 1) * TILE]) + offset).astype(jnp.bfloat16)
                for g in range(GROUP)
            ],
            0,
        )
        held_rows[slot] = src_rel
        held_slope[slot] = slope

    def grads(q, slot):
        dst_rows, where, rows = group(q)
        slope = held_slope[slot]
        src_terms = jnp.dot(slope, dst_all[dst_rows, :], preferred_element_type=jnp.float32)
        dst_grad[dst_rows, :] += lax.dot_general(
            slope, held_rows[slot], (((0,), (0,)), ((), ())), preferred_element_type=jnp.float32
        )
        for g in range(GROUP):
            src_grad[pl.ds(where[g], TILE), :] += src_terms[g * TILE : (g + 1) * TILE] * rows[g]

    @pl.when(pairs > 0)
    def _():
        slopes(0, 0)

        def two(p, carry):
            q = p * 2
            slopes(q + 1, 1)
            grads(q, 0)
            slopes(q + 2, 0)
            grads(q + 1, 1)
            return carry

        lax.fori_loop(0, pairs, two, 0)

    for i in range(shards):
        parts[i][...] = dst_grad[pl.ds(i * rows_of_shard, rows_of_shard), :].astype(jnp.bfloat16)


def tile_work(index, lists, cut, slots, plan, src_table, rel_rows, shards, src_grad):
    rows, width = shards[0].shape
    carried = [] if src_grad is None else [src_grad]
    out = pl.pallas_call(
        functools.partial(tile_kernel, index, lists, cut, len(shards), len(carried)),
        in_specs=[SMEM] + [VMEM] * (2 + len(shards) + len(carried)),
        out_specs=[VMEM] * (1 + len(shards)),
        out_shape=[jax.ShapeDtypeStruct(src_table.shape, jnp.float32)]
        + [jax.ShapeDtypeStruct((rows, width), jnp.bfloat16)] * len(shards),
        scratch_shapes=[
            pltpu.VMEM(src_table.shape, jnp.float32),
            pltpu.VMEM((len(shards) * rows, width), jnp.bfloat16),
            pltpu.VMEM((len(shards) * rows, width), jnp.float32),
            pltpu.VMEM((2, GROUP * TILE, width), jnp.bfloat16),
            pltpu.VMEM((2, GROUP * TILE, TILE), jnp.bfloat16),
        ],
        input_output_aliases={3 + len(shards): 0} if carried else {},
        cost_estimate=pl.CostEstimate(
            flops=6 * slots * TILE * TILE * width,
            bytes_accessed=4 * src_table.size,
            transcendentals=slots * TILE * TILE,
        ),
        compiler_params=GRANT,
        name="tile_work",
    )(plan, src_table, rel_rows, *shards, *carried)
    return out[0], list(out[1:])


def adagrad_block(table, state, grad):
    row_id = lax.broadcasted_iota(jnp.int32, (TILE, TILE), 0)
    column_id = lax.broadcasted_iota(jnp.int32, (TILE, TILE), 1)
    same = row_id == column_id
    state = jnp.sum(jnp.where(same, state, 0.0), axis=1, keepdims=True)
    state = state + jnp.sum(grad * grad, axis=1, keepdims=True) * (1.0 / grad.shape[1])
    table = table - learn_rate * grad / jnp.sqrt(state)
    return table, jnp.sum(jnp.where(same, state, 0.0), axis=0, keepdims=True)


def source_kernel(table_ref, state_ref, grad_ref, table_out, state_out, table_new, state_new, sem):
    blocks = table_ref.shape[0] // TILE

    def block(i, carry):
        rows = pl.ds(pl.multiple_of(i * TILE, TILE), TILE)
        table_new[rows, :], state_new[pl.ds(i, 1), :] = adagrad_block(
            table_ref[rows, :], state_ref[pl.ds(i, 1), :], grad_ref[rows, :]
        )
        return carry

    lax.fori_loop(0, blocks, block, 0)
    copies = [
        pltpu.make_async_copy(table_new, table_out, sem.at[0]),
        pltpu.make_async_copy(state_new, state_out, sem.at[1]),
    ]
    for copy in copies:
        copy.start()
    for copy in copies:
        copy.wait()


def update_source(table, state, grad):
    return pl.pallas_call(
        source_kernel,
        in_specs=[VMEM] * 3,
        out_specs=[pl.BlockSpec(memory_space=pltpu.HBM)] * 2,
        out_shape=[pltpu.HBM(table.shape, jnp.float32), pltpu.HBM(state.shape, jnp.float32)],
        scratch_shapes=[
            pltpu.VMEM(table.shape, jnp.float32),
            pltpu.VMEM(state.shape, jnp.float32),
            pltpu.SemaphoreType.DMA((2,)),
        ],
        cost_estimate=pl.CostEstimate(
            flops=8 * table.size, bytes_accessed=8 * table.size, transcendentals=table.shape[0]
        ),
        compiler_params=GRANT,
        name="update_source",
    )(table, state, grad)


def target_kernel(parts, last, table_ref, state_ref, *refs):
    for i in range(table_ref.shape[0] // TILE):
        rows = pl.ds(i * TILE, TILE)
        grad = refs[0][rows, :].astype(jnp.float32)
        for other in refs[1:parts]:
            grad = grad + other[rows, :].astype(jnp.float32)
        if parts > 1:
            grad = grad.astype(jnp.bfloat16).astype(jnp.float32)
        table, state = adagrad_block(table_ref[rows, :], state_ref[pl.ds(i, 1), :], grad)
        refs[parts][rows, :] = table
        refs[parts + 1][pl.ds(i, 1), :] = state
        if not last:
            refs[parts + 2][rows, :] = table.astype(jnp.bfloat16)


def update_target(table, state, parts, last):
    low = [] if last else [jax.ShapeDtypeStruct(table.shape, jnp.bfloat16)]
    return pl.pallas_call(
        functools.partial(target_kernel, len(parts), last),
        in_specs=[VMEM] * (2 + len(parts)),
        out_specs=[VMEM] * (2 + len(low)),
        out_shape=[
            jax.ShapeDtypeStruct(table.shape, jnp.float32),
            jax.ShapeDtypeStruct(state.shape, jnp.float32),
        ]
        + low,
        cost_estimate=pl.CostEstimate(
            flops=8 * table.size, bytes_accessed=8 * table.size, transcendentals=table.shape[0]
        ),
        compiler_params=GRANT,
        name="update_target",
    )(table, state, *parts)


def per_device(
    src_table, src_state, dst_table, dst_state, rel_table, partners, tiles, tile_rel, counts
):
    reps = lax.axis_size("rep")
    rounds = partners.shape[0]
    src_state = src_state.reshape(-1, TILE)
    dst_state = dst_state.reshape(-1, TILE)
    shard_blocks = dst_table.shape[0] // TILE
    number = reps * shard_blocks
    slots = tiles.shape[-1]
    lists = layout(number, slots)
    none_rel = rel_table.shape[0]
    near = reps // 2
    cut = near * shard_blocks
    low_chunk, *high_chunks = bit_chunks()
    scalars = (
        lax.axis_index("rep").astype(jnp.int32).reshape(1), tiles[0, 0], tile_rel[0, 0], counts[0, 0],
    )
    plan_shape = jax.ShapeDtypeStruct((1, lists[-1]), jnp.int32)
    plan, rows, rel_rows, *masks = pl.pallas_call(
        functools.partial(first_kernel, rounds, number, cut, none_rel),
        in_specs=[SMEM] * 5 + [VMEM] * 2,
        out_specs=[SMEM, VMEM, VMEM] + [SMEM] * rounds,
        out_shape=[
            plan_shape,
            jax.ShapeDtypeStruct(dst_table.shape, jnp.bfloat16),
            jax.ShapeDtypeStruct((none_rel + 8, rel_table.shape[1]), jnp.float32),
        ]
        + [jax.ShapeDtypeStruct((1, 1), jnp.int32)] * rounds,
        compiler_params=pltpu.CompilerParams(vmem_limit_bytes=FIRST_GRANT),
        name="first",
    )(*scalars, partners, dst_table, rel_table)

    def branch(value, operands, k):
        rows, plan, rel_rows, src_table, src_state, scalars = operands
        shards = []
        for j in range(reps):
            shards.append(send(rows, value, j))
        src_grad, parts = tile_work(
            0, lists, cut, slots // 2, plan, src_table, rel_rows, shards[:near], None
        )
        back = []
        for j in range(near):
            back.append(send(parts[j], value, j))
        src_grad, parts = tile_work(1, lists, cut, slots // 2, plan, src_table, rel_rows, shards[near:], src_grad)
        for j in range(near, reps):
            back.append(send(parts[j - near], value, j))
        if k + 1 < rounds:
            plan = pl.pallas_call(
                functools.partial(later_kernel, k + 1, shard_blocks, number, cut, none_rel),
                in_specs=[SMEM] * 4 + [pl.BlockSpec(memory_space=pl.ANY)],
                out_specs=SMEM,
                out_shape=plan_shape,
                compiler_params=GRANT,
                name="later",
            )(*scalars, src_grad)
        src_table, src_state = update_source(src_table, src_state, src_grad)
        return tuple(back), (plan,) if k + 1 < rounds else (), src_table, src_state

    for k in range(rounds):
        mask = masks[k].reshape(())
        back, plans, src_table, src_state = by_mask(
            mask,
            low_chunk,
            functools.partial(branch, k=k),
            (send_high(rows, mask), plan, rel_rows, src_table, src_state, scalars),
        )
        (plan,) = plans or (None,)
        if high_chunks:
            total = functools.reduce(jnp.add, [x.astype(jnp.float32) for x in back])
            back = [send_high(total.astype(jnp.bfloat16), mask)]
        dst_table, dst_state, *rows = update_target(dst_table, dst_state, back, k + 1 == rounds)
        rows = rows[0] if rows else None
    return (src_table, src_state.reshape(-1), dst_table, dst_state.reshape(-1))


def solution(mesh):
    table, state = P(AXES, None), P(AXES)
    in_specs = (
        table,
        state,
        table,
        state,
        P(),
        P(),
        P("bucket", "rep", None, None),
        P("bucket", "rep", None, None),
        P("bucket", "rep", None),
    )
    return jax.shard_map(
        per_device,
        mesh=mesh,
        in_specs=in_specs,
        out_specs=(table, state, table, state),
        check_vma=False,
    )
```

time: 68.8 us -> 61 us (0.89)
  waiting for transfers between devices: 22.6 us -> 6.82 us
  starting transfers between devices: 23.5 us -> 27.9 us
  Pallas kernels: 19 us -> 21.1 us
  local copies, waits for them, and re-layouts: 1.08 us -> 2.69 us
    ppermute x16, waiting for transfers between devices: 22.6 us -> 6.82 us  [send(): return lax.ppermute(rows, AXES, pairs)]
    ppermute x16, starting transfers between devices: 23.5 us -> 27.9 us  [send(): return lax.ppermute(rows, AXES, pairs)]
    pallas_call x11 -> x10, Pallas kernels: 19 us -> 21.1 us  [the longest x4 11.4 us: tile_work(): pl.pallas_call(functools.partial(tile_kernel, index, lists, cut, len(shar...]
    unnamed x20 -> x14, local copies, waits for them, and re-layouts: 1.08 us -> 2.68 us
  transfers between devices with their start and end apart: 16 -> 16, of which waited for: 10 -> 5; matrix products, arithmetic and copies ran while one was open for 0% -> 0% of each run, Pallas kernels for 13% -> 27%
where the time goes in v2:
time: 61 us; the launch traced here: 60.6 us
  starting transfers between devices  27.9 us (46%)
  Pallas kernels  21.1 us (35%)
  waiting for transfers between devices  6.82 us (11%)
  local copies, waits for them, and re-layouts  2.69 us (4%)
  between operations  2 us (3%)
    ppermute x16, starting transfers between devices, send(): return lax.ppermute(rows, AXES, pairs)  27.9 us
    pallas_call x4, Pallas kernels, tile_work(): pl.pallas_call(functools.partial(tile_kernel, index, lists, cut, len(shar...  11.4 us
    ppermute x16, waiting for transfers between devices, send(): return lax.ppermute(rows, AXES, pairs)  6.82 us
    pallas_call x2, Pallas kernels, update_target(): pl.pallas_call(functools.partial(target_kernel, len(parts), last), in_spe...  2.83 us
    unnamed x14, local copies, waits for them, and re-layouts  2.68 us
    pallas_call x2, Pallas kernels, update_source(): pl.pallas_call(source_kernel, in_specs=[VMEM] * 3, out_specs=[pl.BlockSpe...  2.68 us
    pallas_call x1, Pallas kernels, branch(): pl.pallas_call(functools.partial(later_kernel, k + 1, shard_blocks, numbe...  2.44 us
    pallas_call x1, Pallas kernels, per_device(): pl.pallas_call(functools.partial(first_kernel, rounds, number, cut, none_...  1.76 us
  transfers between devices with their start and end apart: 16, of which 5 were waited for; matrix products, arithmetic and copies ran while one was open for 0% of the time, Pallas kernels for 27%

profile of v2, /device:TPU:0, one launch (start us, length us, event | category | flops | bytes accessed | tf_op | source)
XLA Modules:
  0.0 60.6 jit_solution(12078307298256933288)
XLA Ops:
  0.7 0.7 %copy-done.19 = s32[1,1,2,64]{3,2,1,0:T(2,128)S(1)} copy-done((s32[1,1,2,64]{3,2,1,0:T(2,128)S(1)}, s32[1,1,2,64]{3,2,1,0:T(2,128)}, u32[]{:S(2)}) %copy-start.19) | copy-done | bytes 536
  1.3 0.0 copy-done.18
  1.3 1.8 %first.1 = (s32[1,560]{1,0:T(1,128)S(1)}, bf16[128,256]{1,0:T(8,128)(2,1)S(1)}, f32[72,256]{1,0:T(8,128)S(1)}, s32[1,1]{1,0:T(1,128)}, s32[1,1]{1,0:T(1,128)}) custom-call(s32[1]{0:T(128)} %bitcast.rep, s32[2,64]{1,0:T(2,128)S(1)} %bitcast.18, s32[2,64]{1,0:T(2,128)S(1)} %bitcast.26, s32[2]{0:T(128)S(1)} %bitcast.34, s32[2,8]{1,0:T(2,128)} %partners.1, ...), custom_call_target="tpu_custom_call" | custom-call | tf_op jit(solution)/shard_map/first/pallas_call | solution.py:327
  4.4 0.0 copy-start.16
  4.4 0.7 %copy-done.16 = f32[512]{0:T(512)S(1)} copy-done((f32[512]{0:T(512)S(1)}, f32[512]{0:T(512)}, u32[]{:S(2)}) %copy-start.16) | copy-done | bytes 2072
  5.1 25.1 %conditional.2 = (bf16[128,256]{1,0:T(8,128)(2,1)}, bf16[128,256]{1,0:T(8,128)(2,1)}, bf16[128,256]{1,0:T(8,128)(2,1)}, bf16[128,256]{1,0:T(8,128)(2,1)}, s32[1,...) conditional(s32[]{:T(128)} %bitcast.6, ...), branch_computations={%region_0.0_spmd, %region_1.0_spmd, %region_2.0_spmd, %region_3.0_... | conditional | flops 1611661312 | bytes 6291860 | solution.py:48
  5.1 3.9 %collective-permute-start.9 = (bf16[128,256]{1,0:T(8,128)(2,1)S(1)}, bf16[128,256]{1,0:T(8,128)(2,1)S(1)}, u32[]{:S(2)}, u32[]{:S(2)}) collective-permute-start(bf16[128,256]{1,0:T(8,128)(2,1)S(1)} %get-tuple-element.216), channel_id=1, source_target_pairs={{0,9},{1,8},{2,11},{3,10},{4,13},{5,12},{6,15},{7,14},{8,1},{9,0},... | collective-permute-start | bytes 196616 | tf_op jit(solution)/shard_map/cond/branch_1_fun/ppermute | solution.py:33
  9.0 0.7 %collective-permute-start.8 = (bf16[128,256]{1,0:T(8,128)(2,1)S(1)}, bf16[128,256]{1,0:T(8,128)(2,1)S(1)}, u32[]{:S(2)}, u32[]{:S(2)}) collective-permute-start(bf16[128,256]{1,0:T(8,128)(2,1)S(1)} %get-tuple-element.216), channel_id=1, source_target_pairs={{0,8},{1,9},{2,10},{3,11},{4,12},{5,13},{6,14},{7,15},{8,0},{9,1},... | collective-permute-start | bytes 196616 | tf_op jit(solution)/shard_map/cond/branch_1_fun/ppermute | solution.py:33
  9.7 3.6 %collective-permute-start.13 = (bf16[128,256]{1,0:T(8,128)(2,1)S(1)}, bf16[128,256]{1,0:T(8,128)(2,1)S(1)}, u32[]{:S(2)}, u32[]{:S(2)}) collective-permute-start(bf16[128,256]{1,0:T(8,128)(2,1)S(1)} %get-tuple-element.216), channel_id=1, source_target_pairs={{0,11},{1,10},{2,9},{3,8},{4,15},{5,14},{6,13},{7,12},{8,3},{9,2},... | collective-permute-start | bytes 196616 | tf_op jit(solution)/shard_map/cond/branch_1_fun/ppermute | solution.py:33
  13.3 0.0 collective-permute-start.12
  13.3 0.0 collective-permute-done.9.refs_1_
  13.3 0.0 collective-permute-done.8.refs_0_
  13.3 2.6 %tile_work.30 = (f32[512,256]{1,0:T(8,128)S(1)}, bf16[128,256]{1,0:T(8,128)(2,1)S(1)}, bf16[128,256]{1,0:T(8,128)(2,1)S(1)}) custom-call(s32[1,560]{1,0:T(1,128)S(1)} %get-tuple-element.213.plan, f32[512,256]{1,0:T(8,128)} %get-tuple-element.214.src_ref.table_ref, f32[72,256]{1,0:T(8,128)S(1)} %get-tuple-element.215.row_ref, ...), custom_call_target="tpu_custom_call" | custom-call | flops 805306368 | bytes 524288 | tf_op jit(solution)/shard_map/cond/branch_1_fun/tile_work/pallas_call | solution.py:199
  15.9 1.2 %collective-permute-start.10 = (bf16[128,256]{1,0:T(8,128)(2,1)S(1)}, bf16[128,256]{1,0:T(8,128)(2,1)}, u32[]{:S(2)}, u32[]{:S(2)}) collective-permute-start(bf16[128,256]{1,0:T(8,128)(2,1)S(1)} %get-tuple-element.217), channel_id=1, source_target_pairs={{0,8},{1,9},{2,10},{3,11},{4,12},{5,13},{6,14},{7,15},{8,0},{9,1},... | collective-permute-start | bytes 196616 | tf_op jit(solution)/shard_map/cond/branch_1_fun/ppermute | solution.py:33
  17.1 2.3 %collective-permute-start.11 = (bf16[128,256]{1,0:T(8,128)(2,1)S(1)}, bf16[128,256]{1,0:T(8,128)(2,1)}, u32[]{:S(2)}, u32[]{:S(2)}) collective-permute-start(bf16[128,256]{1,0:T(8,128)(2,1)S(1)} %get-tuple-element.218), channel_id=1, source_target_pairs={{0,9},{1,8},{2,11},{3,10},{4,13},{5,12},{6,15},{7,14},{8,1},{9,0},... | collective-permute-start | bytes 196616 | tf_op jit(solution)/shard_map/cond/branch_1_fun/ppermute | solution.py:33
  19.4 0.0 collective-permute-done.13.refs_1_
  19.4 0.6 collective-permute-done.12.refs_0_
  20.0 1.5 %tile_work.31 = (f32[512,256]{1,0:T(8,128)S(1)}, bf16[128,256]{1,0:T(8,128)(2,1)S(1)}, bf16[128,256]{1,0:T(8,128)(2,1)S(1)}) custom-call(s32[1,560]{1,0:T(1,128)S(1)} %get-tuple-element.213.plan, f32[512,256]{1,0:T(8,128)S(1)} %copy-done.3, f32[72,256]{1,0:T(8,128)S(1)} %get-tuple-element.215.row_ref, ...), custom_call_target="tpu_custom_call", output_to_operand_aliasing={{0}: (5, {})} | custom-call | flops 805306368 | bytes 524288 | tf_op jit(solution)/shard_map/cond/branch_1_fun/tile_work/pallas_call | solution.py:199
  21.4 1.7 %collective-permute-start.14 = (bf16[128,256]{1,0:T(8,128)(2,1)S(1)}, bf16[128,256]{1,0:T(8,128)(2,1)}, u32[]{:S(2)}, u32[]{:S(2)}) collective-permute-start(bf16[128,256]{1,0:T(8,128)(2,1)S(1)} %get-tuple-element.220), channel_id=1, source_target_pairs={{0,10},{1,11},{2,8},{3,9},{4,14},{5,15},{6,12},{7,13},{8,2},{9,3},... | collective-permute-start | bytes 196616 | tf_op jit(solution)/shard_map/cond/branch_1_fun/ppermute | solution.py:33
  23.2 1.6 %collective-permute-start.15 = (bf16[128,256]{1,0:T(8,128)(2,1)S(1)}, bf16[128,256]{1,0:T(8,128)(2,1)}, u32[]{:S(2)}, u32[]{:S(2)}) collective-permute-start(bf16[128,256]{1,0:T(8,128)(2,1)S(1)} %get-tuple-element.221), channel_id=1, source_target_pairs={{0,11},{1,10},{2,9},{3,8},{4,15},{5,14},{6,13},{7,12},{8,3},{9,2},... | collective-permute-start | bytes 196616 | tf_op jit(solution)/shard_map/cond/branch_1_fun/ppermute | solution.py:33
  24.7 2.4 %later.8 = s32[1,560]{1,0:T(1,128)S(1)} custom-call(s32[1]{0:T(128)} %get-tuple-element.222.rep, s32[2,64]{1,0:T(2,128)S(1)} %get-tuple-element.223.tiles, s32[2,64]{1,0:T(2,128)S(1)} %get-tuple-element.224.rel, s32[2]{0:T(128)S(1)} %get-tuple-element.225.counts, f32[512,256]{1,0:T(8,128)S(1)} %get-tuple-element.226.after.grad_ref), custom_call_target="tpu_custom_call" | custom-call | tf_op jit(solution)/shard_map/cond/branch_1_fun/later/pallas_call | solution.py:356
  27.2 1.3 %update_source.15 = (f32[512,256]{1,0:T(8,128)}, f32[4,128]{1,0:T(4,128)}) custom-call(f32[512,256]{1,0:T(8,128)S(1)} %copy-done.3, f32[4,128]{1,0:T(4,128)S(1)} %get-tuple-element.227.state_ref, f32[512,256]{1,0:T(8,128)S(1)} %get-tuple-element.226.after.grad_ref), custom_call_target="tpu_custom_call" | custom-call | flops 1048576 | bytes 1048576 | tf_op jit(solution)/shard_map/cond/branch_1_fun/update_source/pallas_call | solution.py:256
  28.5 0.0 collective-permute-done.10
  28.5 0.0 collective-permute-done.11
  28.6 0.0 collective-permute-done.14
  28.6 1.7 %collective-permute-done.15 = bf16[128,256]{1,0:T(8,128)(2,1)} collective-permute-done((bf16[128,256]{1,0:T(8,128)(2,1)S(1)}, bf16[128,256]{1,0:T(8,128)(2,1)}, u32[]{:S(2)}, u32[]{:S(2)}) %collective-permute-start.15) | collective-permute-done | bytes 65568 | tf_op jit(solution)/shard_map/cond/branch_1_fun/ppermute | solution.py:33
  30.2 0.7 %copy-done.1 = f32[128]{0:T(128)S(1)} copy-done((f32[128]{0:T(128)S(1)}, f32[128]{0:T(128)}, u32[]{:S(2)}) %copy-start.1) | copy-done | bytes 536
  30.9 1.1 %update_target.2 = (f32[128,256]{1,0:T(8,128)S(1)}, f32[1,128]{1,0:T(1,128)S(1)}, bf16[128,256]{1,0:T(8,128)(2,1)S(1)}) custom-call(f32[128,256]{1,0:T(8,128)S(1)} %copy-done, f32[1,128]{1,0:T(1,128)S(1)} %bitcast.10, bf16[128,256]{1,0:T(8,128)(2,1)} %get-tuple-element.438.refs_0_, bf16[128,256]{1,0:T(8,128)(2,1)} %get-tuple-element.439.refs_1_, ...), custom_call_target="tpu_custom_call" | custom-call | flops 262144 | bytes 262144 | tf_op jit(solution)/shard_map/update_target/pallas_call | solution.py:291
  32.0 0.0 copy-start.17
  32.0 0.7 %copy-done.17 = f32[4,128]{1,0:T(4,128)S(1)} copy-done((f32[4,128]{1,0:T(4,128)S(1)}, f32[4,128]{1,0:T(4,128)}, u32[]{:S(2)}) %copy-start.17) | copy-done | bytes 2072
  32.7 26.2 %conditional.3 = (bf16[128,256]{1,0:T(8,128)(2,1)}, bf16[128,256]{1,0:T(8,128)(2,1)}, bf16[128,256]{1,0:T(8,128)(2,1)}, bf16[128,256]{1,0:T(8,128)(2,1)}, f32[512,256]{1,0:T(8,128)}, /*index=5*/f32[4,128]{1,0:T(4,128)}) conditional(s32[]{:T(128)} %bitcast.4, (bf16[128,256]{1,0:T(8,128)(2,1)S(1)}, ...), branch_computations={%region_7.0_spmd, %region_8.0_spmd, %region_9.0_spmd, %region_10.0... | conditional | flops 1611661312 | bytes 6291852 | solution.py:48
  32.7 3.4 %collective-permute-start.81 = (bf16[128,256]{1,0:T(8,128)(2,1)S(1)}, bf16[128,256]{1,0:T(8,128)(2,1)S(1)}, u32[]{:S(2)}, u32[]{:S(2)}) collective-permute-start(bf16[128,256]{1,0:T(8,128)(2,1)S(1)} %get-tuple-element.357), channel_id=1, source_target_pairs={{0,17},{1,16},{2,19},{3,18},{4,21},{5,20},{6,23},{7,22},{8,25},{9,... | collective-permute-start | bytes 196616 | tf_op jit(solution)/shard_map/cond/branch_3_fun/ppermute | solution.py:33
  36.1 0.0 collective-permute-start.80
  36.1 5.0 %collective-permute-start.85 = (bf16[128,256]{1,0:T(8,128)(2,1)S(1)}, bf16[128,256]{1,0:T(8,128)(2,1)S(1)}, u32[]{:S(2)}, u32[]{:S(2)}) collective-permute-start(bf16[128,256]{1,0:T(8,128)(2,1)S(1)} %get-tuple-element.357), channel_id=1, source_target_pairs={{0,19},{1,18},{2,17},{3,16},{4,23},{5,22},{6,21},{7,20},{8,27},{9,... | collective-permute-start | bytes 196616 | tf_op jit(solution)/shard_map/cond/branch_3_fun/ppermute | solution.py:33
  41.1 0.0 collective-permute-start.84
  41.1 4.2 %tile_work.48 = (f32[512,256]{1,0:T(8,128)S(1)}, bf16[128,256]{1,0:T(8,128)(2,1)S(1)}, bf16[128,256]{1,0:T(8,128)(2,1)S(1)}) custom-call(s32[1,560]{1,0:T(1,128)S(1)} %get-tuple-element.354.plan, f32[512,256]{1,0:T(8,128)} %get-tuple-element.355.src_ref.table_ref, f32[72,256]{1,0:T(8,128)S(1)} %get-tuple-element.356.row_ref, ...), custom_call_target="tpu_custom_call" | custom-call | flops 805306368 | bytes 524288 | tf_op jit(solution)/shard_map/cond/branch_3_fun/tile_work/pallas_call | solution.py:199
  45.3 0.1 collective-permute-start.82
  45.4 1.1 %collective-permute-start.83 = (bf16[128,256]{1,0:T(8,128)(2,1)S(1)}, bf16[128,256]{1,0:T(8,128)(2,1)}, u32[]{:S(2)}, u32[]{:S(2)}) collective-permute-start(bf16[128,256]{1,0:T(8,128)(2,1)S(1)} %get-tuple-element.359), channel_id=1, source_target_pairs={{0,17},{1,16},{2,19},{3,18},{4,21},{5,20},{6,23},{7,22},{8,25},{9,... | collective-permute-start | bytes 196616 | tf_op jit(solution)/shard_map/cond/branch_3_fun/ppermute | solution.py:33
  46.5 0.0 collective-permute-done.85.refs_1_
  46.5 0.7 %collective-permute-done.84.refs_0_ = bf16[128,256]{1,0:T(8,128)(2,1)S(1)} collective-permute-done((bf16[128,256]{1,0:T(8,128)(2,1)S(1)}, bf16[128,256]{1,0:T(8,128)(2,1)S(1)}, u32[]{:S(2)}, u32[]{:S(2)}) %collective-permute-start.84) | collective-permute-done | bytes 65568 | tf_op jit(solution)/shard_map/cond/branch_3_fun/ppermute | solution.py:33
  47.2 3.1 %tile_work.49 = (f32[512,256]{1,0:T(8,128)S(1)}, bf16[128,256]{1,0:T(8,128)(2,1)S(1)}, bf16[128,256]{1,0:T(8,128)(2,1)S(1)}) custom-call(s32[1,560]{1,0:T(1,128)S(1)} %get-tuple-element.354.plan, f32[512,256]{1,0:T(8,128)S(1)} %copy-done.12, f32[72,256]{1,0:T(8,128)S(1)} %get-tuple-element.356.row_ref, ...), custom_call_target="tpu_custom_call", output_to_operand_aliasing={{0}: (5, {})} | custom-call | flops 805306368 | bytes 524288 | tf_op jit(solution)/shard_map/cond/branch_3_fun/tile_work/pallas_call | solution.py:199
  50.3 1.5 %collective-permute-start.86 = (bf16[128,256]{1,0:T(8,128)(2,1)S(1)}, bf16[128,256]{1,0:T(8,128)(2,1)}, u32[]{:S(2)}, u32[]{:S(2)}) collective-permute-start(bf16[128,256]{1,0:T(8,128)(2,1)S(1)} %get-tuple-element.361), channel_id=1, source_target_pairs={{0,18},{1,19},{2,16},{3,17},{4,22},{5,23},{6,20},{7,21},{8,26},{9,... | collective-permute-start | bytes 196616 | tf_op jit(solution)/shard_map/cond/branch_3_fun/ppermute | solution.py:33
  51.8 1.9 %collective-permute-start.87 = (bf16[128,256]{1,0:T(8,128)(2,1)S(1)}, bf16[128,256]{1,0:T(8,128)(2,1)}, u32[]{:S(2)}, u32[]{:S(2)}) collective-permute-start(bf16[128,256]{1,0:T(8,128)(2,1)S(1)} %get-tuple-element.362), channel_id=1, source_target_pairs={{0,19},{1,18},{2,17},{3,16},{4,23},{5,22},{6,21},{7,20},{8,27},{9,... | collective-permute-start | bytes 196616 | tf_op jit(solution)/shard_map/cond/branch_3_fun/ppermute | solution.py:33
  53.7 1.3 %update_source.24 = (f32[512,256]{1,0:T(8,128)}, f32[4,128]{1,0:T(4,128)}) custom-call(f32[512,256]{1,0:T(8,128)S(1)} %copy-done.12, f32[4,128]{1,0:T(4,128)S(1)} %get-tuple-element.363.state_ref, f32[512,256]{1,0:T(8,128)S(1)} %get-tuple-element.364.grad_ref), custom_call_target="tpu_custom_call" | custom-call | flops 1048576 | bytes 1048576 | tf_op jit(solution)/shard_map/cond/branch_3_fun/update_source/pallas_call | solution.py:256
  55.0 0.0 collective-permute-done.83
  55.0 2.2 %collective-permute-done.86 = bf16[128,256]{1,0:T(8,128)(2,1)} collective-permute-done((bf16[128,256]{1,0:T(8,128)(2,1)S(1)}, bf16[128,256]{1,0:T(8,128)(2,1)}, u32[]{:S(2)}, u32[]{:S(2)}) %collective-permute-start.86) | collective-permute-done | bytes 65568 | tf_op jit(solution)/shard_map/cond/branch_3_fun/ppermute | solution.py:33
  57.2 1.6 %collective-permute-done.87 = bf16[128,256]{1,0:T(8,128)(2,1)} collective-permute-done((bf16[128,256]{1,0:T(8,128)(2,1)S(1)}, bf16[128,256]{1,0:T(8,128)(2,1)}, u32[]{:S(2)}, u32[]{:S(2)}) %collective-permute-start.87) | collective-permute-done | bytes 65568 | tf_op jit(solution)/shard_map/cond/branch_3_fun/ppermute | solution.py:33
  58.9 1.7 %update_target.3 = (f32[128,256]{1,0:T(8,128)}, f32[1,128]{1,0:T(1,128)}) custom-call(f32[128,256]{1,0:T(8,128)S(1)} %get-tuple-element.448.table_ref, f32[1,128]{1,0:T(1,128)S(1)} %get-tuple-element.449.state_ref, bf16[128,256]{1,0:T(8,128)(2,1)} %get-tuple-element.450.refs_0_, bf16[128,256]{1,0:T(8,128)(2,1)} %get-tuple-element.451.refs_1_, ...), custom_call_target="tpu_custom_call" | custom-call | flops 262144 | bytes 262144 | tf_op jit(solution)/shard_map/update_target/pallas_call | solution.py:291
  (14 shorter events, 0.0 us)
Async XLA Ops:
  0.6 0.7 %copy-start.19 = (s32[1,1,2,64]{3,2,1,0:T(2,128)S(1)}, s32[1,1,2,64]{3,2,1,0:T(2,128)}, u32[]{:S(2)}) copy-start(s32[1,1,2,64]{3,2,1,0:T(2,128)} %param.30) | copy-start | bytes 1540
  0.6 0.7 %copy-start.18 = (s32[1,1,2,64]{3,2,1,0:T(2,128)S(1)}, s32[1,1,2,64]{3,2,1,0:T(2,128)}, u32[]{:S(2)}) copy-start(s32[1,1,2,64]{3,2,1,0:T(2,128)} %param.29) | copy-start | bytes 1540
  0.7 0.7 %copy-start.20 = (s32[1,1,2]{2,1,0:T(1,128)S(1)}, s32[1,1,2]{2,1,0:T(1,128)}, u32[]{:S(2)}) copy-start(s32[1,1,2]{2,1,0:T(1,128)} %param.31) | copy-start | bytes 28
  4.4 0.7 %copy-start.16 = (f32[512]{0:T(512)S(1)}, f32[512]{0:T(512)}, u32[]{:S(2)}) copy-start(f32[512]{0:T(512)} %param.24) | copy-start | bytes 6148
  5.1 25.1 %copy-start = (f32[128,256]{1,0:T(8,128)S(1)}, f32[128,256]{1,0:T(8,128)}, u32[]{:S(2)}) copy-start(f32[128,256]{1,0:T(8,128)} %table_ref.1) | copy-start | bytes 393220
  5.1 8.2 %collective-permute-start.9 = (bf16[128,256]{1,0:T(8,128)(2,1)S(1)}, bf16[128,256]{1,0:T(8,128)(2,1)S(1)}, u32[]{:S(2)}, u32[]{:S(2)}) collective-permute-start(bf16[128,256]{1,0:T(8,128)(2,1)S(1)} %get-tuple-element.216), channel_id=1, source_target_pairs={{0,9},{1,8},{2,11},{3,10},{4,13},{5,12},{6,15},{7,14},{8,1},{9,0},... | collective-permute-start | bytes 196616 | tf_op jit(solution)/shard_map/cond/branch_1_fun/ppermute | solution.py:33
  9.0 4.3 %collective-permute-start.8 = (bf16[128,256]{1,0:T(8,128)(2,1)S(1)}, bf16[128,256]{1,0:T(8,128)(2,1)S(1)}, u32[]{:S(2)}, u32[]{:S(2)}) collective-permute-start(bf16[128,256]{1,0:T(8,128)(2,1)S(1)} %get-tuple-element.216), channel_id=1, source_target_pairs={{0,8},{1,9},{2,10},{3,11},{4,12},{5,13},{6,14},{7,15},{8,0},{9,1},... | collective-permute-start | bytes 196616 | tf_op jit(solution)/shard_map/cond/branch_1_fun/ppermute | solution.py:33
  9.7 9.7 %collective-permute-start.13 = (bf16[128,256]{1,0:T(8,128)(2,1)S(1)}, bf16[128,256]{1,0:T(8,128)(2,1)S(1)}, u32[]{:S(2)}, u32[]{:S(2)}) collective-permute-start(bf16[128,256]{1,0:T(8,128)(2,1)S(1)} %get-tuple-element.216), channel_id=1, source_target_pairs={{0,11},{1,10},{2,9},{3,8},{4,15},{5,14},{6,13},{7,12},{8,3},{9,2},... | collective-permute-start | bytes 196616 | tf_op jit(solution)/shard_map/cond/branch_1_fun/ppermute | solution.py:33
  13.3 6.7 %collective-permute-start.12 = (bf16[128,256]{1,0:T(8,128)(2,1)S(1)}, bf16[128,256]{1,0:T(8,128)(2,1)S(1)}, u32[]{:S(2)}, u32[]{:S(2)}) collective-permute-start(bf16[128,256]{1,0:T(8,128)(2,1)S(1)} %get-tuple-element.216), channel_id=1, source_target_pairs={{0,10},{1,11},{2,8},{3,9},{4,14},{5,15},{6,12},{7,13},{8,2},{9,3},... | collective-permute-start | bytes 196616 | tf_op jit(solution)/shard_map/cond/branch_1_fun/ppermute | solution.py:33
  13.3 6.7 %copy-start.3 = (f32[512,256]{1,0:T(8,128)S(1)}, f32[512,256]{1,0:T(8,128)}, u32[]{:S(2)}) copy-start(f32[512,256]{1,0:T(8,128)} %get-tuple-element.214.src_ref.table_ref) | copy-start | bytes 1572868 | tf_op jit(solution)/shard_map/cond
  15.9 12.6 %collective-permute-start.10 = (bf16[128,256]{1,0:T(8,128)(2,1)S(1)}, bf16[128,256]{1,0:T(8,128)(2,1)}, u32[]{:S(2)}, u32[]{:S(2)}) collective-permute-start(bf16[128,256]{1,0:T(8,128)(2,1)S(1)} %get-tuple-element.217), channel_id=1, source_target_pairs={{0,8},{1,9},{2,10},{3,11},{4,12},{5,13},{6,14},{7,15},{8,0},{9,1},... | collective-permute-start | bytes 196616 | tf_op jit(solution)/shard_map/cond/branch_1_fun/ppermute | solution.py:33
  17.1 11.4 %collective-permute-start.11 = (bf16[128,256]{1,0:T(8,128)(2,1)S(1)}, bf16[128,256]{1,0:T(8,128)(2,1)}, u32[]{:S(2)}, u32[]{:S(2)}) collective-permute-start(bf16[128,256]{1,0:T(8,128)(2,1)S(1)} %get-tuple-element.218), channel_id=1, source_target_pairs={{0,9},{1,8},{2,11},{3,10},{4,13},{5,12},{6,15},{7,14},{8,1},{9,0},... | collective-permute-start | bytes 196616 | tf_op jit(solution)/shard_map/cond/branch_1_fun/ppermute | solution.py:33
  21.4 7.1 %collective-permute-start.14 = (bf16[128,256]{1,0:T(8,128)(2,1)S(1)}, bf16[128,256]{1,0:T(8,128)(2,1)}, u32[]{:S(2)}, u32[]{:S(2)}) collective-permute-start(bf16[128,256]{1,0:T(8,128)(2,1)S(1)} %get-tuple-element.220), channel_id=1, source_target_pairs={{0,10},{1,11},{2,8},{3,9},{4,14},{5,15},{6,12},{7,13},{8,2},{9,3},... | collective-permute-start | bytes 196616 | tf_op jit(solution)/shard_map/cond/branch_1_fun/ppermute | solution.py:33
  23.2 7.1 %collective-permute-start.15 = (bf16[128,256]{1,0:T(8,128)(2,1)S(1)}, bf16[128,256]{1,0:T(8,128)(2,1)}, u32[]{:S(2)}, u32[]{:S(2)}) collective-permute-start(bf16[128,256]{1,0:T(8,128)(2,1)S(1)} %get-tuple-element.221), channel_id=1, source_target_pairs={{0,11},{1,10},{2,9},{3,8},{4,15},{5,14},{6,13},{7,12},{8,3},{9,2},... | collective-permute-start | bytes 196616 | tf_op jit(solution)/shard_map/cond/branch_1_fun/ppermute | solution.py:33
  30.2 0.7 %copy-start.1 = (f32[128]{0:T(128)S(1)}, f32[128]{0:T(128)}, u32[]{:S(2)}) copy-start(f32[128]{0:T(128)} %param.26) | copy-start | bytes 1540
  32.0 0.7 %copy-start.17 = (f32[4,128]{1,0:T(4,128)S(1)}, f32[4,128]{1,0:T(4,128)}, u32[]{:S(2)}) copy-start(f32[4,128]{1,0:T(4,128)} %get-tuple-element.445) | copy-start | bytes 6148
  32.7 8.4 %collective-permute-start.81 = (bf16[128,256]{1,0:T(8,128)(2,1)S(1)}, bf16[128,256]{1,0:T(8,128)(2,1)S(1)}, u32[]{:S(2)}, u32[]{:S(2)}) collective-permute-start(bf16[128,256]{1,0:T(8,128)(2,1)S(1)} %get-tuple-element.357), channel_id=1, source_target_pairs={{0,17},{1,16},{2,19},{3,18},{4,21},{5,20},{6,23},{7,22},{8,25},{9,... | collective-permute-start | bytes 196616 | tf_op jit(solution)/shard_map/cond/branch_3_fun/ppermute | solution.py:33
  36.1 5.0 %collective-permute-start.80 = (bf16[128,256]{1,0:T(8,128)(2,1)S(1)}, bf16[128,256]{1,0:T(8,128)(2,1)S(1)}, u32[]{:S(2)}, u32[]{:S(2)}) collective-permute-start(bf16[128,256]{1,0:T(8,128)(2,1)S(1)} %get-tuple-element.357), channel_id=1, source_target_pairs={{0,16},{1,17},{2,18},{3,19},{4,20},{5,21},{6,22},{7,23},{8,24},{9,... | collective-permute-start | bytes 196616 | tf_op jit(solution)/shard_map/cond/branch_3_fun/ppermute | solution.py:33
  36.1 10.4 %collective-permute-start.85 = (bf16[128,256]{1,0:T(8,128)(2,1)S(1)}, bf16[128,256]{1,0:T(8,128)(2,1)S(1)}, u32[]{:S(2)}, u32[]{:S(2)}) collective-permute-start(bf16[128,256]{1,0:T(8,128)(2,1)S(1)} %get-tuple-element.357), channel_id=1, source_target_pairs={{0,19},{1,18},{2,17},{3,16},{4,23},{5,22},{6,21},{7,20},{8,27},{9,... | collective-permute-start | bytes 196616 | tf_op jit(solution)/shard_map/cond/branch_3_fun/ppermute | solution.py:33
  41.1 6.1 %collective-permute-start.84 = (bf16[128,256]{1,0:T(8,128)(2,1)S(1)}, bf16[128,256]{1,0:T(8,128)(2,1)S(1)}, u32[]{:S(2)}, u32[]{:S(2)}) collective-permute-start(bf16[128,256]{1,0:T(8,128)(2,1)S(1)} %get-tuple-element.357), channel_id=1, source_target_pairs={{0,18},{1,19},{2,16},{3,17},{4,22},{5,23},{6,20},{7,21},{8,26},{9,... | collective-permute-start | bytes 196616 | tf_op jit(solution)/shard_map/cond/branch_3_fun/ppermute | solution.py:33
  41.1 6.1 %copy-start.12 = (f32[512,256]{1,0:T(8,128)S(1)}, f32[512,256]{1,0:T(8,128)}, u32[]{:S(2)}) copy-start(f32[512,256]{1,0:T(8,128)} %get-tuple-element.355.src_ref.table_ref) | copy-start | bytes 1572868 | tf_op jit(solution)/shard_map/cond
  45.3 9.7 %collective-permute-start.82 = (bf16[128,256]{1,0:T(8,128)(2,1)S(1)}, bf16[128,256]{1,0:T(8,128)(2,1)}, u32[]{:S(2)}, u32[]{:S(2)}) collective-permute-start(bf16[128,256]{1,0:T(8,128)(2,1)S(1)} %get-tuple-element.358), channel_id=1, source_target_pairs={{0,16},{1,17},{2,18},{3,19},{4,20},{5,21},{6,22},{7,23},{8,24},{9,... | collective-permute-start | bytes 196616 | tf_op jit(solution)/shard_map/cond/branch_3_fun/ppermute | solution.py:33
  45.4 9.7 %collective-permute-start.83 = (bf16[128,256]{1,0:T(8,128)(2,1)S(1)}, bf16[128,256]{1,0:T(8,128)(2,1)}, u32[]{:S(2)}, u32[]{:S(2)}) collective-permute-start(bf16[128,256]{1,0:T(8,128)(2,1)S(1)} %get-tuple-element.359), channel_id=1, source_target_pairs={{0,17},{1,16},{2,19},{3,18},{4,21},{5,20},{6,23},{7,22},{8,25},{9,... | collective-permute-start | bytes 196616 | tf_op jit(solution)/shard_map/cond/branch_3_fun/ppermute | solution.py:33
  50.3 6.9 %collective-permute-start.86 = (bf16[128,256]{1,0:T(8,128)(2,1)S(1)}, bf16[128,256]{1,0:T(8,128)(2,1)}, u32[]{:S(2)}, u32[]{:S(2)}) collective-permute-start(bf16[128,256]{1,0:T(8,128)(2,1)S(1)} %get-tuple-element.361), channel_id=1, source_target_pairs={{0,18},{1,19},{2,16},{3,17},{4,22},{5,23},{6,20},{7,21},{8,26},{9,... | collective-permute-start | bytes 196616 | tf_op jit(solution)/shard_map/cond/branch_3_fun/ppermute | solution.py:33
  51.8 7.1 %collective-permute-start.87 = (bf16[128,256]{1,0:T(8,128)(2,1)S(1)}, bf16[128,256]{1,0:T(8,128)(2,1)}, u32[]{:S(2)}, u32[]{:S(2)}) collective-permute-start(bf16[128,256]{1,0:T(8,128)(2,1)S(1)} %get-tuple-element.362), channel_id=1, source_target_pairs={{0,19},{1,18},{2,17},{3,16},{4,23},{5,22},{6,21},{7,20},{8,27},{9,... | collective-permute-start | bytes 196616 | tf_op jit(solution)/shard_map/cond/branch_3_fun/ppermute | solution.py:33

commit v3 on v2

--- a/solution.py
+++ b/solution.py
@@ -17,7 +17,7 @@
 AXES = ("bucket", "rep")
 SMEM = pl.BlockSpec(memory_space=pltpu.SMEM)
 VMEM = pl.BlockSpec(memory_space=pltpu.VMEM)
-FIRST_GRANT = 60 * 1024 * 1024
+HBM = pl.BlockSpec(memory_space=pltpu.HBM)
 GRANT = pltpu.CompilerParams(vmem_limit_bytes=12 * 1024 * 1024)
 
 
@@ -98,17 +98,40 @@
             plan[0, at + q + extra] = blocks[0] * room + ends[blocks[0]]
 
 
-def first_kernel(rounds, number, cut, none_rel, rep, tiles, rel, counts, partners, dst_ref, rel_ref, plan, rows_ref, row_ref, *masks):
+def in_hbm(*arrays):
+    return [pltpu.with_memory_space_constraint(array, pltpu.HBM) for array in arrays]
+
+
+def fetch(sources, targets, sem):
+    copies = [
+        pltpu.make_async_copy(source, target, sem.at[i])
+        for i, (source, target) in enumerate(zip(sources, targets))
+    ]
+    for copy in copies:
+        copy.start()
+    return copies
+
+
+def first_kernel(number, cut, none_rel, rep, *refs):
+    sources, (plan, rows_ref, row_ref, mask), held, sem = refs[:6], refs[6:10], refs[10:16], refs[16]
+    copies = fetch(sources, held, sem)
+    tiles, rel, counts, partners, dst_ref, rel_ref = held
+    for copy in copies:
+        copy.wait()
     rows_ref[...] = dst_ref[...].astype(jnp.bfloat16)
     row_ref[pl.ds(0, none_rel), :] = rel_ref[...] * (0.5 * rel_ref.shape[1] ** -0.5)
     row_ref[pl.ds(none_rel, 8), :] = jnp.zeros((8, rel_ref.shape[1]), jnp.float32)
-    for k in range(rounds):
-        masks[k][0, 0] = partners[k, 0]
+    mask[0, 0] = partners[0, 0]
     flip = rep[0] * (dst_ref.shape[0] // TILE)
     sort_tiles(0, cut, none_rel, flip, number, tiles, rel, counts, plan)
 
 
-def later_kernel(k, shard_blocks, number, cut, none_rel, rep, tiles, rel, counts, after, plan):
+def later_kernel(k, shard_blocks, number, cut, none_rel, rep, *refs):
+    sources, (plan, mask), held, sem = refs[:4], refs[5:7], refs[7:11], refs[11]
+    for copy in fetch(sources, held, sem):
+        copy.wait()
+    tiles, rel, counts, partners = held
+    mask[0, 0] = partners[k, 0]
     sort_tiles(k, cut, none_rel, rep[0] * shard_blocks, number, tiles, rel, counts, plan)
 
 
@@ -231,8 +254,10 @@
     return table, jnp.sum(jnp.where(same, state, 0.0), axis=0, keepdims=True)
 
 
-def source_kernel(table_ref, state_ref, grad_ref, table_out, state_out, table_new, state_new, sem):
+def source_kernel(table_ref, state_hbm, grad_ref, table_out, state_out, table_new, state_new, state_ref, sem):
     blocks = table_ref.shape[0] // TILE
+    (state_in,) = fetch([state_hbm], [state_ref], sem)
+    state_in.wait()
 
     def block(i, carry):
         rows = pl.ds(pl.multiple_of(i * TILE, TILE), TILE)
@@ -242,24 +267,19 @@
         return carry
 
     lax.fori_loop(0, blocks, block, 0)
-    copies = [
-        pltpu.make_async_copy(table_new, table_out, sem.at[0]),
-        pltpu.make_async_copy(state_new, state_out, sem.at[1]),
-    ]
-    for copy in copies:
-        copy.start()
-    for copy in copies:
+    for copy in fetch([table_new, state_new], [table_out, state_out], sem):
         copy.wait()
 
 
 def update_source(table, state, grad):
     return pl.pallas_call(
         source_kernel,
-        in_specs=[VMEM] * 3,
-        out_specs=[pl.BlockSpec(memory_space=pltpu.HBM)] * 2,
+        in_specs=[VMEM, HBM, VMEM],
+        out_specs=[HBM] * 2,
         out_shape=[pltpu.HBM(table.shape, jnp.float32), pltpu.HBM(state.shape, jnp.float32)],
         scratch_shapes=[
             pltpu.VMEM(table.shape, jnp.float32),
+            pltpu.VMEM(state.shape, jnp.float32),
             pltpu.VMEM(state.shape, jnp.float32),
             pltpu.SemaphoreType.DMA((2,)),
         ],
@@ -268,30 +288,37 @@
         ),
         compiler_params=GRANT,
         name="update_source",
-    )(table, state, grad)
-
-
-def target_kernel(parts, last, table_ref, state_ref, *refs):
+    )(table, *in_hbm(state), grad)
+
+
+def target_kernel(parts, last, table_ref, *refs):
+    sources, outs = refs[: parts + 1], refs[parts + 1 : parts + 3 + (not last)]
+    *held, sem = refs[parts + 3 + (not last) :]
+    for copy in fetch(sources, held, sem):
+        copy.wait()
     for i in range(table_ref.shape[0] // TILE):
         rows = pl.ds(i * TILE, TILE)
-        grad = refs[0][rows, :].astype(jnp.float32)
-        for other in refs[1:parts]:
+        grad = held[1][rows, :].astype(jnp.float32)
+        for other in held[2:]:
             grad = grad + other[rows, :].astype(jnp.float32)
         if parts > 1:
             grad = grad.astype(jnp.bfloat16).astype(jnp.float32)
-        table, state = adagrad_block(table_ref[rows, :], state_ref[pl.ds(i, 1), :], grad)
-        refs[parts][rows, :] = table
-        refs[parts + 1][pl.ds(i, 1), :] = state
+        table, state = adagrad_block(table_ref[rows, :], held[0][pl.ds(i, 1), :], grad)
+        outs[0][rows, :] = table
+        outs[1][pl.ds(i, 1), :] = state
         if not last:
-            refs[parts + 2][rows, :] = table.astype(jnp.bfloat16)
-
-
-def update_target(table, state, parts, last):
+            outs[2][rows, :] = table.astype(jnp.bfloat16)
+
+
+def update_target(table, state, parts, first, last):
     low = [] if last else [jax.ShapeDtypeStruct(table.shape, jnp.bfloat16)]
     return pl.pallas_call(
         functools.partial(target_kernel, len(parts), last),
-        in_specs=[VMEM] * (2 + len(parts)),
+        in_specs=[VMEM] + [HBM] * (1 + len(parts)),
         out_specs=[VMEM] * (2 + len(low)),
+        scratch_shapes=[pltpu.VMEM(state.shape, jnp.float32)]
+        + [pltpu.VMEM(part.shape, part.dtype) for part in parts]
+        + [pltpu.SemaphoreType.DMA((1 + len(parts),))],
         out_shape=[
             jax.ShapeDtypeStruct(table.shape, jnp.float32),
             jax.ShapeDtypeStruct(state.shape, jnp.float32),
@@ -302,7 +329,7 @@
         ),
         compiler_params=GRANT,
         name="update_target",
-    )(table, state, *parts)
+    )(table, *(in_hbm(state) if first else [state]), *parts)
 
 
 def per_device(
@@ -321,22 +348,30 @@
     cut = near * shard_blocks
     low_chunk, *high_chunks = bit_chunks()
     scalars = (
-        lax.axis_index("rep").astype(jnp.int32).reshape(1), tiles[0, 0], tile_rel[0, 0], counts[0, 0],
+        lax.axis_index("rep").astype(jnp.int32).reshape(1), tiles[0, 0], tile_rel[0, 0], counts[0, 0], partners,
     )
+    held = [pltpu.SMEM(x.shape, jnp.int32) for x in scalars[1:]]
+    mask_shape = jax.ShapeDtypeStruct((1, 1), jnp.int32)
     plan_shape = jax.ShapeDtypeStruct((1, lists[-1]), jnp.int32)
-    plan, rows, rel_rows, *masks = pl.pallas_call(
-        functools.partial(first_kernel, rounds, number, cut, none_rel),
-        in_specs=[SMEM] * 5 + [VMEM] * 2,
-        out_specs=[SMEM, VMEM, VMEM] + [SMEM] * rounds,
+    plan, rows, rel_rows, mask = pl.pallas_call(
+        functools.partial(first_kernel, number, cut, none_rel),
+        in_specs=[SMEM] + [HBM] * 6,
+        out_specs=[SMEM, VMEM, VMEM, SMEM],
         out_shape=[
             plan_shape,
             jax.ShapeDtypeStruct(dst_table.shape, jnp.bfloat16),
             jax.ShapeDtypeStruct((none_rel + 8, rel_table.shape[1]), jnp.float32),
-        ]
-        + [jax.ShapeDtypeStruct((1, 1), jnp.int32)] * rounds,
-        compiler_params=pltpu.CompilerParams(vmem_limit_bytes=FIRST_GRANT),
+            mask_shape,
+        ],
+        scratch_shapes=held
+        + [
+            pltpu.VMEM(dst_table.shape, jnp.float32),
+            pltpu.VMEM(rel_table.shape, jnp.float32),
+            pltpu.SemaphoreType.DMA((6,)),
+        ],
+        compiler_params=GRANT,
         name="first",
-    )(*scalars, partners, dst_table, rel_table)
+    )(scalars[0], *in_hbm(*scalars[1:], dst_table, rel_table))
 
     def branch(value, operands, k):
         rows, plan, rel_rows, src_table, src_state, scalars = operands
@@ -352,31 +387,35 @@
         src_grad, parts = tile_work(1, lists, cut, slots // 2, plan, src_table, rel_rows, shards[near:], src_grad)
         for j in range(near, reps):
             back.append(send(parts[j - near], value, j))
+        following = ()
         if k + 1 < rounds:
-            plan = pl.pallas_call(
+            following = pl.pallas_call(
                 functools.partial(later_kernel, k + 1, shard_blocks, number, cut, none_rel),
-                in_specs=[SMEM] * 4 + [pl.BlockSpec(memory_space=pl.ANY)],
-                out_specs=SMEM,
-                out_shape=plan_shape,
+                in_specs=[SMEM] + [HBM] * 4 + [pl.BlockSpec(memory_space=pl.ANY)],
+                out_specs=[SMEM] * 2,
+                out_shape=[plan_shape, mask_shape],
+                scratch_shapes=held + [pltpu.SemaphoreType.DMA((4,))],
                 compiler_params=GRANT,
                 name="later",
-            )(*scalars, src_grad)
+            )(scalars[0], *in_hbm(*scalars[1:]), src_grad)
         src_table, src_state = update_source(src_table, src_state, src_grad)
-        return tuple(back), (plan,) if k + 1 < rounds else (), src_table, src_state
+        return tuple(back), tuple(following), src_table, src_state
 
     for k in range(rounds):
-        mask = masks[k].reshape(())
-        back, plans, src_table, src_state = by_mask(
-            mask,
+        round_mask = mask.reshape(())
+        back, following, src_table, src_state = by_mask(
+            round_mask,
             low_chunk,
             functools.partial(branch, k=k),
-            (send_high(rows, mask), plan, rel_rows, src_table, src_state, scalars),
-        )
-        (plan,) = plans or (None,)
+            (send_high(rows, round_mask), plan, rel_rows, src_table, src_state, scalars),
+        )
+        plan, mask = following or (None, None)
         if high_chunks:
             total = functools.reduce(jnp.add, [x.astype(jnp.float32) for x in back])
-            back = [send_high(total.astype(jnp.bfloat16), mask)]
-        dst_table, dst_state, *rows = update_target(dst_table, dst_state, back, k + 1 == rounds)
+            back = [send_high(total.astype(jnp.bfloat16), round_mask)]
+        dst_table, dst_state, *rows = update_target(
+            dst_table, dst_state, back, k == 0, k + 1 == rounds
+        )
         rows = rows[0] if rows else None
     return (src_table, src_state.reshape(-1), dst_table, dst_state.reshape(-1))
 

time: 61 us -> 58.8 us (0.964)
  local copies, waits for them, and re-layouts: 2.69 us -> 0.01 us
  waiting for transfers between devices: 6.82 us -> 4.96 us
  Pallas kernels: 21.1 us -> 22.8 us
    unnamed x14 -> x2, local copies, waits for them, and re-layouts: 2.68 us -> 0.01 us
    ppermute x16, waiting for transfers between devices: 6.82 us -> 4.96 us  [send(): return lax.ppermute(rows, AXES, pairs)]
    pallas_call x3, Pallas kernels: 4.44 us -> 5.87 us  [the longest x2 4.07 us: update_source(): pl.pallas_call(source_kernel, in_specs=[VMEM, HBM, VMEM], out_specs=[HBM]...]
  transfers between devices with their start and end apart: 16 -> 16, of which waited for: 5 -> 5; matrix products, arithmetic and copies ran while one was open for 0% -> 0% of each run, Pallas kernels for 27% -> 31%
where the time goes in v3:
time: 58.8 us; the launch traced here: 58.4 us
  starting transfers between devices  28.3 us (48%)
  Pallas kernels  22.8 us (39%)
  waiting for transfers between devices  4.96 us (8%)
  between operations  2.13 us (4%)
    ppermute x16, starting transfers between devices, send(): return lax.ppermute(rows, AXES, pairs)  28.3 us
    pallas_call x4, Pallas kernels, tile_work(): pl.pallas_call(functools.partial(tile_kernel, index, lists, cut, len(shar...  11.4 us
    ppermute x16, waiting for transfers between devices, send(): return lax.ppermute(rows, AXES, pairs)  4.96 us
    pallas_call x2, Pallas kernels, update_source(): pl.pallas_call(source_kernel, in_specs=[VMEM, HBM, VMEM], out_specs=[HBM]...  4.07 us
    pallas_call x2, Pallas kernels, update_target(): pl.pallas_call(functools.partial(target_kernel, len(parts), last), in_spe...  2.94 us
    pallas_call x1, Pallas kernels, branch(): pl.pallas_call(functools.partial(later_kernel, k + 1, shard_blocks, numbe...  2.64 us
    pallas_call x1, Pallas kernels, per_device(): pl.pallas_call(functools.partial(first_kernel, number, cut, none_rel), in...  1.8 us
  transfers between devices with their start and end apart: 16, of which 5 were waited for; matrix products, arithmetic and copies ran while one was open for 0% of the time, Pallas kernels for 31%

profile of v3, /device:TPU:0, one launch (start us, length us, event | category | flops | bytes accessed | tf_op | source)
XLA Modules:
  0.0 58.4 jit_solution(14900690948053002000)
XLA Ops:
  0.6 1.8 %first.1 = (s32[1,560]{1,0:T(1,128)S(1)}, bf16[128,256]{1,0:T(8,128)(2,1)S(1)}, f32[72,256]{1,0:T(8,128)S(1)}, s32[1,1]{1,0:T(1,128)}) custom-call(s32[1]{0:T(128)} %bitcast.rep, s32[2,64]{1,0:T(2,128)} %bitcast.17, s32[2,64]{1,0:T(2,128)} %bitcast.25, s32[2]{0:T(128)} %bitcast.33, s32[2,8]{1,0:T(2,128)} %refs_3_.1, f32[128,256]{1,0:T(8,128)} %table_ref.1, ...), custom_call_target="tpu_custom_call" | custom-call | tf_op jit(solution)/shard_map/first/pallas_call | solution.py:356
  3.1 0.0 copy-start
  3.1 25.2 %conditional.2 = (bf16[128,256]{1,0:T(8,128)(2,1)}, bf16[128,256]{1,0:T(8,128)(2,1)}, bf16[128,256]{1,0:T(8,128)(2,1)}, bf16[128,256]{1,0:T(8,128)(2,1)}, s32[1,...) conditional(s32[]{:T(128)} %bitcast.4, ...), branch_computations={%region_0.0_spmd, %region_1.0_spmd, %region_2.0_spmd, %region_3.0_... | conditional | flops 1611661312 | bytes 6291868 | solution.py:48
  3.1 4.0 %collective-permute-start.9 = (bf16[128,256]{1,0:T(8,128)(2,1)S(1)}, bf16[128,256]{1,0:T(8,128)(2,1)S(1)}, u32[]{:S(2)}, u32[]{:S(2)}) collective-permute-start(bf16[128,256]{1,0:T(8,128)(2,1)S(1)} %get-tuple-element.233), channel_id=1, source_target_pairs={{0,9},{1,8},{2,11},{3,10},{4,13},{5,12},{6,15},{7,14},{8,1},{9,0},... | collective-permute-start | bytes 196616 | tf_op jit(solution)/shard_map/cond/branch_1_fun/ppermute | solution.py:33
  7.1 0.7 %collective-permute-start.8 = (bf16[128,256]{1,0:T(8,128)(2,1)S(1)}, bf16[128,256]{1,0:T(8,128)(2,1)S(1)}, u32[]{:S(2)}, u32[]{:S(2)}) collective-permute-start(bf16[128,256]{1,0:T(8,128)(2,1)S(1)} %get-tuple-element.233), channel_id=1, source_target_pairs={{0,8},{1,9},{2,10},{3,11},{4,12},{5,13},{6,14},{7,15},{8,0},{9,1},... | collective-permute-start | bytes 196616 | tf_op jit(solution)/shard_map/cond/branch_1_fun/ppermute | solution.py:33
  7.8 3.6 %collective-permute-start.13 = (bf16[128,256]{1,0:T(8,128)(2,1)S(1)}, bf16[128,256]{1,0:T(8,128)(2,1)S(1)}, u32[]{:S(2)}, u32[]{:S(2)}) collective-permute-start(bf16[128,256]{1,0:T(8,128)(2,1)S(1)} %get-tuple-element.233), channel_id=1, source_target_pairs={{0,11},{1,10},{2,9},{3,8},{4,15},{5,14},{6,13},{7,12},{8,3},{9,2},... | collective-permute-start | bytes 196616 | tf_op jit(solution)/shard_map/cond/branch_1_fun/ppermute | solution.py:33
  11.4 0.0 collective-permute-start.12
  11.4 0.0 collective-permute-done.9.refs_1_
  11.4 0.0 collective-permute-done.8.refs_0_
  11.4 2.6 %tile_work.30 = (f32[512,256]{1,0:T(8,128)S(1)}, bf16[128,256]{1,0:T(8,128)(2,1)S(1)}, bf16[128,256]{1,0:T(8,128)(2,1)S(1)}) custom-call(s32[1,560]{1,0:T(1,128)S(1)} %get-tuple-element.230.plan, f32[512,256]{1,0:T(8,128)} %get-tuple-element.231.src_ref.table_ref, f32[72,256]{1,0:T(8,128)S(1)} %get-tuple-element.232.row_ref, ...), custom_call_target="tpu_custom_call" | custom-call | flops 805306368 | bytes 524288 | tf_op jit(solution)/shard_map/cond/branch_1_fun/tile_work/pallas_call | solution.py:222
  14.0 1.2 %collective-permute-start.10 = (bf16[128,256]{1,0:T(8,128)(2,1)S(1)}, bf16[128,256]{1,0:T(8,128)(2,1)}, u32[]{:S(2)}, u32[]{:S(2)}) collective-permute-start(bf16[128,256]{1,0:T(8,128)(2,1)S(1)} %get-tuple-element.234), channel_id=1, source_target_pairs={{0,8},{1,9},{2,10},{3,11},{4,12},{5,13},{6,14},{7,15},{8,0},{9,1},... | collective-permute-start | bytes 196616 | tf_op jit(solution)/shard_map/cond/branch_1_fun/ppermute | solution.py:33
  15.2 2.3 %collective-permute-start.11 = (bf16[128,256]{1,0:T(8,128)(2,1)S(1)}, bf16[128,256]{1,0:T(8,128)(2,1)}, u32[]{:S(2)}, u32[]{:S(2)}) collective-permute-start(bf16[128,256]{1,0:T(8,128)(2,1)S(1)} %get-tuple-element.235), channel_id=1, source_target_pairs={{0,9},{1,8},{2,11},{3,10},{4,13},{5,12},{6,15},{7,14},{8,1},{9,0},... | collective-permute-start | bytes 196616 | tf_op jit(solution)/shard_map/cond/branch_1_fun/ppermute | solution.py:33
  17.5 0.0 collective-permute-done.13.refs_1_
  17.5 0.6 collective-permute-done.12.refs_0_
  18.1 0.0 copy-done.2
  18.1 1.5 %tile_work.31 = (f32[512,256]{1,0:T(8,128)S(1)}, bf16[128,256]{1,0:T(8,128)(2,1)S(1)}, bf16[128,256]{1,0:T(8,128)(2,1)S(1)}) custom-call(s32[1,560]{1,0:T(1,128)S(1)} %get-tuple-element.230.plan, f32[512,256]{1,0:T(8,128)S(1)} %copy-done.2, f32[72,256]{1,0:T(8,128)S(1)} %get-tuple-element.232.row_ref, ...), custom_call_target="tpu_custom_call", output_to_operand_aliasing={{0}: (5, {})} | custom-call | flops 805306368 | bytes 524288 | tf_op jit(solution)/shard_map/cond/branch_1_fun/tile_work/pallas_call | solution.py:222
  19.5 1.7 %collective-permute-start.14 = (bf16[128,256]{1,0:T(8,128)(2,1)S(1)}, bf16[128,256]{1,0:T(8,128)(2,1)}, u32[]{:S(2)}, u32[]{:S(2)}) collective-permute-start(bf16[128,256]{1,0:T(8,128)(2,1)S(1)} %get-tuple-element.237), channel_id=1, source_target_pairs={{0,10},{1,11},{2,8},{3,9},{4,14},{5,15},{6,12},{7,13},{8,2},{9,3},... | collective-permute-start | bytes 196616 | tf_op jit(solution)/shard_map/cond/branch_1_fun/ppermute | solution.py:33
  21.3 1.6 %collective-permute-start.15 = (bf16[128,256]{1,0:T(8,128)(2,1)S(1)}, bf16[128,256]{1,0:T(8,128)(2,1)}, u32[]{:S(2)}, u32[]{:S(2)}) collective-permute-start(bf16[128,256]{1,0:T(8,128)(2,1)S(1)} %get-tuple-element.238), channel_id=1, source_target_pairs={{0,11},{1,10},{2,9},{3,8},{4,15},{5,14},{6,13},{7,12},{8,3},{9,2},... | collective-permute-start | bytes 196616 | tf_op jit(solution)/shard_map/cond/branch_1_fun/ppermute | solution.py:33
  22.8 2.6 %later.8 = (s32[1,560]{1,0:T(1,128)S(1)}, s32[1,1]{1,0:T(1,128)}) custom-call(s32[1]{0:T(128)} %get-tuple-element.239.rep, s32[2,64]{1,0:T(2,128)} %get-tuple-element.240.refs_0_, s32[2,64]{1,0:T(2,128)} %get-tuple-element.241.refs_1_, s32[2]{0:T(128)} %get-tuple-element.242.refs_2_, s32[2,8]{1,0:T(2,128)} %get-tuple-element.243.refs_3_, ...), custom_call_target="tpu_custom_call" | custom-call | tf_op jit(solution)/shard_map/cond/branch_1_fun/later/pallas_call | solution.py:392
  25.5 2.0 %update_source.15 = (f32[512,256]{1,0:T(8,128)}, f32[4,128]{1,0:T(4,128)}) custom-call(f32[512,256]{1,0:T(8,128)S(1)} %copy-done.2, f32[4,128]{1,0:T(4,128)} %get-tuple-element.247.state_hbm, f32[512,256]{1,0:T(8,128)S(1)} %get-tuple-element.244.refs_4_.grad_ref), custom_call_target="tpu_custom_call" | custom-call | flops 1048576 | bytes 1048576 | tf_op jit(solution)/shard_map/cond/branch_1_fun/update_source/pallas_call | solution.py:275
  27.5 0.0 collective-permute-done.10
  27.5 0.0 collective-permute-done.11
  27.6 0.0 collective-permute-done.14
  27.6 0.8 %collective-permute-done.15 = bf16[128,256]{1,0:T(8,128)(2,1)} collective-permute-done((bf16[128,256]{1,0:T(8,128)(2,1)S(1)}, bf16[128,256]{1,0:T(8,128)(2,1)}, u32[]{:S(2)}, u32[]{:S(2)}) %collective-permute-start.15) | collective-permute-done | bytes 65568 | tf_op jit(solution)/shard_map/cond/branch_1_fun/ppermute | solution.py:33
  29.0 0.0 copy-done
  29.0 1.2 %update_target.2 = (f32[128,256]{1,0:T(8,128)S(1)}, f32[1,128]{1,0:T(1,128)S(1)}, bf16[128,256]{1,0:T(8,128)(2,1)S(1)}) custom-call(f32[128,256]{1,0:T(8,128)S(1)} %copy-done, f32[1,128]{1,0:T(1,128)} %bitcast.41, bf16[128,256]{1,0:T(8,128)(2,1)} %get-tuple-element.473.refs_1_, bf16[128,256]{1,0:T(8,128)(2,1)} %get-tuple-element.474.refs_2_, ...), custom_call_target="tpu_custom_call" | custom-call | flops 262144 | bytes 262144 | tf_op jit(solution)/shard_map/update_target/pallas_call | solution.py:315
  30.2 26.3 %conditional.3 = (bf16[128,256]{1,0:T(8,128)(2,1)}, bf16[128,256]{1,0:T(8,128)(2,1)}, bf16[128,256]{1,0:T(8,128)(2,1)}, bf16[128,256]{1,0:T(8,128)(2,1)}, f32[512,256]{1,0:T(8,128)}, /*index=5*/f32[4,128]{1,0:T(4,128)}) conditional(s32[]{:T(128)} %bitcast.6, (bf16[128,256]{1,0:T(8,128)(2,1)S(1)}, ...), branch_computations={%region_7.0_spmd, %region_8.0_spmd, %region_9.0_spmd, %region_10.0... | conditional | flops 1611661312 | bytes 6291852 | solution.py:48
  30.2 3.5 %collective-permute-start.81 = (bf16[128,256]{1,0:T(8,128)(2,1)S(1)}, bf16[128,256]{1,0:T(8,128)(2,1)S(1)}, u32[]{:S(2)}, u32[]{:S(2)}) collective-permute-start(bf16[128,256]{1,0:T(8,128)(2,1)S(1)} %get-tuple-element.392), channel_id=1, source_target_pairs={{0,17},{1,16},{2,19},{3,18},{4,21},{5,20},{6,23},{7,22},{8,25},{9,... | collective-permute-start | bytes 196616 | tf_op jit(solution)/shard_map/cond/branch_3_fun/ppermute | solution.py:33
  33.7 0.0 collective-permute-start.80
  33.7 5.0 %collective-permute-start.85 = (bf16[128,256]{1,0:T(8,128)(2,1)S(1)}, bf16[128,256]{1,0:T(8,128)(2,1)S(1)}, u32[]{:S(2)}, u32[]{:S(2)}) collective-permute-start(bf16[128,256]{1,0:T(8,128)(2,1)S(1)} %get-tuple-element.392), channel_id=1, source_target_pairs={{0,19},{1,18},{2,17},{3,16},{4,23},{5,22},{6,21},{7,20},{8,27},{9,... | collective-permute-start | bytes 196616 | tf_op jit(solution)/shard_map/cond/branch_3_fun/ppermute | solution.py:33
  38.7 0.0 collective-permute-start.84
  38.7 0.0 collective-permute-done.81.refs_1_
  38.7 0.0 collective-permute-done.80.refs_0_
  38.7 0.0 copy-start.11
  38.7 4.2 %tile_work.48 = (f32[512,256]{1,0:T(8,128)S(1)}, bf16[128,256]{1,0:T(8,128)(2,1)S(1)}, bf16[128,256]{1,0:T(8,128)(2,1)S(1)}) custom-call(s32[1,560]{1,0:T(1,128)S(1)} %get-tuple-element.389.plan, f32[512,256]{1,0:T(8,128)} %get-tuple-element.390.src_ref.table_ref, f32[72,256]{1,0:T(8,128)S(1)} %get-tuple-element.391.row_ref, ...), custom_call_target="tpu_custom_call" | custom-call | flops 805306368 | bytes 524288 | tf_op jit(solution)/shard_map/cond/branch_3_fun/tile_work/pallas_call | solution.py:222
  42.9 0.1 collective-permute-start.82
  43.0 1.4 %collective-permute-start.83 = (bf16[128,256]{1,0:T(8,128)(2,1)S(1)}, bf16[128,256]{1,0:T(8,128)(2,1)}, u32[]{:S(2)}, u32[]{:S(2)}) collective-permute-start(bf16[128,256]{1,0:T(8,128)(2,1)S(1)} %get-tuple-element.394), channel_id=1, source_target_pairs={{0,17},{1,16},{2,19},{3,18},{4,21},{5,20},{6,23},{7,22},{8,25},{9,... | collective-permute-start | bytes 196616 | tf_op jit(solution)/shard_map/cond/branch_3_fun/ppermute | solution.py:33
  44.3 0.0 collective-permute-done.85.refs_1_
  44.3 0.4 collective-permute-done.84.refs_0_
  44.8 3.1 %tile_work.49 = (f32[512,256]{1,0:T(8,128)S(1)}, bf16[128,256]{1,0:T(8,128)(2,1)S(1)}, bf16[128,256]{1,0:T(8,128)(2,1)S(1)}) custom-call(s32[1,560]{1,0:T(1,128)S(1)} %get-tuple-element.389.plan, f32[512,256]{1,0:T(8,128)S(1)} %copy-done.11, f32[72,256]{1,0:T(8,128)S(1)} %get-tuple-element.391.row_ref, ...), custom_call_target="tpu_custom_call", output_to_operand_aliasing={{0}: (5, {})} | custom-call | flops 805306368 | bytes 524288 | tf_op jit(solution)/shard_map/cond/branch_3_fun/tile_work/pallas_call | solution.py:222
  47.9 1.5 %collective-permute-start.86 = (bf16[128,256]{1,0:T(8,128)(2,1)S(1)}, bf16[128,256]{1,0:T(8,128)(2,1)}, u32[]{:S(2)}, u32[]{:S(2)}) collective-permute-start(bf16[128,256]{1,0:T(8,128)(2,1)S(1)} %get-tuple-element.396), channel_id=1, source_target_pairs={{0,18},{1,19},{2,16},{3,17},{4,22},{5,23},{6,20},{7,21},{8,26},{9,... | collective-permute-start | bytes 196616 | tf_op jit(solution)/shard_map/cond/branch_3_fun/ppermute | solution.py:33
  49.4 1.9 %collective-permute-start.87 = (bf16[128,256]{1,0:T(8,128)(2,1)S(1)}, bf16[128,256]{1,0:T(8,128)(2,1)}, u32[]{:S(2)}, u32[]{:S(2)}) collective-permute-start(bf16[128,256]{1,0:T(8,128)(2,1)S(1)} %get-tuple-element.397), channel_id=1, source_target_pairs={{0,19},{1,18},{2,17},{3,16},{4,23},{5,22},{6,21},{7,20},{8,27},{9,... | collective-permute-start | bytes 196616 | tf_op jit(solution)/shard_map/cond/branch_3_fun/ppermute | solution.py:33
  51.3 2.0 %update_source.24 = (f32[512,256]{1,0:T(8,128)}, f32[4,128]{1,0:T(4,128)}) custom-call(f32[512,256]{1,0:T(8,128)S(1)} %copy-done.11, f32[4,128]{1,0:T(4,128)} %get-tuple-element.398.state_hbm, f32[512,256]{1,0:T(8,128)S(1)} %get-tuple-element.399.grad_ref), custom_call_target="tpu_custom_call" | custom-call | flops 1048576 | bytes 1048576 | tf_op jit(solution)/shard_map/cond/branch_3_fun/update_source/pallas_call | solution.py:275
  53.3 0.0 collective-permute-done.82
  53.3 0.0 collective-permute-done.83
  53.3 1.7 %collective-permute-done.86 = bf16[128,256]{1,0:T(8,128)(2,1)} collective-permute-done((bf16[128,256]{1,0:T(8,128)(2,1)S(1)}, bf16[128,256]{1,0:T(8,128)(2,1)}, u32[]{:S(2)}, u32[]{:S(2)}) %collective-permute-start.86) | collective-permute-done | bytes 65568 | tf_op jit(solution)/shard_map/cond/branch_3_fun/ppermute | solution.py:33
  55.0 1.5 %collective-permute-done.87 = bf16[128,256]{1,0:T(8,128)(2,1)} collective-permute-done((bf16[128,256]{1,0:T(8,128)(2,1)S(1)}, bf16[128,256]{1,0:T(8,128)(2,1)}, u32[]{:S(2)}, u32[]{:S(2)}) %collective-permute-start.87) | collective-permute-done | bytes 65568 | tf_op jit(solution)/shard_map/cond/branch_3_fun/ppermute | solution.py:33
  56.5 1.8 %update_target.3 = (f32[128,256]{1,0:T(8,128)}, f32[1,128]{1,0:T(1,128)}) custom-call(f32[128,256]{1,0:T(8,128)S(1)} %get-tuple-element.483.table_ref, f32[1,128]{1,0:T(1,128)S(1)} %get-tuple-element.484.refs_0_, bf16[128,256]{1,0:T(8,128)(2,1)} %get-tuple-element.485.refs_1_, bf16[128,256]{1,0:T(8,128)(2,1)} %get-tuple-element.486.refs_2_, ...), custom_call_target="tpu_custom_call" | custom-call | flops 262144 | bytes 262144 | tf_op jit(solution)/shard_map/update_target/pallas_call | solution.py:315
  (2 shorter events, 0.0 us)
Async XLA Ops:
  3.1 25.9 %copy-start = (f32[128,256]{1,0:T(8,128)S(1)}, f32[128,256]{1,0:T(8,128)}, u32[]{:S(2)}) copy-start(f32[128,256]{1,0:T(8,128)} %table_ref.1) | copy-start | bytes 393220
  3.1 8.3 %collective-permute-start.9 = (bf16[128,256]{1,0:T(8,128)(2,1)S(1)}, bf16[128,256]{1,0:T(8,128)(2,1)S(1)}, u32[]{:S(2)}, u32[]{:S(2)}) collective-permute-start(bf16[128,256]{1,0:T(8,128)(2,1)S(1)} %get-tuple-element.233), channel_id=1, source_target_pairs={{0,9},{1,8},{2,11},{3,10},{4,13},{5,12},{6,15},{7,14},{8,1},{9,0},... | collective-permute-start | bytes 196616 | tf_op jit(solution)/shard_map/cond/branch_1_fun/ppermute | solution.py:33
  7.1 4.3 %collective-permute-start.8 = (bf16[128,256]{1,0:T(8,128)(2,1)S(1)}, bf16[128,256]{1,0:T(8,128)(2,1)S(1)}, u32[]{:S(2)}, u32[]{:S(2)}) collective-permute-start(bf16[128,256]{1,0:T(8,128)(2,1)S(1)} %get-tuple-element.233), channel_id=1, source_target_pairs={{0,8},{1,9},{2,10},{3,11},{4,12},{5,13},{6,14},{7,15},{8,0},{9,1},... | collective-permute-start | bytes 196616 | tf_op jit(solution)/shard_map/cond/branch_1_fun/ppermute | solution.py:33
  7.8 9.7 %collective-permute-start.13 = (bf16[128,256]{1,0:T(8,128)(2,1)S(1)}, bf16[128,256]{1,0:T(8,128)(2,1)S(1)}, u32[]{:S(2)}, u32[]{:S(2)}) collective-permute-start(bf16[128,256]{1,0:T(8,128)(2,1)S(1)} %get-tuple-element.233), channel_id=1, source_target_pairs={{0,11},{1,10},{2,9},{3,8},{4,15},{5,14},{6,13},{7,12},{8,3},{9,2},... | collective-permute-start | bytes 196616 | tf_op jit(solution)/shard_map/cond/branch_1_fun/ppermute | solution.py:33
  11.4 6.7 %collective-permute-start.12 = (bf16[128,256]{1,0:T(8,128)(2,1)S(1)}, bf16[128,256]{1,0:T(8,128)(2,1)S(1)}, u32[]{:S(2)}, u32[]{:S(2)}) collective-permute-start(bf16[128,256]{1,0:T(8,128)(2,1)S(1)} %get-tuple-element.233), channel_id=1, source_target_pairs={{0,10},{1,11},{2,8},{3,9},{4,14},{5,15},{6,12},{7,13},{8,2},{9,3},... | collective-permute-start | bytes 196616 | tf_op jit(solution)/shard_map/cond/branch_1_fun/ppermute | solution.py:33
  11.4 6.7 %copy-start.2 = (f32[512,256]{1,0:T(8,128)S(1)}, f32[512,256]{1,0:T(8,128)}, u32[]{:S(2)}) copy-start(f32[512,256]{1,0:T(8,128)} %get-tuple-element.231.src_ref.table_ref) | copy-start | bytes 1572868 | tf_op jit(solution)/shard_map/cond
  14.0 13.5 %collective-permute-start.10 = (bf16[128,256]{1,0:T(8,128)(2,1)S(1)}, bf16[128,256]{1,0:T(8,128)(2,1)}, u32[]{:S(2)}, u32[]{:S(2)}) collective-permute-start(bf16[128,256]{1,0:T(8,128)(2,1)S(1)} %get-tuple-element.234), channel_id=1, source_target_pairs={{0,8},{1,9},{2,10},{3,11},{4,12},{5,13},{6,14},{7,15},{8,0},{9,1},... | collective-permute-start | bytes 196616 | tf_op jit(solution)/shard_map/cond/branch_1_fun/ppermute | solution.py:33
  15.2 12.4 %collective-permute-start.11 = (bf16[128,256]{1,0:T(8,128)(2,1)S(1)}, bf16[128,256]{1,0:T(8,128)(2,1)}, u32[]{:S(2)}, u32[]{:S(2)}) collective-permute-start(bf16[128,256]{1,0:T(8,128)(2,1)S(1)} %get-tuple-element.235), channel_id=1, source_target_pairs={{0,9},{1,8},{2,11},{3,10},{4,13},{5,12},{6,15},{7,14},{8,1},{9,0},... | collective-permute-start | bytes 196616 | tf_op jit(solution)/shard_map/cond/branch_1_fun/ppermute | solution.py:33
  19.5 8.0 %collective-permute-start.14 = (bf16[128,256]{1,0:T(8,128)(2,1)S(1)}, bf16[128,256]{1,0:T(8,128)(2,1)}, u32[]{:S(2)}, u32[]{:S(2)}) collective-permute-start(bf16[128,256]{1,0:T(8,128)(2,1)S(1)} %get-tuple-element.237), channel_id=1, source_target_pairs={{0,10},{1,11},{2,8},{3,9},{4,14},{5,15},{6,12},{7,13},{8,2},{9,3},... | collective-permute-start | bytes 196616 | tf_op jit(solution)/shard_map/cond/branch_1_fun/ppermute | solution.py:33
  21.3 7.1 %collective-permute-start.15 = (bf16[128,256]{1,0:T(8,128)(2,1)S(1)}, bf16[128,256]{1,0:T(8,128)(2,1)}, u32[]{:S(2)}, u32[]{:S(2)}) collective-permute-start(bf16[128,256]{1,0:T(8,128)(2,1)S(1)} %get-tuple-element.238), channel_id=1, source_target_pairs={{0,11},{1,10},{2,9},{3,8},{4,15},{5,14},{6,13},{7,12},{8,3},{9,2},... | collective-permute-start | bytes 196616 | tf_op jit(solution)/shard_map/cond/branch_1_fun/ppermute | solution.py:33
  30.2 8.5 %collective-permute-start.81 = (bf16[128,256]{1,0:T(8,128)(2,1)S(1)}, bf16[128,256]{1,0:T(8,128)(2,1)S(1)}, u32[]{:S(2)}, u32[]{:S(2)}) collective-permute-start(bf16[128,256]{1,0:T(8,128)(2,1)S(1)} %get-tuple-element.392), channel_id=1, source_target_pairs={{0,17},{1,16},{2,19},{3,18},{4,21},{5,20},{6,23},{7,22},{8,25},{9,... | collective-permute-start | bytes 196616 | tf_op jit(solution)/shard_map/cond/branch_3_fun/ppermute | solution.py:33
  33.7 5.0 %collective-permute-start.80 = (bf16[128,256]{1,0:T(8,128)(2,1)S(1)}, bf16[128,256]{1,0:T(8,128)(2,1)S(1)}, u32[]{:S(2)}, u32[]{:S(2)}) collective-permute-start(bf16[128,256]{1,0:T(8,128)(2,1)S(1)} %get-tuple-element.392), channel_id=1, source_target_pairs={{0,16},{1,17},{2,18},{3,19},{4,20},{5,21},{6,22},{7,23},{8,24},{9,... | collective-permute-start | bytes 196616 | tf_op jit(solution)/shard_map/cond/branch_3_fun/ppermute | solution.py:33
  33.7 10.7 %collective-permute-start.85 = (bf16[128,256]{1,0:T(8,128)(2,1)S(1)}, bf16[128,256]{1,0:T(8,128)(2,1)S(1)}, u32[]{:S(2)}, u32[]{:S(2)}) collective-permute-start(bf16[128,256]{1,0:T(8,128)(2,1)S(1)} %get-tuple-element.392), channel_id=1, source_target_pairs={{0,19},{1,18},{2,17},{3,16},{4,23},{5,22},{6,21},{7,20},{8,27},{9,... | collective-permute-start | bytes 196616 | tf_op jit(solution)/shard_map/cond/branch_3_fun/ppermute | solution.py:33
  38.7 6.1 %collective-permute-start.84 = (bf16[128,256]{1,0:T(8,128)(2,1)S(1)}, bf16[128,256]{1,0:T(8,128)(2,1)S(1)}, u32[]{:S(2)}, u32[]{:S(2)}) collective-permute-start(bf16[128,256]{1,0:T(8,128)(2,1)S(1)} %get-tuple-element.392), channel_id=1, source_target_pairs={{0,18},{1,19},{2,16},{3,17},{4,22},{5,23},{6,20},{7,21},{8,26},{9,... | collective-permute-start | bytes 196616 | tf_op jit(solution)/shard_map/cond/branch_3_fun/ppermute | solution.py:33
  38.7 6.1 %copy-start.11 = (f32[512,256]{1,0:T(8,128)S(1)}, f32[512,256]{1,0:T(8,128)}, u32[]{:S(2)}) copy-start(f32[512,256]{1,0:T(8,128)} %get-tuple-element.390.src_ref.table_ref) | copy-start | bytes 1572868 | tf_op jit(solution)/shard_map/cond
  42.9 10.4 %collective-permute-start.82 = (bf16[128,256]{1,0:T(8,128)(2,1)S(1)}, bf16[128,256]{1,0:T(8,128)(2,1)}, u32[]{:S(2)}, u32[]{:S(2)}) collective-permute-start(bf16[128,256]{1,0:T(8,128)(2,1)S(1)} %get-tuple-element.393), channel_id=1, source_target_pairs={{0,16},{1,17},{2,18},{3,19},{4,20},{5,21},{6,22},{7,23},{8,24},{9,... | collective-permute-start | bytes 196616 | tf_op jit(solution)/shard_map/cond/branch_3_fun/ppermute | solution.py:33
  43.0 10.3 %collective-permute-start.83 = (bf16[128,256]{1,0:T(8,128)(2,1)S(1)}, bf16[128,256]{1,0:T(8,128)(2,1)}, u32[]{:S(2)}, u32[]{:S(2)}) collective-permute-start(bf16[128,256]{1,0:T(8,128)(2,1)S(1)} %get-tuple-element.394), channel_id=1, source_target_pairs={{0,17},{1,16},{2,19},{3,18},{4,21},{5,20},{6,23},{7,22},{8,25},{9,... | collective-permute-start | bytes 196616 | tf_op jit(solution)/shard_map/cond/branch_3_fun/ppermute | solution.py:33
  47.9 7.1 %collective-permute-start.86 = (bf16[128,256]{1,0:T(8,128)(2,1)S(1)}, bf16[128,256]{1,0:T(8,128)(2,1)}, u32[]{:S(2)}, u32[]{:S(2)}) collective-permute-start(bf16[128,256]{1,0:T(8,128)(2,1)S(1)} %get-tuple-element.396), channel_id=1, source_target_pairs={{0,18},{1,19},{2,16},{3,17},{4,22},{5,23},{6,20},{7,21},{8,26},{9,... | collective-permute-start | bytes 196616 | tf_op jit(solution)/shard_map/cond/branch_3_fun/ppermute | solution.py:33
  49.4 7.1 %collective-permute-start.87 = (bf16[128,256]{1,0:T(8,128)(2,1)S(1)}, bf16[128,256]{1,0:T(8,128)(2,1)}, u32[]{:S(2)}, u32[]{:S(2)}) collective-permute-start(bf16[128,256]{1,0:T(8,128)(2,1)S(1)} %get-tuple-element.397), channel_id=1, source_target_pairs={{0,19},{1,18},{2,17},{3,16},{4,23},{5,22},{6,21},{7,20},{8,27},{9,... | collective-permute-start | bytes 196616 | tf_op jit(solution)/shard_map/cond/branch_3_fun/ppermute | solution.py:33

commit v4 on v3

--- a/solution.py
+++ b/solution.py
@@ -67,18 +67,25 @@
     bits = number.bit_length() - 1
     first, second, start, room, _ = layout(number, tiles.shape[1])
 
-    def place(t, ends):
-        code = tiles[k, t]
-        e = jnp.bitwise_xor(jnp.bitwise_and(code, number - 1), flip)
-        p = ends[0]
-        for i in range(1, number):
-            p = jnp.where(e == i, ends[i], p)
-        plan[0, start + e * room + p] = jnp.bitwise_or(
-            jnp.left_shift(jnp.right_shift(code, bits), SHIFT), rel[k, t]
-        )
-        return tuple(ends[i] + jnp.where(e == i, 1, 0) for i in range(number))
-
-    ends = lax.fori_loop(0, counts[k], place, (jnp.int32(0),) * number)
+    live, slots = counts[k], tiles.shape[1]
+    some = next(n for n in (4, 2, 1) if slots % n == 0)
+
+    def place(q, ends):
+        for u in range(some):
+            t = q * some + u
+            code = tiles[k, t]
+            e = jnp.bitwise_xor(jnp.bitwise_and(code, number - 1), flip)
+            p = ends[0]
+            for i in range(1, number):
+                p = jnp.where(e == i, ends[i], p)
+            plan[0, start + e * room + p] = jnp.bitwise_or(
+                jnp.left_shift(jnp.right_shift(code, bits), SHIFT), rel[k, t]
+            )
+            e = jnp.where(t < live, e, number)
+            ends = tuple(ends[i] + jnp.where(e == i, 1, 0) for i in range(number))
+        return ends
+
+    ends = lax.fori_loop(0, (live + (some - 1)) // some, place, (jnp.int32(0),) * number)
     for i in range(number):
         for extra in range(2 * GROUP):
             plan[0, start + i * room + ends[i] + extra] = jnp.int32(none_rel)
@@ -138,7 +145,8 @@
 def tile_kernel(index, lists, cut, shards, carried, plan, src_ref, row_ref, *refs):
     dst_refs, refs = refs[:shards], refs[shards + carried :]
     src_grad, parts, refs = refs[0], refs[1 : 1 + shards], refs[1 + shards :]
-    low_ref, dst_all, dst_grad, held_rows, held_slope = refs
+    *low_out, dst_all, dst_grad, held_rows, held_slope = refs
+    (low_ref,) = low_out or (src_ref,)
     _, _, start, room, _ = lists
     at_list = lists[index]
     rows_of_shard = dst_refs[0].shape[0]
@@ -147,11 +155,11 @@
     def begin(i, carry):
         rows = pl.ds(pl.multiple_of(i * TILE, TILE), TILE)
         low_ref[rows, :] = src_ref[rows, :].astype(jnp.bfloat16).astype(jnp.float32)
-        if not carried:
-            src_grad[rows, :] = jnp.zeros((TILE, src_grad.shape[1]), jnp.float32)
+        src_grad[rows, :] = jnp.zeros((TILE, src_grad.shape[1]), jnp.float32)
         return carry
 
-    lax.fori_loop(0, src_ref.shape[0] // TILE, begin, 0)
+    if not carried:
+        lax.fori_loop(0, src_ref.shape[0] // TILE, begin, 0)
     for i in range(shards):
         dst_all[pl.ds(i * rows_of_shard, rows_of_shard), :] = dst_refs[i][...]
     dst_grad[...] = jnp.zeros_like(dst_grad)
@@ -222,11 +230,11 @@
     out = pl.pallas_call(
         functools.partial(tile_kernel, index, lists, cut, len(shards), len(carried)),
         in_specs=[SMEM] + [VMEM] * (2 + len(shards) + len(carried)),
-        out_specs=[VMEM] * (1 + len(shards)),
+        out_specs=[VMEM] * (1 + len(shards) + (not carried)),
         out_shape=[jax.ShapeDtypeStruct(src_table.shape, jnp.float32)]
-        + [jax.ShapeDtypeStruct((rows, width), jnp.bfloat16)] * len(shards),
+        + [jax.ShapeDtypeStruct((rows, width), jnp.bfloat16)] * len(shards)
+        + [jax.ShapeDtypeStruct(src_table.shape, jnp.float32)] * (not carried),
         scratch_shapes=[
-            pltpu.VMEM(src_table.shape, jnp.float32),
             pltpu.VMEM((len(shards) * rows, width), jnp.bfloat16),
             pltpu.VMEM((len(shards) * rows, width), jnp.float32),
             pltpu.VMEM((2, GROUP * TILE, width), jnp.bfloat16),
@@ -241,7 +249,7 @@
         compiler_params=GRANT,
         name="tile_work",
     )(plan, src_table, rel_rows, *shards, *carried)
-    return out[0], list(out[1:])
+    return out[0], list(out[1 : 1 + len(shards)]), out[-1]
 
 
 def adagrad_block(table, state, grad):
@@ -291,11 +299,14 @@
     )(table, *in_hbm(state), grad)
 
 
-def target_kernel(parts, last, table_ref, *refs):
+def target_kernel(parts, last, inside, table_ref, *refs):
     sources, outs = refs[: parts + 1], refs[parts + 1 : parts + 3 + (not last)]
-    *held, sem = refs[parts + 3 + (not last) :]
-    for copy in fetch(sources, held, sem):
-        copy.wait()
+    if inside:
+        held = sources
+    else:
+        *held, sem = refs[parts + 3 + (not last) :]
+        for copy in fetch(sources, held, sem):
+            copy.wait()
     for i in range(table_ref.shape[0] // TILE):
         rows = pl.ds(i * TILE, TILE)
         grad = held[1][rows, :].astype(jnp.float32)
@@ -310,13 +321,15 @@
             outs[2][rows, :] = table.astype(jnp.bfloat16)
 
 
-def update_target(table, state, parts, first, last):
+def update_target(table, state, parts, first, last, inside):
     low = [] if last else [jax.ShapeDtypeStruct(table.shape, jnp.bfloat16)]
     return pl.pallas_call(
-        functools.partial(target_kernel, len(parts), last),
-        in_specs=[VMEM] + [HBM] * (1 + len(parts)),
+        functools.partial(target_kernel, len(parts), last, inside),
+        in_specs=[VMEM] + [VMEM if inside else HBM] * (1 + len(parts)),
         out_specs=[VMEM] * (2 + len(low)),
-        scratch_shapes=[pltpu.VMEM(state.shape, jnp.float32)]
+        scratch_shapes=[]
+        if inside
+        else [pltpu.VMEM(state.shape, jnp.float32)]
         + [pltpu.VMEM(part.shape, part.dtype) for part in parts]
         + [pltpu.SemaphoreType.DMA((1 + len(parts),))],
         out_shape=[
@@ -329,7 +342,7 @@
         ),
         compiler_params=GRANT,
         name="update_target",
-    )(table, *(in_hbm(state) if first else [state]), *parts)
+    )(table, *(in_hbm(state) if first and not inside else [state]), *parts)
 
 
 def per_device(
@@ -374,17 +387,17 @@
     )(scalars[0], *in_hbm(*scalars[1:], dst_table, rel_table))
 
     def branch(value, operands, k):
-        rows, plan, rel_rows, src_table, src_state, scalars = operands
+        rows, plan, rel_rows, src_table, src_state, scalars, target = operands
         shards = []
         for j in range(reps):
             shards.append(send(rows, value, j))
-        src_grad, parts = tile_work(
-            0, lists, cut, slots // 2, plan, src_table, rel_rows, shards[:near], None
-        )
+        src_grad, parts, low = tile_work(0, lists, cut, slots // 2, plan, src_table, rel_rows, shards[:near], None)
         back = []
         for j in range(near):
             back.append(send(parts[j], value, j))
-        src_grad, parts = tile_work(1, lists, cut, slots // 2, plan, src_table, rel_rows, shards[near:], src_grad)
+        src_grad, parts, _ = tile_work(
+            1, lists, cut, slots // 2, plan, low, rel_rows, shards[near:], src_grad
+        )
         for j in range(near, reps):
             back.append(send(parts[j - near], value, j))
         following = ()
@@ -399,22 +412,31 @@
                 name="later",
             )(scalars[0], *in_hbm(*scalars[1:]), src_grad)
         src_table, src_state = update_source(src_table, src_state, src_grad)
+        if target:
+            back = update_target(*target, back, k == 0, True, True)
         return tuple(back), tuple(following), src_table, src_state
 
     for k in range(rounds):
         round_mask = mask.reshape(())
+        inside = k + 1 == rounds and not high_chunks
         back, following, src_table, src_state = by_mask(
             round_mask,
             low_chunk,
             functools.partial(branch, k=k),
-            (send_high(rows, round_mask), plan, rel_rows, src_table, src_state, scalars),
+            (
+                send_high(rows, round_mask), plan, rel_rows, src_table, src_state, scalars,
+                (dst_table, dst_state) if inside else (),
+            ),
         )
         plan, mask = following or (None, None)
+        if inside:
+            dst_table, dst_state = back
+            break
         if high_chunks:
             total = functools.reduce(jnp.add, [x.astype(jnp.float32) for x in back])
             back = [send_high(total.astype(jnp.bfloat16), round_mask)]
         dst_table, dst_state, *rows = update_target(
-            dst_table, dst_state, back, k == 0, k + 1 == rounds
+            dst_table, dst_state, back, k == 0, k + 1 == rounds, False
         )
         rows = rows[0] if rows else None
     return (src_table, src_state.reshape(-1), dst_table, dst_state.reshape(-1))

time: 58.8 us -> 57 us (0.969)
  Pallas kernels: 22.8 us -> 21.3 us
  starting transfers between devices: 28.3 us -> 27 us
  waiting for transfers between devices: 4.96 us -> 6.08 us
    ppermute x16, starting transfers between devices: 28.3 us -> 27 us  [send(): return lax.ppermute(rows, AXES, pairs)]
    ppermute x16, waiting for transfers between devices: 4.96 us -> 6.08 us  [send(): return lax.ppermute(rows, AXES, pairs)]
    pallas_call x2, Pallas kernels: 2.94 us -> 1.96 us  [update_target(): pl.pallas_call(functools.partial(target_kernel, len(parts), last, inside)...]
  transfers between devices with their start and end apart: 16 -> 16, of which waited for: 5 -> 6; matrix products, arithmetic and copies ran while one was open for 0% -> 0% of each run, Pallas kernels for 31% -> 31%
where the time goes in v4:
time: 57 us; the launch traced here: 56.6 us
  starting transfers between devices  27 us (47%)
  Pallas kernels  21.3 us (37%)
  waiting for transfers between devices  6.08 us (11%)
  between operations  1.97 us (3%)
    ppermute x16, starting transfers between devices, send(): return lax.ppermute(rows, AXES, pairs)  27 us
    pallas_call x4, Pallas kernels, tile_work(): pl.pallas_call(functools.partial(tile_kernel, index, lists, cut, len(shar...  11.1 us
    ppermute x16, waiting for transfers between devices, send(): return lax.ppermute(rows, AXES, pairs)  6.08 us
    pallas_call x2, Pallas kernels, update_source(): pl.pallas_call(source_kernel, in_specs=[VMEM, HBM, VMEM], out_specs=[HBM]...  4.04 us
    pallas_call x1, Pallas kernels, branch(): pl.pallas_call(functools.partial(later_kernel, k + 1, shard_blocks, numbe...  2.37 us
    pallas_call x2, Pallas kernels, update_target(): pl.pallas_call(functools.partial(target_kernel, len(parts), last, inside)...  1.96 us
    pallas_call x1, Pallas kernels, per_device(): pl.pallas_call(functools.partial(first_kernel, number, cut, none_rel), in...  1.8 us
  transfers between devices with their start and end apart: 16, of which 6 were waited for; matrix products, arithmetic and copies ran while one was open for 0% of the time, Pallas kernels for 31%

profile of v4, /device:TPU:0, one launch (start us, length us, event | category | flops | bytes accessed | tf_op | source)
XLA Modules:
  0.0 56.6 jit_solution(13837643099850186235)
XLA Ops:
  0.6 1.8 %first.1 = (s32[1,560]{1,0:T(1,128)S(1)}, bf16[128,256]{1,0:T(8,128)(2,1)S(1)}, f32[72,256]{1,0:T(8,128)S(1)}, s32[1,1]{1,0:T(1,128)}) custom-call(s32[1]{0:T(128)} %bitcast.rep, s32[2,64]{1,0:T(2,128)} %bitcast.17, s32[2,64]{1,0:T(2,128)} %bitcast.25, s32[2]{0:T(128)} %bitcast.33, s32[2,8]{1,0:T(2,128)} %refs_3_.1, f32[128,256]{1,0:T(8,128)} %table_ref.1, ...), custom_call_target="tpu_custom_call" | custom-call | tf_op jit(solution)/shard_map/first/pallas_call | solution.py:369
  3.1 0.0 copy-start
  3.1 25.3 %conditional.2 = (bf16[128,256]{1,0:T(8,128)(2,1)}, bf16[128,256]{1,0:T(8,128)(2,1)}, bf16[128,256]{1,0:T(8,128)(2,1)}, bf16[128,256]{1,0:T(8,128)(2,1)}, s32[1,...) conditional(s32[]{:T(128)} %bitcast.4, ...), branch_computations={%region_0.0_spmd, %region_1.0_spmd, %region_2.0_spmd, %region_3.0_... | conditional | flops 1611661312 | bytes 6291868 | solution.py:48
  3.1 4.0 %collective-permute-start.9 = (bf16[128,256]{1,0:T(8,128)(2,1)S(1)}, bf16[128,256]{1,0:T(8,128)(2,1)S(1)}, u32[]{:S(2)}, u32[]{:S(2)}) collective-permute-start(bf16[128,256]{1,0:T(8,128)(2,1)S(1)} %get-tuple-element.262), channel_id=1, source_target_pairs={{0,9},{1,8},{2,11},{3,10},{4,13},{5,12},{6,15},{7,14},{8,1},{9,0},... | collective-permute-start | bytes 196616 | tf_op jit(solution)/shard_map/cond/branch_1_fun/ppermute | solution.py:33
  7.1 0.6 %collective-permute-start.8 = (bf16[128,256]{1,0:T(8,128)(2,1)S(1)}, bf16[128,256]{1,0:T(8,128)(2,1)S(1)}, u32[]{:S(2)}, u32[]{:S(2)}) collective-permute-start(bf16[128,256]{1,0:T(8,128)(2,1)S(1)} %get-tuple-element.262), channel_id=1, source_target_pairs={{0,8},{1,9},{2,10},{3,11},{4,12},{5,13},{6,14},{7,15},{8,0},{9,1},... | collective-permute-start | bytes 196616 | tf_op jit(solution)/shard_map/cond/branch_1_fun/ppermute | solution.py:33
  7.8 3.5 %collective-permute-start.13 = (bf16[128,256]{1,0:T(8,128)(2,1)S(1)}, bf16[128,256]{1,0:T(8,128)(2,1)S(1)}, u32[]{:S(2)}, u32[]{:S(2)}) collective-permute-start(bf16[128,256]{1,0:T(8,128)(2,1)S(1)} %get-tuple-element.262), channel_id=1, source_target_pairs={{0,11},{1,10},{2,9},{3,8},{4,15},{5,14},{6,13},{7,12},{8,3},{9,2},... | collective-permute-start | bytes 196616 | tf_op jit(solution)/shard_map/cond/branch_1_fun/ppermute | solution.py:33
  11.3 0.0 collective-permute-start.12
  11.3 0.0 collective-permute-done.9.refs_1_
  11.3 0.1 collective-permute-done.8.refs_0_
  11.4 2.5 %tile_work.30 = (f32[512,256]{1,0:T(8,128)S(1)}, bf16[128,256]{1,0:T(8,128)(2,1)S(1)}, bf16[128,256]{1,0:T(8,128)(2,1)S(1)}, f32[512,256]{1,0:T(8,128)S(1)}) custom-call(s32[1,560]{1,0:T(1,128)S(1)} %get-tuple-element.259.plan, f32[512,256]{1,0:T(8,128)} %get-tuple-element.260.src_ref.table_ref, f32[72,256]{1,0:T(8,128)S(1)} %get-tuple-element.261.row_ref, ...), custom_call_target="tpu_custom_call" | custom-call | flops 805306368 | bytes 524288 | tf_op jit(solution)/shard_map/cond/branch_1_fun/tile_work/pallas_call | solution.py:230
  13.9 1.1 %collective-permute-start.10 = (bf16[128,256]{1,0:T(8,128)(2,1)S(1)}, bf16[128,256]{1,0:T(8,128)(2,1)}, u32[]{:S(2)}, u32[]{:S(2)}) collective-permute-start(bf16[128,256]{1,0:T(8,128)(2,1)S(1)} %get-tuple-element.263), channel_id=1, source_target_pairs={{0,8},{1,9},{2,10},{3,11},{4,12},{5,13},{6,14},{7,15},{8,0},{9,1},... | collective-permute-start | bytes 196616 | tf_op jit(solution)/shard_map/cond/branch_1_fun/ppermute | solution.py:33
  15.0 2.3 %collective-permute-start.11 = (bf16[128,256]{1,0:T(8,128)(2,1)S(1)}, bf16[128,256]{1,0:T(8,128)(2,1)}, u32[]{:S(2)}, u32[]{:S(2)}) collective-permute-start(bf16[128,256]{1,0:T(8,128)(2,1)S(1)} %get-tuple-element.264), channel_id=1, source_target_pairs={{0,9},{1,8},{2,11},{3,10},{4,13},{5,12},{6,15},{7,14},{8,1},{9,0},... | collective-permute-start | bytes 196616 | tf_op jit(solution)/shard_map/cond/branch_1_fun/ppermute | solution.py:33
  17.3 0.0 collective-permute-done.13.refs_1_
  17.3 0.7 %collective-permute-done.12.refs_0_ = bf16[128,256]{1,0:T(8,128)(2,1)S(1)} collective-permute-done((bf16[128,256]{1,0:T(8,128)(2,1)S(1)}, bf16[128,256]{1,0:T(8,128)(2,1)S(1)}, u32[]{:S(2)}, u32[]{:S(2)}) %collective-permute-start.12) | collective-permute-done | bytes 65568 | tf_op jit(solution)/shard_map/cond/branch_1_fun/ppermute | solution.py:33
  18.0 1.4 %tile_work.31 = (f32[512,256]{1,0:T(8,128)S(1)}, bf16[128,256]{1,0:T(8,128)(2,1)S(1)}, bf16[128,256]{1,0:T(8,128)(2,1)S(1)}) custom-call(s32[1,560]{1,0:T(1,128)S(1)} %get-tuple-element.259.plan, f32[512,256]{1,0:T(8,128)S(1)} %get-tuple-element.265.src_ref, f32[72,256]{1,0:T(8,128)S(1)} %get-tuple-element.261.row_ref, ...), custom_call_target="tpu_custom_call", output_to_operand_aliasing={{0}: (5, {})} | custom-call | flops 805306368 | bytes 524288 | tf_op jit(solution)/shard_map/cond/branch_1_fun/tile_work/pallas_call | solution.py:230
  19.5 0.0 copy-start.2
  19.5 1.7 %collective-permute-start.14 = (bf16[128,256]{1,0:T(8,128)(2,1)S(1)}, bf16[128,256]{1,0:T(8,128)(2,1)}, u32[]{:S(2)}, u32[]{:S(2)}) collective-permute-start(bf16[128,256]{1,0:T(8,128)(2,1)S(1)} %get-tuple-element.267), channel_id=1, source_target_pairs={{0,10},{1,11},{2,8},{3,9},{4,14},{5,15},{6,12},{7,13},{8,2},{9,3},... | collective-permute-start | bytes 196616 | tf_op jit(solution)/shard_map/cond/branch_1_fun/ppermute | solution.py:33
  21.1 1.5 %collective-permute-start.15 = (bf16[128,256]{1,0:T(8,128)(2,1)S(1)}, bf16[128,256]{1,0:T(8,128)(2,1)}, u32[]{:S(2)}, u32[]{:S(2)}) collective-permute-start(bf16[128,256]{1,0:T(8,128)(2,1)S(1)} %get-tuple-element.268), channel_id=1, source_target_pairs={{0,11},{1,10},{2,9},{3,8},{4,15},{5,14},{6,13},{7,12},{8,3},{9,2},... | collective-permute-start | bytes 196616 | tf_op jit(solution)/shard_map/cond/branch_1_fun/ppermute | solution.py:33
  22.6 2.4 %later.8 = (s32[1,560]{1,0:T(1,128)S(1)}, s32[1,1]{1,0:T(1,128)}) custom-call(s32[1]{0:T(128)} %get-tuple-element.269.rep, s32[2,64]{1,0:T(2,128)} %get-tuple-element.270.refs_0_, s32[2,64]{1,0:T(2,128)} %get-tuple-element.271.refs_1_, s32[2]{0:T(128)} %get-tuple-element.272.refs_2_, s32[2,8]{1,0:T(2,128)} %get-tuple-element.273.refs_3_, ...), custom_call_target="tpu_custom_call" | custom-call | tf_op jit(solution)/shard_map/cond/branch_1_fun/later/pallas_call | solution.py:405
  25.0 0.0 copy-done.2
  25.0 2.0 %update_source.15 = (f32[512,256]{1,0:T(8,128)}, f32[4,128]{1,0:T(4,128)}) custom-call(f32[512,256]{1,0:T(8,128)S(1)} %copy-done.2, f32[4,128]{1,0:T(4,128)} %get-tuple-element.277.state_hbm, f32[512,256]{1,0:T(8,128)S(1)} %get-tuple-element.274.refs_4_.grad_ref), custom_call_target="tpu_custom_call" | custom-call | flops 1048576 | bytes 1048576 | tf_op jit(solution)/shard_map/cond/branch_1_fun/update_source/pallas_call | solution.py:283
  27.0 0.0 collective-permute-done.10
  27.1 0.0 collective-permute-done.11
  27.1 0.0 collective-permute-done.14
  27.1 1.3 %collective-permute-done.15 = bf16[128,256]{1,0:T(8,128)(2,1)} collective-permute-done((bf16[128,256]{1,0:T(8,128)(2,1)S(1)}, bf16[128,256]{1,0:T(8,128)(2,1)}, u32[]{:S(2)}, u32[]{:S(2)}) %collective-permute-start.15) | collective-permute-done | bytes 65568 | tf_op jit(solution)/shard_map/cond/branch_1_fun/ppermute | solution.py:33
  29.0 0.0 copy-done
  29.1 1.2 %update_target.15 = (f32[128,256]{1,0:T(8,128)S(1)}, f32[1,128]{1,0:T(1,128)S(1)}, bf16[128,256]{1,0:T(8,128)(2,1)S(1)}) custom-call(f32[128,256]{1,0:T(8,128)S(1)} %copy-done, f32[1,128]{1,0:T(1,128)} %bitcast.41, bf16[128,256]{1,0:T(8,128)(2,1)} %get-tuple-element.539.refs_1_, bf16[128,256]{1,0:T(8,128)(2,1)} %get-tuple-element.540.refs_2_, ...), custom_call_target="tpu_custom_call" | custom-call | flops 262144 | bytes 262144 | tf_op jit(solution)/shard_map/update_target/pallas_call | solution.py:326
  30.2 26.4 %conditional.3 = (f32[128,256]{1,0:T(8,128)}, f32[1,128]{1,0:T(1,128)}, f32[512,256]{1,0:T(8,128)}, f32[4,128]{1,0:T(4,128)}) conditional(s32[]{:T(128)} %bitcast.6, (bf16[128,256]{1,0:T(8,128)(2,1)S(1)}, s32[1,560]{1,0:T(1,128)S(1)}, f32[512,256]{1,0:T(8,128)}, f32[72,256]{1,0:T(8,128)S(1)}, ...), branch_computations={%region_7.0_spmd, %region_8.0_spmd, %region_9.0_spmd, %region_10.0... | conditional | flops 1611923456 | bytes 6553980 | solution.py:48
  30.2 3.4 %collective-permute-start.81 = (bf16[128,256]{1,0:T(8,128)(2,1)S(1)}, bf16[128,256]{1,0:T(8,128)(2,1)S(1)}, u32[]{:S(2)}, u32[]{:S(2)}) collective-permute-start(bf16[128,256]{1,0:T(8,128)(2,1)S(1)} %get-tuple-element.444), channel_id=1, source_target_pairs={{0,17},{1,16},{2,19},{3,18},{4,21},{5,20},{6,23},{7,22},{8,25},{9,... | collective-permute-start | bytes 196616 | tf_op jit(solution)/shard_map/cond/branch_3_fun/ppermute | solution.py:33
  33.6 0.0 collective-permute-start.80
  33.6 4.6 %collective-permute-start.85 = (bf16[128,256]{1,0:T(8,128)(2,1)S(1)}, bf16[128,256]{1,0:T(8,128)(2,1)S(1)}, u32[]{:S(2)}, u32[]{:S(2)}) collective-permute-start(bf16[128,256]{1,0:T(8,128)(2,1)S(1)} %get-tuple-element.444), channel_id=1, source_target_pairs={{0,19},{1,18},{2,17},{3,16},{4,23},{5,22},{6,21},{7,20},{8,27},{9,... | collective-permute-start | bytes 196616 | tf_op jit(solution)/shard_map/cond/branch_3_fun/ppermute | solution.py:33
  38.2 0.0 collective-permute-start.84
  38.2 0.0 collective-permute-done.81.refs_1_
  38.2 0.0 collective-permute-done.80.refs_0_
  38.2 4.2 %tile_work.48 = (f32[512,256]{1,0:T(8,128)S(1)}, bf16[128,256]{1,0:T(8,128)(2,1)S(1)}, bf16[128,256]{1,0:T(8,128)(2,1)S(1)}, f32[512,256]{1,0:T(8,128)S(1)}) custom-call(s32[1,560]{1,0:T(1,128)S(1)} %get-tuple-element.441.plan, f32[512,256]{1,0:T(8,128)} %get-tuple-element.442.src_ref.table_ref, f32[72,256]{1,0:T(8,128)S(1)} %get-tuple-element.443.row_ref, ...), custom_call_target="tpu_custom_call" | custom-call | flops 805306368 | bytes 524288 | tf_op jit(solution)/shard_map/cond/branch_3_fun/tile_work/pallas_call | solution.py:230
  42.4 0.1 collective-permute-start.82
  42.5 1.0 %collective-permute-start.83 = (bf16[128,256]{1,0:T(8,128)(2,1)S(1)}, bf16[128,256]{1,0:T(8,128)(2,1)S(1)}, u32[]{:S(2)}, u32[]{:S(2)}) collective-permute-start(bf16[128,256]{1,0:T(8,128)(2,1)S(1)} %get-tuple-element.446), channel_id=1, source_target_pairs={{0,17},{1,16},{2,19},{3,18},{4,21},{5,20},{6,23},{7,22},{8,25},{9,... | collective-permute-start | bytes 196616 | tf_op jit(solution)/shard_map/cond/branch_3_fun/ppermute | solution.py:33
  43.5 0.0 collective-permute-done.85.refs_1_
  43.5 0.9 %collective-permute-done.84.refs_0_ = bf16[128,256]{1,0:T(8,128)(2,1)S(1)} collective-permute-done((bf16[128,256]{1,0:T(8,128)(2,1)S(1)}, bf16[128,256]{1,0:T(8,128)(2,1)S(1)}, u32[]{:S(2)}, u32[]{:S(2)}) %collective-permute-start.84) | collective-permute-done | bytes 65568 | tf_op jit(solution)/shard_map/cond/branch_3_fun/ppermute | solution.py:33
  44.4 3.1 %tile_work.49 = (f32[512,256]{1,0:T(8,128)S(1)}, bf16[128,256]{1,0:T(8,128)(2,1)S(1)}, bf16[128,256]{1,0:T(8,128)(2,1)S(1)}) custom-call(s32[1,560]{1,0:T(1,128)S(1)} %get-tuple-element.441.plan, f32[512,256]{1,0:T(8,128)S(1)} %get-tuple-element.447.src_ref, f32[72,256]{1,0:T(8,128)S(1)} %get-tuple-element.443.row_ref, ...), custom_call_target="tpu_custom_call", output_to_operand_aliasing={{0}: (5, {})} | custom-call | flops 805306368 | bytes 524288 | tf_op jit(solution)/shard_map/cond/branch_3_fun/tile_work/pallas_call | solution.py:230
  47.4 1.4 %collective-permute-start.86 = (bf16[128,256]{1,0:T(8,128)(2,1)S(1)}, bf16[128,256]{1,0:T(8,128)(2,1)S(1)}, u32[]{:S(2)}, u32[]{:S(2)}) collective-permute-start(bf16[128,256]{1,0:T(8,128)(2,1)S(1)} %get-tuple-element.449), channel_id=1, source_target_pairs={{0,18},{1,19},{2,16},{3,17},{4,22},{5,23},{6,20},{7,21},{8,26},{9,... | collective-permute-start | bytes 196616 | tf_op jit(solution)/shard_map/cond/branch_3_fun/ppermute | solution.py:33
  48.8 1.9 %collective-permute-start.87 = (bf16[128,256]{1,0:T(8,128)(2,1)S(1)}, bf16[128,256]{1,0:T(8,128)(2,1)S(1)}, u32[]{:S(2)}, u32[]{:S(2)}) collective-permute-start(bf16[128,256]{1,0:T(8,128)(2,1)S(1)} %get-tuple-element.450), channel_id=1, source_target_pairs={{0,19},{1,18},{2,17},{3,16},{4,23},{5,22},{6,21},{7,20},{8,27},{9,... | collective-permute-start | bytes 196616 | tf_op jit(solution)/shard_map/cond/branch_3_fun/ppermute | solution.py:33
  50.7 2.0 %update_source.24 = (f32[512,256]{1,0:T(8,128)}, f32[4,128]{1,0:T(4,128)}) custom-call(f32[512,256]{1,0:T(8,128)S(1)} %copy-done.11, f32[4,128]{1,0:T(4,128)} %get-tuple-element.453.state_hbm, f32[512,256]{1,0:T(8,128)S(1)} %get-tuple-element.454.grad_ref), custom_call_target="tpu_custom_call" | custom-call | flops 1048576 | bytes 1048576 | tf_op jit(solution)/shard_map/cond/branch_3_fun/update_source/pallas_call | solution.py:283
  52.7 0.0 collective-permute-done.82.refs_1_
  52.7 0.0 collective-permute-done.83.refs_2_
  52.8 1.4 %collective-permute-done.86.refs_3_ = bf16[128,256]{1,0:T(8,128)(2,1)S(1)} collective-permute-done((bf16[128,256]{1,0:T(8,128)(2,1)S(1)}, bf16[128,256]{1,0:T(8,128)(2,1)S(1)}, u32[]{:S(2)}, u32[]{:S(2)}) %collective-permute-start.86) | collective-permute-done | bytes 65568 | tf_op jit(solution)/shard_map/cond/branch_3_fun/ppermute | solution.py:33
  54.2 1.6 %collective-permute-done.87.refs_4_ = bf16[128,256]{1,0:T(8,128)(2,1)S(1)} collective-permute-done((bf16[128,256]{1,0:T(8,128)(2,1)S(1)}, bf16[128,256]{1,0:T(8,128)(2,1)S(1)}, u32[]{:S(2)}, u32[]{:S(2)}) %collective-permute-start.87) | collective-permute-done | bytes 65568 | tf_op jit(solution)/shard_map/cond/branch_3_fun/ppermute | solution.py:33
  55.8 0.8 %update_target.11 = (f32[128,256]{1,0:T(8,128)}, f32[1,128]{1,0:T(1,128)}) custom-call(f32[128,256]{1,0:T(8,128)S(1)} %get-tuple-element.439.table_ref, f32[1,128]{1,0:T(1,128)S(1)} %get-tuple-element.440.refs_0_, bf16[128,256]{1,0:T(8,128)(2,1)S(1)} %collective-permute-done.82.refs_1_, bf16[128,256]{1,0:T(8,128)(2,1)S(1)} %collective-permute-done.83.refs_2_, ...), custom_call_target="tpu_custom_call" | custom-call | flops 262144 | bytes 262144 | tf_op jit(solution)/shard_map/cond/branch_3_fun/update_target/pallas_call | solution.py:326
  (2 shorter events, 0.0 us)
Async XLA Ops:
  3.1 26.0 %copy-start = (f32[128,256]{1,0:T(8,128)S(1)}, f32[128,256]{1,0:T(8,128)}, u32[]{:S(2)}) copy-start(f32[128,256]{1,0:T(8,128)} %table_ref.1) | copy-start | bytes 393220
  3.1 8.2 %collective-permute-start.9 = (bf16[128,256]{1,0:T(8,128)(2,1)S(1)}, bf16[128,256]{1,0:T(8,128)(2,1)S(1)}, u32[]{:S(2)}, u32[]{:S(2)}) collective-permute-start(bf16[128,256]{1,0:T(8,128)(2,1)S(1)} %get-tuple-element.262), channel_id=1, source_target_pairs={{0,9},{1,8},{2,11},{3,10},{4,13},{5,12},{6,15},{7,14},{8,1},{9,0},... | collective-permute-start | bytes 196616 | tf_op jit(solution)/shard_map/cond/branch_1_fun/ppermute | solution.py:33
  7.1 4.3 %collective-permute-start.8 = (bf16[128,256]{1,0:T(8,128)(2,1)S(1)}, bf16[128,256]{1,0:T(8,128)(2,1)S(1)}, u32[]{:S(2)}, u32[]{:S(2)}) collective-permute-start(bf16[128,256]{1,0:T(8,128)(2,1)S(1)} %get-tuple-element.262), channel_id=1, source_target_pairs={{0,8},{1,9},{2,10},{3,11},{4,12},{5,13},{6,14},{7,15},{8,0},{9,1},... | collective-permute-start | bytes 196616 | tf_op jit(solution)/shard_map/cond/branch_1_fun/ppermute | solution.py:33
  7.8 9.6 %collective-permute-start.13 = (bf16[128,256]{1,0:T(8,128)(2,1)S(1)}, bf16[128,256]{1,0:T(8,128)(2,1)S(1)}, u32[]{:S(2)}, u32[]{:S(2)}) collective-permute-start(bf16[128,256]{1,0:T(8,128)(2,1)S(1)} %get-tuple-element.262), channel_id=1, source_target_pairs={{0,11},{1,10},{2,9},{3,8},{4,15},{5,14},{6,13},{7,12},{8,3},{9,2},... | collective-permute-start | bytes 196616 | tf_op jit(solution)/shard_map/cond/branch_1_fun/ppermute | solution.py:33
  11.3 6.7 %collective-permute-start.12 = (bf16[128,256]{1,0:T(8,128)(2,1)S(1)}, bf16[128,256]{1,0:T(8,128)(2,1)S(1)}, u32[]{:S(2)}, u32[]{:S(2)}) collective-permute-start(bf16[128,256]{1,0:T(8,128)(2,1)S(1)} %get-tuple-element.262), channel_id=1, source_target_pairs={{0,10},{1,11},{2,8},{3,9},{4,14},{5,15},{6,12},{7,13},{8,2},{9,3},... | collective-permute-start | bytes 196616 | tf_op jit(solution)/shard_map/cond/branch_1_fun/ppermute | solution.py:33
  13.9 13.1 %collective-permute-start.10 = (bf16[128,256]{1,0:T(8,128)(2,1)S(1)}, bf16[128,256]{1,0:T(8,128)(2,1)}, u32[]{:S(2)}, u32[]{:S(2)}) collective-permute-start(bf16[128,256]{1,0:T(8,128)(2,1)S(1)} %get-tuple-element.263), channel_id=1, source_target_pairs={{0,8},{1,9},{2,10},{3,11},{4,12},{5,13},{6,14},{7,15},{8,0},{9,1},... | collective-permute-start | bytes 196616 | tf_op jit(solution)/shard_map/cond/branch_1_fun/ppermute | solution.py:33
  15.0 12.0 %collective-permute-start.11 = (bf16[128,256]{1,0:T(8,128)(2,1)S(1)}, bf16[128,256]{1,0:T(8,128)(2,1)}, u32[]{:S(2)}, u32[]{:S(2)}) collective-permute-start(bf16[128,256]{1,0:T(8,128)(2,1)S(1)} %get-tuple-element.264), channel_id=1, source_target_pairs={{0,9},{1,8},{2,11},{3,10},{4,13},{5,12},{6,15},{7,14},{8,1},{9,0},... | collective-permute-start | bytes 196616 | tf_op jit(solution)/shard_map/cond/branch_1_fun/ppermute | solution.py:33
  19.5 5.5 %copy-start.2 = (f32[512,256]{1,0:T(8,128)S(1)}, f32[512,256]{1,0:T(8,128)}, u32[]{:S(2)}) copy-start(f32[512,256]{1,0:T(8,128)} %get-tuple-element.260.src_ref.table_ref) | copy-start | bytes 1572868 | tf_op jit(solution)/shard_map/cond
  19.5 7.6 %collective-permute-start.14 = (bf16[128,256]{1,0:T(8,128)(2,1)S(1)}, bf16[128,256]{1,0:T(8,128)(2,1)}, u32[]{:S(2)}, u32[]{:S(2)}) collective-permute-start(bf16[128,256]{1,0:T(8,128)(2,1)S(1)} %get-tuple-element.267), channel_id=1, source_target_pairs={{0,10},{1,11},{2,8},{3,9},{4,14},{5,15},{6,12},{7,13},{8,2},{9,3},... | collective-permute-start | bytes 196616 | tf_op jit(solution)/shard_map/cond/branch_1_fun/ppermute | solution.py:33
  21.1 7.3 %collective-permute-start.15 = (bf16[128,256]{1,0:T(8,128)(2,1)S(1)}, bf16[128,256]{1,0:T(8,128)(2,1)}, u32[]{:S(2)}, u32[]{:S(2)}) collective-permute-start(bf16[128,256]{1,0:T(8,128)(2,1)S(1)} %get-tuple-element.268), channel_id=1, source_target_pairs={{0,11},{1,10},{2,9},{3,8},{4,15},{5,14},{6,13},{7,12},{8,3},{9,2},... | collective-permute-start | bytes 196616 | tf_op jit(solution)/shard_map/cond/branch_1_fun/ppermute | solution.py:33
  30.2 8.0 %collective-permute-start.81 = (bf16[128,256]{1,0:T(8,128)(2,1)S(1)}, bf16[128,256]{1,0:T(8,128)(2,1)S(1)}, u32[]{:S(2)}, u32[]{:S(2)}) collective-permute-start(bf16[128,256]{1,0:T(8,128)(2,1)S(1)} %get-tuple-element.444), channel_id=1, source_target_pairs={{0,17},{1,16},{2,19},{3,18},{4,21},{5,20},{6,23},{7,22},{8,25},{9,... | collective-permute-start | bytes 196616 | tf_op jit(solution)/shard_map/cond/branch_3_fun/ppermute | solution.py:33
  33.6 4.6 %collective-permute-start.80 = (bf16[128,256]{1,0:T(8,128)(2,1)S(1)}, bf16[128,256]{1,0:T(8,128)(2,1)S(1)}, u32[]{:S(2)}, u32[]{:S(2)}) collective-permute-start(bf16[128,256]{1,0:T(8,128)(2,1)S(1)} %get-tuple-element.444), channel_id=1, source_target_pairs={{0,16},{1,17},{2,18},{3,19},{4,20},{5,21},{6,22},{7,23},{8,24},{9,... | collective-permute-start | bytes 196616 | tf_op jit(solution)/shard_map/cond/branch_3_fun/ppermute | solution.py:33
  33.6 9.8 %collective-permute-start.85 = (bf16[128,256]{1,0:T(8,128)(2,1)S(1)}, bf16[128,256]{1,0:T(8,128)(2,1)S(1)}, u32[]{:S(2)}, u32[]{:S(2)}) collective-permute-start(bf16[128,256]{1,0:T(8,128)(2,1)S(1)} %get-tuple-element.444), channel_id=1, source_target_pairs={{0,19},{1,18},{2,17},{3,16},{4,23},{5,22},{6,21},{7,20},{8,27},{9,... | collective-permute-start | bytes 196616 | tf_op jit(solution)/shard_map/cond/branch_3_fun/ppermute | solution.py:33
  38.2 6.2 %collective-permute-start.84 = (bf16[128,256]{1,0:T(8,128)(2,1)S(1)}, bf16[128,256]{1,0:T(8,128)(2,1)S(1)}, u32[]{:S(2)}, u32[]{:S(2)}) collective-permute-start(bf16[128,256]{1,0:T(8,128)(2,1)S(1)} %get-tuple-element.444), channel_id=1, source_target_pairs={{0,18},{1,19},{2,16},{3,17},{4,22},{5,23},{6,20},{7,21},{8,26},{9,... | collective-permute-start | bytes 196616 | tf_op jit(solution)/shard_map/cond/branch_3_fun/ppermute | solution.py:33
  42.4 10.3 %collective-permute-start.82 = (bf16[128,256]{1,0:T(8,128)(2,1)S(1)}, bf16[128,256]{1,0:T(8,128)(2,1)S(1)}, u32[]{:S(2)}, u32[]{:S(2)}) collective-permute-start(bf16[128,256]{1,0:T(8,128)(2,1)S(1)} %get-tuple-element.445), channel_id=1, source_target_pairs={{0,16},{1,17},{2,18},{3,19},{4,20},{5,21},{6,22},{7,23},{8,24},{9,... | collective-permute-start | bytes 196616 | tf_op jit(solution)/shard_map/cond/branch_3_fun/ppermute | solution.py:33
  42.5 10.3 %collective-permute-start.83 = (bf16[128,256]{1,0:T(8,128)(2,1)S(1)}, bf16[128,256]{1,0:T(8,128)(2,1)S(1)}, u32[]{:S(2)}, u32[]{:S(2)}) collective-permute-start(bf16[128,256]{1,0:T(8,128)(2,1)S(1)} %get-tuple-element.446), channel_id=1, source_target_pairs={{0,17},{1,16},{2,19},{3,18},{4,21},{5,20},{6,23},{7,22},{8,25},{9,... | collective-permute-start | bytes 196616 | tf_op jit(solution)/shard_map/cond/branch_3_fun/ppermute | solution.py:33
  44.4 6.3 %copy-start.11 = (f32[512,256]{1,0:T(8,128)S(1)}, f32[512,256]{1,0:T(8,128)}, u32[]{:S(2)}) copy-start(f32[512,256]{1,0:T(8,128)} %get-tuple-element.442.src_ref.table_ref) | copy-start | bytes 1572868 | tf_op jit(solution)/shard_map/cond
  47.4 6.7 %collective-permute-start.86 = (bf16[128,256]{1,0:T(8,128)(2,1)S(1)}, bf16[128,256]{1,0:T(8,128)(2,1)S(1)}, u32[]{:S(2)}, u32[]{:S(2)}) collective-permute-start(bf16[128,256]{1,0:T(8,128)(2,1)S(1)} %get-tuple-element.449), channel_id=1, source_target_pairs={{0,18},{1,19},{2,16},{3,17},{4,22},{5,23},{6,20},{7,21},{8,26},{9,... | collective-permute-start | bytes 196616 | tf_op jit(solution)/shard_map/cond/branch_3_fun/ppermute | solution.py:33
  48.8 7.0 %collective-permute-start.87 = (bf16[128,256]{1,0:T(8,128)(2,1)S(1)}, bf16[128,256]{1,0:T(8,128)(2,1)S(1)}, u32[]{:S(2)}, u32[]{:S(2)}) collective-permute-start(bf16[128,256]{1,0:T(8,128)(2,1)S(1)} %get-tuple-element.450), channel_id=1, source_target_pairs={{0,19},{1,18},{2,17},{3,16},{4,23},{5,22},{6,21},{7,20},{8,27},{9,... | collective-permute-start | bytes 196616 | tf_op jit(solution)/shard_map/cond/branch_3_fun/ppermute | solution.py:33
